TPU v7x, 32 devices: a whole 2x2x4 slice. The times are simulated.
32 devices in a mesh: batch: 2 (over y), freq: 16 (over z, x, core).
Axes of the slice: x: 2, y: 2, z: 4, core: 2. Of those that a mesh axis runs over, the one named last changes fastest.
Arguments:
- images: bfloat16 [128, 128, 512], P(('batch', 'freq')), may hold values from -50 to 50
- radial_counts: int32 [256], replicated, may hold values from 1 to 120, as said below
- order: int32 [256], replicated, may hold values from 0 to 255, as said below
- zeros_table: int32 [256, 128], replicated, may hold values from 1 to 128, as said below
- noise_var: float32 [256], replicated, may hold values from 0.25 to 4
Outputs:
- denoised: bfloat16 [128, 128, 512], P(('batch', 'freq'))
- wiener_blocks: float32 [256, 128, 128], P('freq')
Inputs may be any that keep to these rules, and one draw needn't show every extreme that they name: `radial_counts`: frequencies from 128 on have at most 64 radial modes, and frequency 128 has exactly 64; frequency 0 has exactly 120. `order`: A permutation of the 256 frequencies. For every d, slots 16d and 16d + 1 hold frequencies below 128, and the other 8 slots of d hold frequencies from 128 on. `zeros_table`: the values of one row are distinct.
All inputs are finite; a program needn't handle non-finite values.
Results may differ from a plain program's by a relative error of at most 0.0085.
Values may be sent and summed in bfloat16 or wider, within the bound.
No kernel may reach another device: no remote copies, remote signals or barrier semaphores. Data moves between devices by JAX's collectives and lax.ppermute only.
A program may use at most 64 MiB of HBM per device.

v0:
```python
import math

import jax
import jax.numpy as jnp
from jax import lax
from jax.sharding import PartitionSpec as P


def make_table(freqs, angles):
    angle_index = jnp.arange(angles, dtype=jnp.int32)
    product = angle_index[:, None] * freqs[None, :] % angles
    phase = 2.0 * math.pi / angles * product.astype(jnp.float32)
    factor = math.sqrt(2.0 / angles)
    return jnp.concatenate([factor * jnp.cos(phase), factor * jnp.sin(phase)], axis=1).astype(
        jnp.bfloat16
    )


def make_basis(freqs, zero_rows, counts, radial):
    slots = zero_rows.shape[1]
    freq_float = freqs.astype(jnp.float32)[:, None, None]
    scaled = math.pi * (zero_rows.astype(jnp.float32)[:, :, None] + 0.5 * freq_float - 0.25)
    grid = (jnp.arange(radial, dtype=jnp.float32) + 0.5) / radial
    phase = scaled * grid[None, None, :] - 0.5 * math.pi * freq_float - 0.25 * math.pi
    keep = jnp.arange(slots, dtype=jnp.int32)[None, :, None] < counts[:, None, None]
    values = math.sqrt(2.0 / radial) * jnp.cos(phase)
    return jnp.where(keep, values, jnp.zeros_like(values)).astype(jnp.bfloat16)


def gram_of(blocks):
    return jnp.einsum("kvq,kvp->kqp", blocks, blocks, preferred_element_type=jnp.float32)


def shrink_from(gram, noise, vectors):
    width = gram.shape[1]
    eye = jnp.eye(width, dtype=jnp.float32)
    covariance = gram / vectors + noise[:, None, None] * eye
    lower = jnp.linalg.cholesky(covariance)
    inv_lower = jax.scipy.linalg.solve_triangular(
        lower, jnp.broadcast_to(eye, covariance.shape), lower=True
    )
    inverse = jnp.einsum("kmq,kmp->kqp", inv_lower, inv_lower, precision=lax.Precision.HIGHEST)
    return eye - noise[:, None, None] * inverse


def apply_shrink(shrinkage, blocks):
    return jnp.einsum(
        "kqp,kvp->kvq", shrinkage.astype(jnp.bfloat16), blocks, preferred_element_type=jnp.float32
    ).astype(jnp.bfloat16)


def per_device(images, radial_counts, order, zeros_table, noise_var):
    count_img, radial, angles = images.shape
    total_freq = order.shape[0]
    block = min(64, total_freq)
    nblocks = total_freq // block
    flat = images.reshape(count_img * radial, angles)
    slot_rows = jnp.take(zeros_table, order, axis=0)
    slot_counts = jnp.take(radial_counts, order)

    def block_tools(index):
        start = index * block
        freqs = lax.dynamic_slice_in_dim(order, start, block)
        table = make_table(freqs, angles)
        rows_here = lax.dynamic_slice_in_dim(slot_rows, start, block, 0)
        counts_here = lax.dynamic_slice_in_dim(slot_counts, start, block)
        return (table, make_basis(freqs, rows_here, counts_here, radial))

    def analyse(index):
        table, basis = block_tools(index)
        spectrum = jnp.dot(flat, table, preferred_element_type=jnp.float32)
        spectrum = spectrum.astype(jnp.bfloat16).reshape(count_img, radial, 2, block)
        return jnp.einsum(
            "ircj,jqr->jciq", spectrum, basis, preferred_element_type=jnp.float32
        ).astype(jnp.bfloat16)

    pieces = lax.map(analyse, jnp.arange(nblocks, dtype=jnp.int32))
    moved = pieces.reshape(total_freq, 2 * count_img, radial)
    owners = lax.axis_size("freq")
    owned = total_freq // owners
    batches = lax.axis_size("batch")
    mine = lax.dynamic_slice_in_dim(order, lax.axis_index("freq") * owned, owned)
    noise_mine = jnp.take(noise_var, mine)
    half_slots = owned // 2
    narrow = radial // 2
    grouped = moved.reshape(owners, owned, 2 * count_img, radial)
    lower_part = grouped[:, :half_slots].reshape(owners * half_slots, 2 * count_img, radial)
    upper_part = grouped[:, half_slots:, :, :narrow].reshape(
        owners * half_slots, 2 * count_img, narrow
    )
    low_recv, high_recv = (
        lax.all_to_all(lower_part, "freq", split_axis=0, concat_axis=1, tiled=True),
        lax.all_to_all(upper_part, "freq", split_axis=0, concat_axis=1, tiled=True),
    )
    gram_low, gram_high = lax.psum((gram_of(low_recv), gram_of(high_recv)), "batch")
    vectors = low_recv.shape[1] * batches
    shrink_lower = shrink_from(gram_low, noise_mine[:half_slots], vectors)
    shrink_upper = shrink_from(gram_high, noise_mine[half_slots:], vectors)
    low_back, high_back = (
        lax.all_to_all(
            apply_shrink(shrink_lower, low_recv), "freq", split_axis=1, concat_axis=0, tiled=True
        ),
        lax.all_to_all(
            apply_shrink(shrink_upper, high_recv), "freq", split_axis=1, concat_axis=0, tiled=True
        ),
    )
    high_wide = jnp.pad(high_back, ((0, 0), (0, 0), (0, radial - narrow)))
    returned = jnp.concatenate(
        [
            low_back.reshape(owners, half_slots, 2 * count_img, radial),
            high_wide.reshape(owners, half_slots, 2 * count_img, radial),
        ],
        axis=1,
    )
    returned = returned.reshape(total_freq, 2 * count_img, radial)
    upper_wide = jnp.pad(shrink_upper, ((0, 0), (0, radial - narrow), (0, radial - narrow)))
    wiener_blocks = jnp.concatenate([shrink_lower, upper_wide], axis=0)
    filtered_blocks = returned.reshape(nblocks, block, 2, count_img, radial)

    def synthesise(index, total):
        table, basis = block_tools(index)
        piece = lax.dynamic_index_in_dim(filtered_blocks, index, 0, keepdims=False)
        spectrum_out = jnp.einsum(
            "jciq,jqr->ircj", piece, basis, preferred_element_type=jnp.float32
        )
        spectrum_out = spectrum_out.astype(jnp.bfloat16).reshape(count_img * radial, 2 * block)
        return total + lax.dot_general(
            spectrum_out, table, (((1,), (1,)), ((), ())), preferred_element_type=jnp.float32
        )

    summed = lax.fori_loop(
        0, nblocks, synthesise, jnp.zeros((count_img * radial, angles), jnp.float32)
    )
    denoised = summed.astype(jnp.bfloat16).reshape(count_img, radial, angles)
    return (denoised, wiener_blocks)


def solution(mesh):
    return jax.shard_map(
        per_device,
        mesh=mesh,
        in_specs=(P(("batch", "freq"), None, None), P(), P(), P(), P()),
        out_specs=(P(("batch", "freq"), None, None), P("freq", None, None)),
        check_vma=False,
    )
```

profile of v0, /device:TPU:0, one launch (start us, length us, event | category | flops | bytes accessed | tf_op | source)
XLA Modules:
  0.0 535.8 jit_solution(11724055597043136557)
XLA Ops:
  8.0 2.0 gather_fusion
  10.9 82.4 %while.28 = (s32[]{:T(128)}, bf16[4,64,2,4,128]{4,3,2,1,0:T(4,128)(2,1)S(1)}, s32[4]{0:T(128)S(1)}, s32[256]{0:T(256)S(1)}, s32[256,128]{1,0:T(8,128)S(1)}, /*in...) while((s32[]{:T(128)}, ...), condition=%wide.region_1.2_spmd, body=%wide.region_0.1_spmd.sunk | while | flops 91202056 | bytes 1560767 | solution.py:77
  13.4 18.1 %fusion.99 = bf16[4,64,2,4,128]{4,3,2,1,0:T(4,128)(2,1)S(1)} fusion(bf16[4,64,2,4,128]{4,3,2,1,0:T(4,128)(2,1)S(1)} %get-tuple-element.454, s32[]{:T(128)S(6)} %copy.273, f32[64]{0:T(128)S(1)} %convert_multiply_fusion.9, f32[128]{0:T(128)S(1)} %add_multiply_fusion.8, f32[64,128]{1,0:T(8,128)S(1)} %add_multiply_fusion.9, ...), kind=kOutput, calls=%fused_computation.11.clone.1 | convolution fusion | flops 23134208 | bytes 304132 | tf_op jit(solution)/shard_map/while/body/eval_jaxpr/ircj,jqr->jciq/dot_general | solution.py:73
  34.0 18.1 %fusion.99 = bf16[4,64,2,4,128]{4,3,2,1,0:T(4,128)(2,1)S(1)} fusion(bf16[4,64,2,4,128]{4,3,2,1,0:T(4,128)(2,1)S(1)} %get-tuple-element.454, s32[]{:T(128)S(6)} %copy.273, f32[64]{0:T(128)S(1)} %convert_multiply_fusion.9, f32[128]{0:T(128)S(1)} %add_multiply_fusion.8, f32[64,128]{1,0:T(8,128)S(1)} %add_multiply_fusion.9, ...), kind=kOutput, calls=%fused_computation.11.clone.1 | convolution fusion | flops 23134208 | bytes 304132 | tf_op jit(solution)/shard_map/while/body/eval_jaxpr/ircj,jqr->jciq/dot_general | solution.py:73
  54.6 18.1 %fusion.99 = bf16[4,64,2,4,128]{4,3,2,1,0:T(4,128)(2,1)S(1)} fusion(bf16[4,64,2,4,128]{4,3,2,1,0:T(4,128)(2,1)S(1)} %get-tuple-element.454, s32[]{:T(128)S(6)} %copy.273, f32[64]{0:T(128)S(1)} %convert_multiply_fusion.9, f32[128]{0:T(128)S(1)} %add_multiply_fusion.8, f32[64,128]{1,0:T(8,128)S(1)} %add_multiply_fusion.9, ...), kind=kOutput, calls=%fused_computation.11.clone.1 | convolution fusion | flops 23134208 | bytes 304132 | tf_op jit(solution)/shard_map/while/body/eval_jaxpr/ircj,jqr->jciq/dot_general | solution.py:73
  75.2 18.1 %fusion.99 = bf16[4,64,2,4,128]{4,3,2,1,0:T(4,128)(2,1)S(1)} fusion(bf16[4,64,2,4,128]{4,3,2,1,0:T(4,128)(2,1)S(1)} %get-tuple-element.454, s32[]{:T(128)S(6)} %copy.273, f32[64]{0:T(128)S(1)} %convert_multiply_fusion.9, f32[128]{0:T(128)S(1)} %add_multiply_fusion.8, f32[64,128]{1,0:T(8,128)S(1)} %add_multiply_fusion.9, ...), kind=kOutput, calls=%fused_computation.11.clone.1 | convolution fusion | flops 23134208 | bytes 304132 | tf_op jit(solution)/shard_map/while/body/eval_jaxpr/ircj,jqr->jciq/dot_general | solution.py:73
  93.3 0.9 reshape.206
  94.2 7.4 %all-to-all-start.2 = ((bf16[16,2,2048]{2,1,0:T(2,128)(2,1)}), bf16[16,2,2048]{2,1,0:T(2,128)(2,1)S(1)}, u32[]{:S(2)}, u32[]{:S(2)}) async-start(bf16[16,2,2048]{2,1,0:T(2,128)(2,1)} %reshape.206), calls=%async_computation.2 | async-start | bytes 262144 | tf_op jit(solution)/shard_map/all_to_all | solution.py:93
  102.4 7.1 %all-to-all-done.2 = bf16[16,2,2048]{2,1,0:T(2,128)(2,1)S(1)} async-done(((bf16[16,2,2048]{2,1,0:T(2,128)(2,1)}), bf16[16,2,2048]{2,1,0:T(2,128)(2,1)S(1)}, u32[]{:S(2)}, u32[]{:S(2)}) %all-to-all-start.2) | async-done | bytes 131104 | tf_op jit(solution)/shard_map/all_to_all | solution.py:93
  109.5 3.5 all-to-all-start
  114.2 1.0 fusion.62
  115.2 7.8 %all-to-all-done = bf16[128,8,128]{2,1,0:T(8,128)(2,1)S(1)} async-done(((bf16[128,8,128]{2,1,0:T(8,128)(2,1)}), bf16[128,8,128]{2,1,0:T(8,128)(2,1)S(1)}, u32[]{:S(2)}, u32[]{:S(2)}) %all-to-all-start) | async-done | bytes 262176 | tf_op jit(solution)/shard_map/all_to_all | solution.py:92
  123.0 1.1 fusion.65
  124.3 32.6 %all-reduce.5.cloned.1.call-done = (f32[8,64,64]{1,2,0:T(8,128)}, f32[8,128,128]{1,2,0:T(8,128)}) async-done(((f32[8,64,64]{1,2,0:T(8,128)}, f32[8,128,128]{1,2,0:T(8,128)}), (f32[8,64,64]{1,2,0:T(8,128)}, f32[8,128,128]{1,2,0:T(8,128)})) %all-reduce.5.cloned.1.call-update) | async-done | bytes 655376 | tf_op jit(solution)/shard_map/psum | solution.py:95
  156.9 1.2 multiply_add_fusion
  158.7 94.0 %custom-call.16 = f32[8,128,128]{2,1,0:T(8,128)S(1)} custom-call(f32[8,128,128]{2,1,0:T(8,128)S(1)} %copy.186), custom_call_target="Cholesky" | custom-call | tf_op jit(solution)/shard_map/jit(cholesky)/cholesky | solution.py:38
  253.0 78.6 %custom-call.17 = f32[8,1,128,128]{2,3,1,0:T(8,128)S(1)} custom-call(f32[8,1,128,128]{3,2,1,0:T(8,128)S(1)} %select_bitcast_fusion), custom_call_target="InvertDiagBlocksLowerTriangular" | custom-call | tf_op jit(solution)/shard_map/jit(_solve_triangular)/vmap()/triangular_solve | solution.py:39
  331.6 1.0 fusion.55
  332.6 1.1 fusion.53
  334.0 46.9 %custom-call.18 = f32[8,64,64]{2,1,0:T(8,128)S(1)} custom-call(f32[8,64,64]{2,1,0:T(8,128)S(1)} %fusion.60), custom_call_target="Cholesky" | custom-call | tf_op jit(solution)/shard_map/jit(cholesky)/cholesky | solution.py:38
  381.2 39.3 %custom-call.19 = f32[8,1,64,64]{2,3,1,0:T(8,128)S(1)} custom-call(f32[8,1,64,64]{3,2,1,0:T(8,128)S(1)} %select_bitcast_fusion.1), custom_call_target="InvertDiagBlocksLowerTriangular" | custom-call | tf_op jit(solution)/shard_map/jit(_solve_triangular)/vmap()/triangular_solve | solution.py:39
  422.2 0.9 reshape.208
  423.1 5.6 %all-to-all-start.3 = ((bf16[16,2,2048]{2,1,0:T(2,128)(2,1)}), bf16[16,2,2048]{2,1,0:T(2,128)(2,1)S(1)}, u32[]{:S(2)}, u32[]{:S(2)}) async-start(bf16[16,2,2048]{2,1,0:T(2,128)(2,1)} %reshape.208), calls=%async_computation.3 | async-start | bytes 262144 | tf_op jit(solution)/shard_map/all_to_all | solution.py:103
  429.8 6.8 %all-to-all-done.3 = bf16[16,2,2048]{2,1,0:T(2,128)(2,1)S(1)} async-done(((bf16[16,2,2048]{2,1,0:T(2,128)(2,1)}), bf16[16,2,2048]{2,1,0:T(2,128)(2,1)S(1)}, u32[]{:S(2)}, u32[]{:S(2)}) %all-to-all-start.3) | async-done | bytes 131104 | tf_op jit(solution)/shard_map/all_to_all | solution.py:103
  436.6 3.5 all-to-all-start.1
  440.3 1.3 copy.212
  441.9 8.2 %all-to-all-done.1 = bf16[8,128,128]{2,0,1:T(8,128)(2,1)S(1)} async-done(((bf16[8,128,128]{2,0,1:T(8,128)(2,1)}), bf16[8,128,128]{2,0,1:T(8,128)(2,1)S(1)}, u32[]{:S(2)}, u32[]{:S(2)}) %all-to-all-start.1) | async-done | bytes 262176 | tf_op jit(solution)/shard_map/all_to_all | solution.py:100
  450.6 77.5 %while.29 = (s32[]{:T(128)}, f32[512,512]{1,0:T(8,128)S(1)}, s32[256]{0:T(256)S(1)}, s32[256,128]{1,0:T(8,128)S(1)}, s32[256]{0:T(256)S(1)}, /*index=5*/bf16[4,6...) while((s32[]{:T(128)}, f32[512,512]{1,0:T(8,128)S(1)}, ...), condition=%wide.region_9.10_spmd.clone, body=%wide.region_8.9_spmd.clone.sunk | while | flops 91660808 | bytes 3395509 | solution.py:131
  451.0 17.9 %fusion.103 = bf16[4,128,2,64]{1,0,2,3:T(4,128)(2,1)S(1)} fusion(f32[64]{0:T(128)S(1)} %convert_multiply_fusion.11, f32[128]{0:T(128)S(1)} %add_multiply_fusion.10, f32[64,128]{1,0:T(8,128)S(1)} %add_multiply_fusion.11, pred[64,128]{1,0:T(8,128)(4,1)S(1)} %iota_compare_fusion.10, bf16[1,64,2,4,128]{4,1,0,3,2:T(8,128)(2,1)S(1)} %constant_dynamic-slice_fusion.2), kind=kOutput, calls=%fused_computation.42.clone.1 | convolution fusion | flops 23134208 | bytes 303872 | tf_op jit(solution)/shard_map/while/body/eval_jaxpr/jciq,jqr->ircj/dot_general | solution.py:123
  470.4 17.9 %fusion.103 = bf16[4,128,2,64]{1,0,2,3:T(4,128)(2,1)S(1)} fusion(f32[64]{0:T(128)S(1)} %convert_multiply_fusion.11, f32[128]{0:T(128)S(1)} %add_multiply_fusion.10, f32[64,128]{1,0:T(8,128)S(1)} %add_multiply_fusion.11, pred[64,128]{1,0:T(8,128)(4,1)S(1)} %iota_compare_fusion.10, bf16[1,64,2,4,128]{4,1,0,3,2:T(8,128)(2,1)S(1)} %constant_dynamic-slice_fusion.2), kind=kOutput, calls=%fused_computation.42.clone.1 | convolution fusion | flops 23134208 | bytes 303872 | tf_op jit(solution)/shard_map/while/body/eval_jaxpr/jciq,jqr->ircj/dot_general | solution.py:123
  489.8 17.9 %fusion.103 = bf16[4,128,2,64]{1,0,2,3:T(4,128)(2,1)S(1)} fusion(f32[64]{0:T(128)S(1)} %convert_multiply_fusion.11, f32[128]{0:T(128)S(1)} %add_multiply_fusion.10, f32[64,128]{1,0:T(8,128)S(1)} %add_multiply_fusion.11, pred[64,128]{1,0:T(8,128)(4,1)S(1)} %iota_compare_fusion.10, bf16[1,64,2,4,128]{4,1,0,3,2:T(8,128)(2,1)S(1)} %constant_dynamic-slice_fusion.2), kind=kOutput, calls=%fused_computation.42.clone.1 | convolution fusion | flops 23134208 | bytes 303872 | tf_op jit(solution)/shard_map/while/body/eval_jaxpr/jciq,jqr->ircj/dot_general | solution.py:123
  509.1 17.9 %fusion.103 = bf16[4,128,2,64]{1,0,2,3:T(4,128)(2,1)S(1)} fusion(f32[64]{0:T(128)S(1)} %convert_multiply_fusion.11, f32[128]{0:T(128)S(1)} %add_multiply_fusion.10, f32[64,128]{1,0:T(8,128)S(1)} %add_multiply_fusion.11, pred[64,128]{1,0:T(8,128)(4,1)S(1)} %iota_compare_fusion.10, bf16[1,64,2,4,128]{4,1,0,3,2:T(8,128)(2,1)S(1)} %constant_dynamic-slice_fusion.2), kind=kOutput, calls=%fused_computation.42.clone.1 | convolution fusion | flops 23134208 | bytes 303872 | tf_op jit(solution)/shard_map/while/body/eval_jaxpr/jciq,jqr->ircj/dot_general | solution.py:123
  (144 shorter events, 22.7 us)
Async XLA Ops:
  7.2 2.8 copy-start
  7.2 2.8 copy-start.5
  7.9 2.9 copy-start.2
  93.3 20.0 %copy-start.1 = (f32[256]{0:T(256)S(1)}, f32[256]{0:T(256)}, u32[]{:S(2)}) copy-start(f32[256]{0:T(256)} %param.13) | copy-start | bytes 3076
  94.2 15.3 %all-to-all-start.2 = ((bf16[16,2,2048]{2,1,0:T(2,128)(2,1)}), bf16[16,2,2048]{2,1,0:T(2,128)(2,1)S(1)}, u32[]{:S(2)}, u32[]{:S(2)}) async-start(bf16[16,2,2048]{2,1,0:T(2,128)(2,1)} %reshape.206), calls=%async_computation.2 | async-start | bytes 262144 | tf_op jit(solution)/shard_map/all_to_all | solution.py:93
  109.5 13.5 %all-to-all-start = ((bf16[128,8,128]{2,1,0:T(8,128)(2,1)}), bf16[128,8,128]{2,1,0:T(8,128)(2,1)S(1)}, u32[]{:S(2)}, u32[]{:S(2)}) async-start(bf16[128,8,128]{2,1,0:T(8,128)(2,1)} %bitcast.8), calls=%async_computation | async-start | bytes 524288 | tf_op jit(solution)/shard_map/all_to_all | solution.py:92
  113.0 43.8 %all-reduce.5.cloned.1.call-start = ((), (), s32[]{:S(2)}) async-start(), calls=%async_computation.4 | async-start | bytes 1572864 | tf_op jit(solution)/shard_map/psum | solution.py:95
  156.9 1.4 copy-start.3
  332.6 1.1 copy-start.4
  423.1 13.5 %all-to-all-start.3 = ((bf16[16,2,2048]{2,1,0:T(2,128)(2,1)}), bf16[16,2,2048]{2,1,0:T(2,128)(2,1)S(1)}, u32[]{:S(2)}, u32[]{:S(2)}) async-start(bf16[16,2,2048]{2,1,0:T(2,128)(2,1)} %reshape.208), calls=%async_computation.3 | async-start | bytes 262144 | tf_op jit(solution)/shard_map/all_to_all | solution.py:103
  436.6 13.5 %all-to-all-start.1 = ((bf16[8,128,128]{2,0,1:T(8,128)(2,1)}), bf16[8,128,128]{2,0,1:T(8,128)(2,1)S(1)}, u32[]{:S(2)}, u32[]{:S(2)}) async-start(bf16[8,128,128]{2,0,1:T(8,128)(2,1)} %copy.192), calls=%async_computation.1 | async-start | bytes 524288 | tf_op jit(solution)/shard_map/all_to_all | solution.py:100
Sparse Core Ops, SparseCore 0:
  124.2 32.6 all-reduce.4
where the time goes:
time: 536 us
  other arithmetic  270 us (50%)
  matrix products  153 us (29%)
  waiting for transfers between devices  62.5 us (12%)
  starting transfers between devices  20.1 us (4%)
  between operations  14.4 us (3%)
  local copies, waits for them, and re-layouts  13.4 us (2%)
    another operation x6, other arithmetic, shrink_from(): lower = jnp.linalg.cholesky(covariance)  141 us
    another operation x6, other arithmetic, shrink_from(): jax.scipy.linalg.solve_triangular(lower, jnp.broadcast_to(eye, covariance...  118 us
    dot_general x4, matrix products, analyse(): jnp.einsum('ircj,jqr->jciq', spectrum, basis, preferred_element_type=jnp....  72.2 us
    dot_general x4, matrix products, synthesise(): jnp.einsum('jciq,jqr->ircj', piece, basis, preferred_element_type=jnp.flo...  71.7 us
    psum x1, waiting for transfers between devices, per_device(): lax.psum((gram_of(low_recv), gram_of(high_recv)), 'batch')  32.6 us
  transfers between devices with their start and end apart: 5, of which 5 were waited for; matrix products, arithmetic and copies ran while one was open for 1% of the time, Pallas kernels for 0%

commit v1 on v0

--- a/solution.py
+++ b/solution.py
@@ -1,8 +1,11 @@
+import functools
 import math
 
 import jax
 import jax.numpy as jnp
 from jax import lax
+from jax.experimental import pallas as pl
+from jax.experimental.pallas import tpu as pltpu
 from jax.sharding import PartitionSpec as P
 
 
@@ -135,9 +138,316 @@
     return (denoised, wiener_blocks)
 
 
+MASKED = 0
+
+
+def cos_sin(turns, steps):
+    quarter = steps // 4
+    eighth = steps // 8
+    shifted = turns + eighth
+    quadrant = jnp.right_shift(shifted, int(math.log2(quarter)))
+    x = ((shifted & (quarter - 1)) - eighth).astype(jnp.float32) * (2.0 * math.pi / steps)
+    x2 = x * x
+    s = x * (1.0 + x2 * (-1.0 / 6 + x2 * (1.0 / 120 + x2 * (-1.0 / 5040 + x2 / 362880))))
+    c = 1.0 + x2 * (-0.5 + x2 * (1.0 / 24 + x2 * (-1.0 / 720 + x2 * (1.0 / 40320))))
+    odd = (quadrant & 1) == 1
+    cosine = jnp.where(odd, s, c)
+    sine = jnp.where(odd, c, s)
+    cosine = jnp.where(((quadrant + 1) & 2) != 0, -cosine, cosine)
+    sine = jnp.where((quadrant & 2) != 0, -sine, sine)
+    return cosine, sine
+
+
+def iota(shape, dim):
+    return lax.broadcasted_iota(jnp.int32, shape, dim)
+
+
+class Plan:
+    def __init__(self, images, order, owners, batches):
+        self.count_img, self.radial, self.angles = images
+        self.total = order
+        self.owners, self.batches = owners, batches
+        self.devices = owners * batches
+        self.owned = order // owners
+        self.half = self.owned // 2
+        self.quota = self.half // batches if self.half % batches == 0 else 0
+        self.slots = 2 * self.quota
+        self.vecs = 2 * self.count_img
+        power = lambda n: n > 0 and n & (n - 1) == 0
+        self.fits = (
+            self.slots == 8
+            and self.radial == 128
+            and all(power(n) for n in (self.angles, self.total, owners, batches))
+        )
+
+
+def analysis_kernel(plan, order_ref, images_ref, coef_ref, table_ref, cb_ref, sb_ref, wave_ref):
+    n, radial, angles, total = plan.count_img, plan.radial, plan.angles, plan.total
+    row = iota((total, total), 0)
+    place = row & (plan.quota - 1)
+    side = (row // plan.quota) & 1
+    owner = (row // plan.slots) & (plan.owners - 1)
+    batch = row // (plan.slots * plan.owners)
+    slot = owner * plan.owned + side * plan.half + batch * plan.quota + place
+    pick = (slot == iota((total, total), 1)).astype(jnp.float32).astype(jnp.bfloat16)
+    held = jnp.broadcast_to(order_ref[...].astype(jnp.float32), (128, total)).astype(jnp.bfloat16)
+    freq = lax.dot_general(pick, held, (((1,), (1,)), ((), ())), preferred_element_type=jnp.float32)
+    freq = freq.astype(jnp.int32)
+    lane = iota((total, 128), 1)
+    for part in range(angles // 128):
+        turns = ((lane + part * 128) * freq) & (angles - 1)
+        cosine, sine = cos_sin(turns, angles)
+        factor = math.sqrt(2.0 / angles)
+        cols = slice(part * 128, part * 128 + 128)
+        table_ref[0:total, cols] = (factor * cosine).astype(jnp.bfloat16)
+        table_ref[total : 2 * total, cols] = (factor * sine).astype(jnp.bfloat16)
+    steps = 16 * radial
+    turns = ((2 * freq - 1) * (2 * lane + 1) - 4 * radial * freq - 2 * radial) & (steps - 1)
+    cosine, sine = cos_sin(turns, steps)
+    cb_ref[...] = cosine
+    sb_ref[...] = sine
+    zero = iota((radial, radial), 1) + 1
+    turns = (zero * (2 * iota((radial, radial), 0) + 1)) & (4 * radial - 1)
+    cosine, sine = cos_sin(turns, 4 * radial)
+    factor = math.sqrt(2.0 / radial)
+    wave_ref[0:radial, :] = (factor * cosine).astype(jnp.bfloat16)
+    wave_ref[radial : 2 * radial, :] = (-factor * sine).astype(jnp.bfloat16)
+    for i in range(n):
+        spectrum = lax.dot_general(
+            table_ref[...],
+            images_ref[i],
+            (((1,), (1,)), ((), ())),
+            preferred_element_type=jnp.float32,
+        )
+        pieces = []
+        for c in range(2):
+            part = spectrum[c * total : (c + 1) * total]
+            turned = jnp.concatenate(
+                [(part * cb_ref[...]).astype(jnp.bfloat16), (part * sb_ref[...]).astype(jnp.bfloat16)],
+                axis=1,
+            )
+            coef = jnp.dot(turned, wave_ref[...], preferred_element_type=jnp.float32)
+            pieces.append(coef.reshape(plan.devices, plan.slots, radial))
+        both = jnp.concatenate(pieces, axis=1).astype(jnp.bfloat16)
+        coef_ref[:, 2 * plan.slots * i : 2 * plan.slots * (i + 1), :] = both
+
+
+def sweep(ref, base, step, lanes_of):
+    height = ref.shape[1]
+    shape = (8, 128)
+    start = pl.multiple_of(step * 8, 8)
+    panel = ref[base, pl.ds(start, 8), :]
+    sub = iota(shape, 0)
+    lane = iota(shape, 1)
+    for i in range(8):
+        index = lanes_of(lane, step * 8 + i)
+        here = lane == index
+        col = jnp.take_along_axis(panel, index, axis=1)
+        pivot = jnp.broadcast_to(col[i : i + 1], shape)
+        line = jnp.broadcast_to(panel[i : i + 1], shape)
+        scaled = jnp.where(here, 1.0, line) / pivot
+        rest = jnp.where(here, 0.0, panel) - col * scaled
+        panel = jnp.where(sub == i, scaled, rest)
+    full = (height, 128)
+    lane = iota(full, 1)
+    block = ref[base]
+    total = block
+    first = lanes_of(lane, step * 8)
+    total = jnp.where((lane >= first) & (lane < first + 8), 0.0, block)
+    for j in range(8):
+        col = jnp.take_along_axis(block, lanes_of(lane, step * 8 + j), axis=1)
+        total = total - col * panel[j : j + 1]
+    ref[base] = total
+    ref[base, pl.ds(start, 8), :] = panel
+
+
+def filter_kernel(
+    plan, order_ref, noise_ref, counts_ref, zeros_ref, recv_ref,
+    back_ref, low_ref, high_ref, wide_ref, full_ref, pair_ref, pick_ref,
+):
+    radial, quota, slots = plan.radial, plan.quota, plan.slots
+    narrow = radial // 2
+    rows = plan.devices * plan.vecs
+    freq_at, batch_at = lax.axis_index("freq"), lax.axis_index("batch")
+    wide_ref[...] = recv_ref[...].astype(jnp.float32).reshape(rows * slots, radial)
+    square = (radial, radial)
+    eye = (iota(square, 0) == iota(square, 1)).astype(jnp.float32)
+    noises = []
+    for s in range(slots):
+        side = s // quota
+        slot = freq_at * plan.owned + side * plan.half + batch_at * quota + (s - side * quota)
+        k = order_ref[slot]
+        noise = noise_ref[k]
+        noises.append(noise)
+        zero = zeros_ref[pl.ds(k, 1), :]
+        zero = jnp.where(iota((1, radial), 1) < counts_ref[k], zero, MASKED)
+        pick = (iota(square, 0) + 1 == zero).astype(jnp.float32).astype(jnp.bfloat16)
+        pick_ref[s] = pick
+        vectors = wide_ref[pl.ds(s, rows, stride=slots), :].astype(jnp.bfloat16)
+        coef = jnp.dot(vectors, pick, preferred_element_type=jnp.float32).astype(jnp.bfloat16)
+        gram = lax.dot_general(
+            coef, coef, (((0,), (0,)), ((), ())), preferred_element_type=jnp.float32
+        )
+        covariance = gram / float(rows) + noise * eye
+        if side == 0:
+            full_ref[s] = covariance
+        else:
+            at = s - quota
+            upper = covariance[:narrow]
+            if at % 2:
+                upper = pltpu.roll(upper, narrow, axis=1)
+                held = pair_ref[at // 2]
+                upper = jnp.where(iota((narrow, radial), 1) < narrow, held, upper)
+            pair_ref[at // 2] = upper
+    whole_lane = lambda lane, k: jnp.zeros_like(lane) + k
+    half_lane = lambda lane, k: (lane & narrow) + k
+
+    def both(step, carry):
+        for m in range(quota):
+            sweep(full_ref, m, step, whole_lane)
+        for m in range(quota // 2):
+            sweep(pair_ref, m, step, half_lane)
+        return carry
+
+    def lower(step, carry):
+        for m in range(quota):
+            sweep(full_ref, m, step, whole_lane)
+        return carry
+
+    lax.fori_loop(0, narrow // 8, both, 0)
+    lax.fori_loop(narrow // 8, radial // 8, lower, 0)
+    for s in range(slots):
+        side = s // quota
+        if side == 0:
+            shrink = eye - noises[s] * full_ref[s]
+            low_ref[s] = shrink
+        else:
+            at = s - quota
+            upper = pair_ref[at // 2]
+            if at % 2:
+                upper = pltpu.roll(upper, narrow, axis=1)
+            lane = iota((narrow, radial), 1)
+            upper = jnp.where(lane < narrow, eye[:narrow] - noises[s] * upper, 0.0)
+            shrink = jnp.concatenate([upper, jnp.zeros((radial - narrow, radial), jnp.float32)], axis=0)
+            high_ref[at] = upper
+        pick = pick_ref[s]
+        shrink = shrink.astype(jnp.bfloat16)
+        moved = lax.dot_general(
+            shrink, pick, (((0,), (1,)), ((), ())), preferred_element_type=jnp.float32
+        ).astype(jnp.bfloat16)
+        spread = jnp.dot(pick, moved, preferred_element_type=jnp.float32).astype(jnp.bfloat16)
+        vectors = wide_ref[pl.ds(s, rows, stride=slots), :].astype(jnp.bfloat16)
+        filtered = jnp.dot(vectors, spread, preferred_element_type=jnp.float32)
+        wide_ref[pl.ds(s, rows, stride=slots), :] = filtered
+    back_ref[...] = wide_ref[...].reshape(back_ref.shape).astype(jnp.bfloat16)
+
+
+def synthesis_kernel(
+    plan, table_ref, cb_ref, sb_ref, wave_ref, low_ref, high_ref, other_low_ref, other_high_ref,
+    recv_ref, out_ref, wiener_ref,
+):
+    n, radial, total = plan.count_img, plan.radial, plan.total
+    slots, quota = plan.slots, plan.quota
+    batch_at = lax.axis_index("batch")
+    for i in range(n):
+        both = recv_ref[:, 2 * slots * i : 2 * slots * (i + 1), :].astype(jnp.float32)
+        pieces = []
+        for c in range(2):
+            filtered = both[:, c * slots : (c + 1) * slots, :].reshape(total, radial)
+            turned = lax.dot_general(
+                filtered.astype(jnp.bfloat16),
+                wave_ref[...],
+                (((1,), (1,)), ((), ())),
+                preferred_element_type=jnp.float32,
+            )
+            part = turned[:, :radial] * cb_ref[...] + turned[:, radial:] * sb_ref[...]
+            pieces.append(part.astype(jnp.bfloat16))
+        spectrum = jnp.concatenate(pieces, axis=0)
+        image = lax.dot_general(
+            spectrum, table_ref[...], (((0,), (0,)), ((), ())), preferred_element_type=jnp.float32
+        )
+        out_ref[i] = image.astype(jnp.bfloat16)
+    for here, low, high in ((batch_at, low_ref, high_ref), (1 - batch_at, other_low_ref, other_high_ref)):
+        for s in range(quota):
+            wiener_ref[here * quota + s] = low[s]
+            narrow = radial // 2
+            at = plan.half + here * quota + s
+            wiener_ref[at, 0:narrow, :] = high[s]
+            wiener_ref[at, narrow:radial, :] = jnp.zeros((radial - narrow, radial), jnp.float32)
+
+
+VMEM = pl.BlockSpec(memory_space=pltpu.VMEM)
+SMEM = pl.BlockSpec(memory_space=pltpu.SMEM)
+
+
+def call(kernel, outs, ins, scratch=()):
+    return pl.pallas_call(
+        kernel,
+        out_shape=outs,
+        in_specs=ins,
+        out_specs=jax.tree.map(lambda _: VMEM, outs),
+        scratch_shapes=scratch,
+    )
+
+
+def fast_device(plan, images, radial_counts, order, zeros_table, noise_var):
+    both = ("batch", "freq")
+    radial, total, slots, quota = plan.radial, plan.total, plan.slots, plan.quota
+    narrow = radial // 2
+    width = plan.vecs * slots
+    shape = jax.ShapeDtypeStruct
+    coef, table, cb, sb, wave = call(
+        functools.partial(analysis_kernel, plan),
+        (
+            shape((plan.devices, width, radial), jnp.bfloat16),
+            shape((2 * total, plan.angles), jnp.bfloat16),
+            shape((total, radial), jnp.float32),
+            shape((total, radial), jnp.float32),
+            shape((2 * radial, radial), jnp.bfloat16),
+        ),
+        [VMEM, VMEM],
+    )(order.reshape(1, total), images)
+    recv = lax.all_to_all(coef, both, split_axis=0, concat_axis=0, tiled=True)
+    back, low, high = call(
+        functools.partial(filter_kernel, plan),
+        (
+            shape((plan.devices, width, radial), jnp.bfloat16),
+            shape((quota, radial, radial), jnp.float32),
+            shape((quota, narrow, radial), jnp.float32),
+        ),
+        [SMEM, SMEM, SMEM, VMEM, VMEM],
+        [
+            pltpu.VMEM((plan.devices * width, radial), jnp.float32),
+            pltpu.VMEM((quota, radial, radial), jnp.float32),
+            pltpu.VMEM((quota // 2, narrow, radial), jnp.float32),
+            pltpu.VMEM((slots, radial, radial), jnp.bfloat16),
+        ],
+    )(order, noise_var, radial_counts, zeros_table, recv)
+    swap = [(0, 1), (1, 0)]
+    other_low = lax.ppermute(low, "batch", swap)
+    other_high = lax.ppermute(high, "batch", swap)
+    returned = lax.all_to_all(back, both, split_axis=0, concat_axis=0, tiled=True)
+    return call(
+        functools.partial(synthesis_kernel, plan),
+        (
+            shape((plan.count_img, radial, plan.angles), jnp.bfloat16),
+            shape((plan.owned, radial, radial), jnp.float32),
+        ),
+        [VMEM] * 9,
+    )(table, cb, sb, wave, low, high, other_low, other_high, returned)
+
+
 def solution(mesh):
+    owners, batches = mesh.shape["freq"], mesh.shape["batch"]
+
+    def body(images, radial_counts, order, zeros_table, noise_var):
+        plan = Plan(images.shape, order.shape[0], owners, batches)
+        if plan.fits and batches == 2:
+            return fast_device(plan, images, radial_counts, order, zeros_table, noise_var)
+        return per_device(images, radial_counts, order, zeros_table, noise_var)
+
     return jax.shard_map(
-        per_device,
+        body,
         mesh=mesh,
         in_specs=(P(("batch", "freq"), None, None), P(), P(), P(), P()),
         out_specs=(P(("batch", "freq"), None, None), P("freq", None, None)),

time: 536 us -> 104 us (0.19)
  other arithmetic: 270 us -> 0 us
  matrix products: 153 us -> 0 us
  Pallas kernels: 0 us -> 59.6 us
  waiting for transfers between devices: 62.5 us -> 14.7 us
  blocking collectives: 0 us -> 23.3 us
  starting transfers between devices: 20.1 us -> 4.84 us
  between operations: 14.4 us -> 0.66 us
  local copies, waits for them, and re-layouts: 13.4 us -> 0.89 us
    another operation x20 -> x0, other arithmetic: 264 us -> none  [the longest x6 141 us: shrink_from(): lower = jnp.linalg.cholesky(covariance)]
    dot_general x22 -> x0, matrix products: 151 us -> none  [the longest x4 72.2 us: analyse(): jnp.einsum('ircj,jqr->jciq', spectrum, basis, preferred_element_type=jnp....]
    pallas_call x0 -> x3, Pallas kernels: none -> 59.6 us  [the longest x1 50.9 us: fast_device(): call(functools.partial(filter_kernel, plan), (shape((plan.devices, width,...]
    psum x1 -> x0, waiting for transfers between devices: 32.6 us -> none  [per_device(): lax.psum((gram_of(low_recv), gram_of(high_recv)), 'batch')]
    all_to_all x4 -> x1, waiting for transfers between devices: 29.9 us -> 0.01 us  [fast_device(): lax.all_to_all(back, both, split_axis=0, concat_axis=0, tiled=True)]
    all_to_all x0 -> x1, blocking collectives: none -> 23.3 us  [fast_device(): recv = lax.all_to_all(coef, both, split_axis=0, concat_axis=0, tiled=True)]
    all_to_all x4 -> x1, starting transfers between devices: 20.1 us -> 2.75 us  [fast_device(): lax.all_to_all(back, both, split_axis=0, concat_axis=0, tiled=True)]
    ppermute x0 -> x2, waiting for transfers between devices: none -> 14.7 us  [the longest x1 14.7 us: fast_device(): other_high = lax.ppermute(high, 'batch', swap)]
  transfers between devices with their start and end apart: 5 -> 3, of which waited for: 5 -> 1; matrix products, arithmetic and copies ran while one was open for 1% -> 0% of each run, Pallas kernels for 0% -> 0%
where the time goes in v1:
time: 104 us
  Pallas kernels  59.6 us (57%)
  blocking collectives  23.3 us (22%)
  waiting for transfers between devices  14.7 us (14%)
  starting transfers between devices  4.84 us (5%)
    pallas_call x1, Pallas kernels, fast_device(): call(functools.partial(filter_kernel, plan), (shape((plan.devices, width,...  50.9 us
    all_to_all x1, blocking collectives, fast_device(): recv = lax.all_to_all(coef, both, split_axis=0, concat_axis=0, tiled=True)  23.3 us
    ppermute x1, waiting for transfers between devices, fast_device(): other_high = lax.ppermute(high, 'batch', swap)  14.7 us
    pallas_call x1, Pallas kernels, fast_device(): call(functools.partial(analysis_kernel, plan), (shape((plan.devices, widt...  4.58 us
    pallas_call x1, Pallas kernels, fast_device(): call(functools.partial(synthesis_kernel, plan), (shape((plan.count_img, r...  4.11 us
    all_to_all x1, starting transfers between devices, fast_device(): lax.all_to_all(back, both, split_axis=0, concat_axis=0, tiled=True)  2.75 us
  transfers between devices with their start and end apart: 3, of which 1 were waited for; matrix products, arithmetic and copies ran while one was open for 0% of the time, Pallas kernels for 0%

profile of v1, /device:TPU:0, one launch (start us, length us, event | category | flops | bytes accessed | tf_op | source)
XLA Modules:
  0.0 104.0 jit_solution(8377163038846447078)
XLA Ops:
  0.6 4.6 %shard_map.68 = (bf16[32,64,128]{2,1,0:T(8,128)(2,1)}, bf16[512,512]{1,0:T(8,128)(2,1)}, f32[256,128]{1,0:T(8,128)}, f32[256,128]{1,0:T(8,128)}, bf16[256,128]{1,0:T(8,128)(2,1)}) custom-call(s32[1,256]{1,0:T(1,128)} %bitcast.1, bf16[4,128,512]{2,1,0:T(8,128)(2,1)} %images_ref.1), custom_call_target="tpu_custom_call" | custom-call | tf_op jit(solution)/shard_map/pallas_call | solution.py:399
  5.2 23.3 %all_to_all.10.recv_ref = bf16[32,64,128]{2,1,0:T(8,128)(2,1)} all-to-all(bf16[32,64,128]{2,1,0:T(8,128)(2,1)} %get-tuple-element.14), channel_id=1, replica_groups=mesh['batch'=2,'freq'=16] {'batch','freq'}, dimensions={0} | all-to-all | bytes 1048576 | tf_op jit(solution)/shard_map/all_to_all | solution.py:410
  28.5 50.9 %shard_map.69 = (bf16[32,64,128]{2,1,0:T(8,128)(2,1)}, f32[4,128,128]{2,1,0:T(8,128)}, f32[4,64,128]{2,1,0:T(8,128)}) custom-call(s32[256]{0:T(256)} %order_ref.1, f32[256]{0:T(256)} %noise_ref.1, s32[256]{0:T(256)} %counts_ref.1, s32[256,128]{1,0:T(8,128)} %zeros_ref.1, bf16[32,64,128]{2,1,0:T(8,128)(2,1)} %all_to_all.10.recv_ref), custom_call_target="tpu_custom_call" | custom-call | tf_op jit(solution)/shard_map/pallas_call | solution.py:411
  79.4 0.0 copy-start.1
  79.4 0.0 copy-start.3
  79.4 2.8 %all-to-all-start.1 = ((bf16[32,64,128]{2,1,0:T(8,128)(2,1)}), bf16[32,64,128]{2,1,0:T(8,128)(2,1)S(1)}, u32[]{:S(2)}, u32[]{:S(2)}) async-start(bf16[32,64,128]{2,1,0:T(8,128)(2,1)} %get-tuple-element.17), calls=%async_computation.1 | async-start | bytes 1048576 | tf_op jit(solution)/shard_map/all_to_all | solution.py:429
  82.2 0.0 copy-done.1
  82.2 1.7 %collective-permute-start = (f32[4,128,128]{2,1,0:T(8,128)S(1)}, f32[4,128,128]{2,1,0:T(8,128)S(1)}, u32[]{:S(2)}, u32[]{:S(2)}) collective-permute-start(f32[4,128,128]{2,1,0:T(8,128)S(1)} %copy-done.1), channel_id=1, source_target_pairs={{0,16},{16,0},{1,17},{17,1},{2,18},{18,2},{3,19},{19,3},{4,20},{20... | collective-permute-start | bytes 786440 | tf_op jit(solution)/shard_map/ppermute | solution.py:427
  83.9 0.0 copy-done.3
  83.9 0.4 collective-permute-start.1
  84.3 14.7 %collective-permute-done.1.other_high_ref = f32[4,64,128]{2,1,0:T(8,128)S(1)} collective-permute-done((f32[4,64,128]{2,1,0:T(8,128)S(1)}, f32[4,64,128]{2,1,0:T(8,128)S(1)}, u32[]{:S(2)}, u32[]{:S(2)}) %collective-permute-start.1) | collective-permute-done | bytes 131104 | tf_op jit(solution)/shard_map/ppermute | solution.py:428
  99.0 0.0 copy-start.4
  99.0 0.0 collective-permute-done.other_low_ref
  99.0 0.0 copy-start.2
  99.0 0.0 all-to-all-done.1.recv_ref
  99.0 0.0 copy-start
  99.0 0.6 copy-done.4
  99.6 0.1 copy-done.2
  99.7 0.1 copy-done
  99.9 4.1 %shard_map.70 = (bf16[4,128,512]{2,1,0:T(8,128)(2,1)}, f32[16,128,128]{2,1,0:T(8,128)}) custom-call(bf16[512,512]{1,0:T(8,128)(2,1)} %get-tuple-element.10.table_ref, f32[256,128]{1,0:T(8,128)} %get-tuple-element.11.cb_ref, f32[256,128]{1,0:T(8,128)} %get-tuple-element.12.sb_ref, bf16[256,128]{1,0:T(8,128)(2,1)} %get-tuple-element.13.wave_ref, ...), custom_call_target="tpu_custom_call" | custom-call | tf_op jit(solution)/shard_map/pallas_call | solution.py:430
Async XLA Ops:
  79.4 2.8 %copy-start.1 = (f32[4,128,128]{2,1,0:T(8,128)S(1)}, f32[4,128,128]{2,1,0:T(8,128)}, u32[]{:S(2)}) copy-start(f32[4,128,128]{2,1,0:T(8,128)} %get-tuple-element.15.low_ref) | copy-start | bytes 786436
  79.4 4.5 %copy-start.3 = (f32[4,64,128]{2,1,0:T(8,128)S(1)}, f32[4,64,128]{2,1,0:T(8,128)}, u32[]{:S(2)}) copy-start(f32[4,64,128]{2,1,0:T(8,128)} %get-tuple-element.16.high_ref) | copy-start | bytes 393220
  79.4 19.5 %all-to-all-start.1 = ((bf16[32,64,128]{2,1,0:T(8,128)(2,1)}), bf16[32,64,128]{2,1,0:T(8,128)(2,1)S(1)}, u32[]{:S(2)}, u32[]{:S(2)}) async-start(bf16[32,64,128]{2,1,0:T(8,128)(2,1)} %get-tuple-element.17), calls=%async_computation.1 | async-start | bytes 1048576 | tf_op jit(solution)/shard_map/all_to_all | solution.py:429
  82.2 16.8 %collective-permute-start = (f32[4,128,128]{2,1,0:T(8,128)S(1)}, f32[4,128,128]{2,1,0:T(8,128)S(1)}, u32[]{:S(2)}, u32[]{:S(2)}) collective-permute-start(f32[4,128,128]{2,1,0:T(8,128)S(1)} %copy-done.1), channel_id=1, source_target_pairs={{0,16},{16,0},{1,17},{17,1},{2,18},{18,2},{3,19},{19,3},{4,20},{20... | collective-permute-start | bytes 786440 | tf_op jit(solution)/shard_map/ppermute | solution.py:427
  83.9 15.0 %collective-permute-start.1 = (f32[4,64,128]{2,1,0:T(8,128)S(1)}, f32[4,64,128]{2,1,0:T(8,128)S(1)}, u32[]{:S(2)}, u32[]{:S(2)}) collective-permute-start(f32[4,64,128]{2,1,0:T(8,128)S(1)} %copy-done.3), channel_id=1, source_target_pairs={{0,16},{16,0},{1,17},{17,1},{2,18},{18,2},{3,19},{19,3},{4,20},{20... | collective-permute-start | bytes 393224 | tf_op jit(solution)/shard_map/ppermute | solution.py:428
  99.0 0.7 copy-start.4
  99.0 0.7 copy-start.2
  99.0 0.9 copy-start

commit v2 on v1

--- a/solution.py
+++ b/solution.py
@@ -232,33 +232,81 @@
         coef_ref[:, 2 * plan.slots * i : 2 * plan.slots * (i + 1), :] = both
 
 
-def sweep(ref, base, step, lanes_of):
-    height = ref.shape[1]
+def thirds(x):
+    first = x.astype(jnp.bfloat16)
+    rest = x - first.astype(jnp.float32)
+    second = rest.astype(jnp.bfloat16)
+    third = (rest - second.astype(jnp.float32)).astype(jnp.bfloat16)
+    return first, second, third
+
+
+def outer(u, v):
+    u1, u2, u3 = thirds(u)
+    v1, v2, v3 = thirds(v)
+    return lax.dot_general(
+        jnp.concatenate([u1, u1, u1, u2, u2, u3], axis=0),
+        jnp.concatenate([v1, v2, v3, v1, v2, v1], axis=0),
+        (((0,), (0,)), ((), ())),
+        preferred_element_type=jnp.float32,
+    )
+
+
+def first_lane(halved, lane, step):
+    return (lane & 64 if halved else jnp.zeros_like(lane)) + step * 8
+
+
+def pivot_panels(panels, halves, step):
     shape = (8, 128)
+    sub, lane = iota(shape, 0), iota(shape, 1)
+    blocks = [
+        [
+            jnp.take_along_axis(panel, first_lane(halved, lane, step) + j, axis=1)
+            for j in range(8)
+        ]
+        for panel, halved in zip(panels, halves)
+    ]
+    for i in range(8):
+        for at, cols in enumerate(blocks):
+            inverse = 1.0 / jnp.broadcast_to(cols[i][i : i + 1], shape)
+            fresh = []
+            for j in range(8):
+                if j == i:
+                    fresh.append(jnp.where(sub == i, inverse, -cols[i] * inverse))
+                else:
+                    line = jnp.broadcast_to(cols[j][i : i + 1], shape) * inverse
+                    fresh.append(jnp.where(sub == i, line, cols[j] - cols[i] * line))
+            blocks[at] = fresh
+    solved = []
+    for panel, halved, cols in zip(panels, halves, blocks):
+        offset = lane - first_lane(halved, lane, step)
+        outside = (offset < 0) | (offset >= 8)
+        total = jnp.zeros(shape, jnp.float32)
+        for j in range(8):
+            line = jnp.broadcast_to(panel[j : j + 1], shape)
+            line = jnp.where(outside, line, jnp.where(offset == j, 1.0, 0.0))
+            total = total + cols[j] * line
+        solved.append(total)
+    return solved
+
+
+def sweep(matrices, step, carry):
     start = pl.multiple_of(step * 8, 8)
-    panel = ref[base, pl.ds(start, 8), :]
-    sub = iota(shape, 0)
-    lane = iota(shape, 1)
-    for i in range(8):
-        index = lanes_of(lane, step * 8 + i)
-        here = lane == index
-        col = jnp.take_along_axis(panel, index, axis=1)
-        pivot = jnp.broadcast_to(col[i : i + 1], shape)
-        line = jnp.broadcast_to(panel[i : i + 1], shape)
-        scaled = jnp.where(here, 1.0, line) / pivot
-        rest = jnp.where(here, 0.0, panel) - col * scaled
-        panel = jnp.where(sub == i, scaled, rest)
-    full = (height, 128)
-    lane = iota(full, 1)
-    block = ref[base]
-    total = block
-    first = lanes_of(lane, step * 8)
-    total = jnp.where((lane >= first) & (lane < first + 8), 0.0, block)
-    for j in range(8):
-        col = jnp.take_along_axis(block, lanes_of(lane, step * 8 + j), axis=1)
-        total = total - col * panel[j : j + 1]
-    ref[base] = total
-    ref[base, pl.ds(start, 8), :] = panel
+    halves = [halved for _, _, halved in matrices]
+    panels = [ref[m, pl.ds(start, 8), :] for ref, m, _ in matrices]
+    solved = pivot_panels(panels, halves, step)
+    for (ref, m, halved), panel, fresh in zip(matrices, panels, solved):
+        height = ref.shape[1]
+        lane = iota((8, 128), 1)
+        done = (lane & 63 if halved else lane) < step * 8
+        update = outer(jnp.where(done, -panel, panel), fresh)
+        lane = iota((height, 128), 1)
+        if halved:
+            update = jnp.where(lane < 64, update[:height], update[height:])
+        offset = lane - first_lane(halved, lane, step)
+        rest = jnp.where((offset >= 0) & (offset < 8), 0.0, ref[m])
+        ref[m] = rest - update
+        ref[m, pl.ds(start, 8), :] = fresh
+    return carry
 
 
 def filter_kernel(
@@ -299,23 +347,11 @@
                 held = pair_ref[at // 2]
                 upper = jnp.where(iota((narrow, radial), 1) < narrow, held, upper)
             pair_ref[at // 2] = upper
-    whole_lane = lambda lane, k: jnp.zeros_like(lane) + k
-    half_lane = lambda lane, k: (lane & narrow) + k
-
-    def both(step, carry):
-        for m in range(quota):
-            sweep(full_ref, m, step, whole_lane)
-        for m in range(quota // 2):
-            sweep(pair_ref, m, step, half_lane)
-        return carry
-
-    def lower(step, carry):
-        for m in range(quota):
-            sweep(full_ref, m, step, whole_lane)
-        return carry
-
+    lower = [(full_ref, m, False) for m in range(quota)]
+    upper_pairs = [(pair_ref, m, True) for m in range(quota // 2)]
+    both = functools.partial(sweep, lower + upper_pairs)
     lax.fori_loop(0, narrow // 8, both, 0)
-    lax.fori_loop(narrow // 8, radial // 8, lower, 0)
+    lax.fori_loop(narrow // 8, radial // 8, functools.partial(sweep, lower), 0)
     for s in range(slots):
         side = s // quota
         if side == 0:

time: 104 us -> 65.9 us (0.63)
  Pallas kernels: 59.6 us -> 21.1 us
    pallas_call x1, Pallas kernels: 50.9 us -> 12.4 us  [fast_device(): call(functools.partial(filter_kernel, plan), (shape((plan.devices, width,...]
where the time goes in v2:
time: 65.9 us; the launch traced here: 65.5 us
  blocking collectives  23.3 us (35%)
  Pallas kernels  21.1 us (32%)
  waiting for transfers between devices  14.7 us (22%)
  starting transfers between devices  4.84 us (7%)
  local copies, waits for them, and re-layouts  0.89 us (1%)
  between operations  0.66 us (1%)
    all_to_all x1, blocking collectives, fast_device(): recv = lax.all_to_all(coef, both, split_axis=0, concat_axis=0, tiled=True)  23.3 us
    ppermute x1, waiting for transfers between devices, fast_device(): other_high = lax.ppermute(high, 'batch', swap)  14.7 us
    pallas_call x1, Pallas kernels, fast_device(): call(functools.partial(filter_kernel, plan), (shape((plan.devices, width,...  12.4 us
    pallas_call x1, Pallas kernels, fast_device(): call(functools.partial(analysis_kernel, plan), (shape((plan.devices, widt...  4.58 us
    pallas_call x1, Pallas kernels, fast_device(): call(functools.partial(synthesis_kernel, plan), (shape((plan.count_img, r...  4.1 us
    all_to_all x1, starting transfers between devices, fast_device(): lax.all_to_all(back, both, split_axis=0, concat_axis=0, tiled=True)  2.75 us
    ppermute x1, starting transfers between devices, fast_device(): other_low = lax.ppermute(low, 'batch', swap)  1.72 us
  transfers between devices with their start and end apart: 3, of which 1 were waited for; matrix products, arithmetic and copies ran while one was open for 0% of the time, Pallas kernels for 0%

profile of v2, /device:TPU:0, one launch (start us, length us, event | category | flops | bytes accessed | tf_op | source)
XLA Modules:
  0.0 65.5 jit_solution(15553612436645392077)
XLA Ops:
  0.6 4.6 %shard_map.68 = (bf16[32,64,128]{2,1,0:T(8,128)(2,1)}, bf16[512,512]{1,0:T(8,128)(2,1)}, f32[256,128]{1,0:T(8,128)}, f32[256,128]{1,0:T(8,128)}, bf16[256,128]{1,0:T(8,128)(2,1)}) custom-call(s32[1,256]{1,0:T(1,128)} %bitcast.1, bf16[4,128,512]{2,1,0:T(8,128)(2,1)} %images_ref.1), custom_call_target="tpu_custom_call" | custom-call | tf_op jit(solution)/shard_map/pallas_call | solution.py:435
  5.2 23.3 %all_to_all.10.recv_ref = bf16[32,64,128]{2,1,0:T(8,128)(2,1)} all-to-all(bf16[32,64,128]{2,1,0:T(8,128)(2,1)} %get-tuple-element.14), channel_id=1, replica_groups=mesh['batch'=2,'freq'=16] {'batch','freq'}, dimensions={0} | all-to-all | bytes 1048576 | tf_op jit(solution)/shard_map/all_to_all | solution.py:446
  28.5 12.4 %shard_map.69 = (bf16[32,64,128]{2,1,0:T(8,128)(2,1)}, f32[4,128,128]{2,1,0:T(8,128)}, f32[4,64,128]{2,1,0:T(8,128)}) custom-call(s32[256]{0:T(256)} %order_ref.1, f32[256]{0:T(256)} %noise_ref.1, s32[256]{0:T(256)} %counts_ref.1, s32[256,128]{1,0:T(8,128)} %zeros_ref.1, bf16[32,64,128]{2,1,0:T(8,128)(2,1)} %all_to_all.10.recv_ref), custom_call_target="tpu_custom_call" | custom-call | tf_op jit(solution)/shard_map/pallas_call | solution.py:447
  41.0 0.0 copy-start.1
  41.0 0.0 copy-start.3
  41.0 2.8 %all-to-all-start.1 = ((bf16[32,64,128]{2,1,0:T(8,128)(2,1)}), bf16[32,64,128]{2,1,0:T(8,128)(2,1)S(1)}, u32[]{:S(2)}, u32[]{:S(2)}) async-start(bf16[32,64,128]{2,1,0:T(8,128)(2,1)} %get-tuple-element.17), calls=%async_computation.1 | async-start | bytes 1048576 | tf_op jit(solution)/shard_map/all_to_all | solution.py:465
  43.7 0.0 copy-done.1
  43.7 1.7 %collective-permute-start = (f32[4,128,128]{2,1,0:T(8,128)S(1)}, f32[4,128,128]{2,1,0:T(8,128)S(1)}, u32[]{:S(2)}, u32[]{:S(2)}) collective-permute-start(f32[4,128,128]{2,1,0:T(8,128)S(1)} %copy-done.1), channel_id=1, source_target_pairs={{0,16},{16,0},{1,17},{17,1},{2,18},{18,2},{3,19},{19,3},{4,20},{20... | collective-permute-start | bytes 786440 | tf_op jit(solution)/shard_map/ppermute | solution.py:463
  45.4 0.0 copy-done.3
  45.4 0.4 collective-permute-start.1
  45.8 14.7 %collective-permute-done.1.other_high_ref = f32[4,64,128]{2,1,0:T(8,128)S(1)} collective-permute-done((f32[4,64,128]{2,1,0:T(8,128)S(1)}, f32[4,64,128]{2,1,0:T(8,128)S(1)}, u32[]{:S(2)}, u32[]{:S(2)}) %collective-permute-start.1) | collective-permute-done | bytes 131104 | tf_op jit(solution)/shard_map/ppermute | solution.py:464
  60.5 0.0 copy-start.4
  60.5 0.0 collective-permute-done.other_low_ref
  60.5 0.0 copy-start.2
  60.5 0.0 all-to-all-done.1.recv_ref
  60.5 0.0 copy-start
  60.5 0.6 copy-done.4
  61.2 0.1 copy-done.2
  61.2 0.1 copy-done
  61.4 4.1 %shard_map.70 = (bf16[4,128,512]{2,1,0:T(8,128)(2,1)}, f32[16,128,128]{2,1,0:T(8,128)}) custom-call(bf16[512,512]{1,0:T(8,128)(2,1)} %get-tuple-element.10.table_ref, f32[256,128]{1,0:T(8,128)} %get-tuple-element.11.cb_ref, f32[256,128]{1,0:T(8,128)} %get-tuple-element.12.sb_ref, bf16[256,128]{1,0:T(8,128)(2,1)} %get-tuple-element.13.wave_ref, ...), custom_call_target="tpu_custom_call" | custom-call | tf_op jit(solution)/shard_map/pallas_call | solution.py:466
Async XLA Ops:
  41.0 2.8 %copy-start.1 = (f32[4,128,128]{2,1,0:T(8,128)S(1)}, f32[4,128,128]{2,1,0:T(8,128)}, u32[]{:S(2)}) copy-start(f32[4,128,128]{2,1,0:T(8,128)} %get-tuple-element.15.low_ref) | copy-start | bytes 786436
  41.0 4.5 %copy-start.3 = (f32[4,64,128]{2,1,0:T(8,128)S(1)}, f32[4,64,128]{2,1,0:T(8,128)}, u32[]{:S(2)}) copy-start(f32[4,64,128]{2,1,0:T(8,128)} %get-tuple-element.16.high_ref) | copy-start | bytes 393220
  41.0 19.5 %all-to-all-start.1 = ((bf16[32,64,128]{2,1,0:T(8,128)(2,1)}), bf16[32,64,128]{2,1,0:T(8,128)(2,1)S(1)}, u32[]{:S(2)}, u32[]{:S(2)}) async-start(bf16[32,64,128]{2,1,0:T(8,128)(2,1)} %get-tuple-element.17), calls=%async_computation.1 | async-start | bytes 1048576 | tf_op jit(solution)/shard_map/all_to_all | solution.py:465
  43.7 16.8 %collective-permute-start = (f32[4,128,128]{2,1,0:T(8,128)S(1)}, f32[4,128,128]{2,1,0:T(8,128)S(1)}, u32[]{:S(2)}, u32[]{:S(2)}) collective-permute-start(f32[4,128,128]{2,1,0:T(8,128)S(1)} %copy-done.1), channel_id=1, source_target_pairs={{0,16},{16,0},{1,17},{17,1},{2,18},{18,2},{3,19},{19,3},{4,20},{20... | collective-permute-start | bytes 786440 | tf_op jit(solution)/shard_map/ppermute | solution.py:463
  45.4 15.0 %collective-permute-start.1 = (f32[4,64,128]{2,1,0:T(8,128)S(1)}, f32[4,64,128]{2,1,0:T(8,128)S(1)}, u32[]{:S(2)}, u32[]{:S(2)}) collective-permute-start(f32[4,64,128]{2,1,0:T(8,128)S(1)} %copy-done.3), channel_id=1, source_target_pairs={{0,16},{16,0},{1,17},{17,1},{2,18},{18,2},{3,19},{19,3},{4,20},{20... | collective-permute-start | bytes 393224 | tf_op jit(solution)/shard_map/ppermute | solution.py:464
  60.5 0.7 %copy-start.4 = (f32[4,64,128]{2,1,0:T(8,128)}, f32[4,64,128]{2,1,0:T(8,128)S(1)}, u32[]{:S(2)}) copy-start(f32[4,64,128]{2,1,0:T(8,128)S(1)} %collective-permute-done.1.other_high_ref) | copy-start | bytes 393220
  60.5 0.7 %copy-start.2 = (f32[4,128,128]{2,1,0:T(8,128)}, f32[4,128,128]{2,1,0:T(8,128)S(1)}, u32[]{:S(2)}) copy-start(f32[4,128,128]{2,1,0:T(8,128)S(1)} %collective-permute-done.other_low_ref) | copy-start | bytes 786436
  60.5 0.9 %copy-start = (bf16[32,64,128]{2,1,0:T(8,128)(2,1)}, bf16[32,64,128]{2,1,0:T(8,128)(2,1)S(1)}, u32[]{:S(2)}) copy-start(bf16[32,64,128]{2,1,0:T(8,128)(2,1)S(1)} %all-to-all-done.1.recv_ref) | copy-start | bytes 1572868

commit v3 on v0

--- a/solution.py
+++ b/solution.py
@@ -1,8 +1,11 @@
+import functools
 import math
 
 import jax
 import jax.numpy as jnp
 from jax import lax
+from jax.experimental import pallas as pl
+from jax.experimental.pallas import tpu as pltpu
 from jax.sharding import PartitionSpec as P
 
 
@@ -135,9 +138,426 @@
     return (denoised, wiener_blocks)
 
 
+COSINE = (
+    -0.9999999889445799,
+    4.934801116644238,
+    -4.058694745523659,
+    1.3351580223122241,
+    -0.23502902263765682,
+    0.025358285764913842,
+    -0.0015936782168350142,
+)
+
+
+def cosine_of(turns, steps):
+    x = ((turns & (steps - 1)) - steps // 2).astype(jnp.float32) * (2.0 / steps)
+    y = x * x
+    total = jnp.full_like(y, COSINE[-1])
+    for term in COSINE[-2::-1]:
+        total = total * y + term
+    return total
+
+
+def iota(shape, dim):
+    return lax.broadcasted_iota(jnp.int32, shape, dim)
+
+
+def nt(a, b):
+    return lax.dot_general(a, b, (((1,), (1,)), ((), ())), preferred_element_type=jnp.float32)
+
+
+def tn(a, b):
+    return lax.dot_general(a, b, (((0,), (0,)), ((), ())), preferred_element_type=jnp.float32)
+
+
+def nn(a, b):
+    return jnp.dot(a, b, preferred_element_type=jnp.float32)
+
+
+def low_bits(mask):
+    return mask.astype(jnp.float32).astype(jnp.bfloat16)
+
+
+class Plan:
+    def __init__(self, images, order, owners, batches):
+        self.count_img, self.radial, self.angles = images
+        self.total = order
+        self.owners, self.batches = owners, batches
+        self.devices = owners * batches
+        self.owned = order // owners
+        self.half = self.owned // 2
+        self.vecs = 2 * self.count_img
+        self.quota = 4
+        self.pairs = self.quota // 2
+        self.narrow = self.radial // 2
+        self.low_rows = self.vecs * self.quota
+        self.rows = self.low_rows + self.vecs * self.pairs
+        self.all_pairs = self.devices * self.pairs
+        power = lambda n: n > 0 and n & (n - 1) == 0
+        self.fits = (
+            batches == 2
+            and self.half == batches * self.quota
+            and self.radial == 128
+            and self.count_img == 4
+            and all(power(n) for n in (self.angles, self.total, owners))
+            and self.angles == 2 * self.total
+        )
+
+    def slot_of(self, device, place):
+        batch, owner = device // self.owners, device & (self.owners - 1)
+        return owner * self.owned + batch * self.quota + place
+
+
+def analysis_kernel(
+    plan, order_ref, counts_ref, zeros_ref, images_ref,
+    coef_ref, table_ref, cb_ref, sb_ref, wave_ref, zero_ref, wide_ref,
+):
+    radial, angles, total = plan.radial, plan.angles, plan.total
+    quota, pairs, narrow = plan.quota, plan.pairs, plan.narrow
+    row = iota((2 * total, total), 0)
+    high = row - total
+    low_slot = plan.slot_of(row // (2 * quota), row & (quota - 1))
+    pair = high & (plan.all_pairs - 1)
+    side = high // (2 * plan.all_pairs)
+    place = plan.half + 2 * (pair & (pairs - 1)) + side
+    high_slot = plan.slot_of(pair // pairs, place)
+    slot = jnp.where(row < total, low_slot, high_slot)
+    pick = low_bits(slot == iota((2 * total, total), 1))
+    spread = lambda ref: jnp.broadcast_to(ref[...].astype(jnp.float32), (128, total)).astype(jnp.bfloat16)
+    held = spread(order_ref)
+    freq = nt(pick, held).astype(jnp.int32)
+    row = iota((2 * total, 128), 0)
+    lane = iota((2 * total, 128), 1)
+    sine_row = jnp.where(row < total, row // quota, row // plan.all_pairs) & 1
+    lag = sine_row * (angles // 4)
+    flip = (1 - 2 * (freq & 1)).astype(jnp.float32)
+    factor = math.sqrt(2.0 / angles)
+    for part in range(angles // 256):
+        cosine = cosine_of((lane + part * 128) * freq - lag, angles) * factor
+        table_ref[:, part * 128 : part * 128 + 128] = cosine.astype(jnp.bfloat16)
+        start = angles // 2 + part * 128
+        table_ref[:, start : start + 128] = (cosine * flip).astype(jnp.bfloat16)
+    steps = 16 * radial
+    turns = (2 * freq - 1) * (2 * lane + 1) - 4 * radial * freq - 2 * radial
+    cb_ref[...] = cosine_of(turns, steps)
+    sb_ref[...] = cosine_of(turns - steps // 4, steps)
+    turns = (iota((radial, radial), 1) + 1) * (2 * iota((radial, radial), 0) + 1)
+    factor = math.sqrt(2.0 / radial)
+    wave_ref[0:radial, :] = (factor * cosine_of(turns, 4 * radial)).astype(jnp.bfloat16)
+    wave_ref[radial : 2 * radial, :] = (-factor * cosine_of(turns - radial, 4 * radial)).astype(
+        jnp.bfloat16
+    )
+    by_freq = low_bits(iota((total, total), 0) == iota((total, total), 1))
+    counts = nt(by_freq, spread(counts_ref)).astype(jnp.int32)
+    zeros = jnp.where(iota((total, radial), 1) < counts, zeros_ref[...], 0)
+    zeros = zeros.astype(jnp.float32).astype(jnp.bfloat16)
+    freq_lane = iota((plan.all_pairs, total), 1)
+    sides = []
+    for e in range(2):
+        start = total + e * 2 * plan.all_pairs
+        named = freq[start : start + plan.all_pairs]
+        named = jnp.concatenate([named] * (total // 128), axis=1)
+        sides.append(nn(low_bits(named == freq_lane), zeros))
+    lane = iota((plan.all_pairs, radial), 1)
+    zero_ref[...] = jnp.where(lane < narrow, sides[0], pltpu.roll(sides[1], narrow, axis=1)).astype(
+        jnp.int32
+    )
+    images = images_ref[...].reshape(plan.count_img * radial, angles)
+    for two in range(plan.count_img // 2):
+        spectrum = nt(table_ref[...], images[2 * two * radial : 2 * (two + 1) * radial])
+        lows = []
+        for i in range(2):
+            part = spectrum[:, i * radial : (i + 1) * radial]
+            turned = jnp.concatenate(
+                [(part * cb_ref[...]).astype(jnp.bfloat16), (part * sb_ref[...]).astype(jnp.bfloat16)],
+                axis=1,
+            )
+            coef = nn(turned, wave_ref[...])
+            lows.append(coef[:total].reshape(plan.devices, 2 * quota, radial))
+            span = 2 * plan.all_pairs
+            for e in range(2):
+                at = (e * plan.count_img + 2 * two + i) * span
+                wide_ref[at : at + span, :] = coef[total + e * span : total + (e + 1) * span]
+        size = 4 * quota
+        coef_ref[:, size * two : size * (two + 1), :] = jnp.concatenate(lows, axis=1).astype(
+            jnp.bfloat16
+        )
+    lane = iota((plan.vecs, radial), 1)
+    zero_here = iota((radial, radial), 0) + 1
+    for device in range(plan.devices):
+        tiles = []
+        for i in range(pairs):
+            at = device * pairs + i
+            vectors = wide_ref[pl.ds(at, 2 * plan.vecs, stride=plan.all_pairs), :]
+            chosen = low_bits(zero_here == zero_ref[at : at + 1, :])
+            both = nn(vectors.astype(jnp.bfloat16), chosen)
+            tiles.append(jnp.where(lane < narrow, both[: plan.vecs], both[plan.vecs :]))
+        coef_ref[device, plan.low_rows : plan.rows, :] = jnp.concatenate(tiles, axis=0).astype(
+            jnp.bfloat16
+        )
+
+
+def thirds(x):
+    first = x.astype(jnp.bfloat16)
+    rest = x - first.astype(jnp.float32)
+    second = rest.astype(jnp.bfloat16)
+    third = (rest - second.astype(jnp.float32)).astype(jnp.bfloat16)
+    return first, second, third
+
+
+def outer(u, v):
+    u1, u2, u3 = thirds(u)
+    v1, v2, v3 = thirds(v)
+    return lax.dot_general(
+        jnp.concatenate([u1, u1, u1, u2, u2, u3], axis=0),
+        jnp.concatenate([v1, v2, v3, v1, v2, v1], axis=0),
+        (((0,), (0,)), ((), ())),
+        preferred_element_type=jnp.float32,
+    )
+
+
+def first_lane(halved, lane, step):
+    return (lane & 64 if halved else jnp.zeros_like(lane)) + step * 8
+
+
+def pivot_panels(panels, halves, step):
+    shape = (8, 128)
+    sub, lane = iota(shape, 0), iota(shape, 1)
+    blocks = [
+        [
+            jnp.take_along_axis(panel, first_lane(halved, lane, step) + j, axis=1)
+            for j in range(8)
+        ]
+        for panel, halved in zip(panels, halves)
+    ]
+    for i in range(8):
+        for at, cols in enumerate(blocks):
+            inverse = 1.0 / jnp.broadcast_to(cols[i][i : i + 1], shape)
+            fresh = []
+            for j in range(8):
+                if j == i:
+                    fresh.append(jnp.where(sub == i, inverse, -cols[i] * inverse))
+                else:
+                    line = jnp.broadcast_to(cols[j][i : i + 1], shape) * inverse
+                    fresh.append(jnp.where(sub == i, line, cols[j] - cols[i] * line))
+            blocks[at] = fresh
+    solved = []
+    for panel, halved, cols in zip(panels, halves, blocks):
+        offset = lane - first_lane(halved, lane, step)
+        outside = (offset < 0) | (offset >= 8)
+        total = jnp.zeros(shape, jnp.float32)
+        for j in range(8):
+            line = jnp.broadcast_to(panel[j : j + 1], shape)
+            line = jnp.where(outside, line, jnp.where(offset == j, 1.0, 0.0))
+            total = total + cols[j] * line
+        solved.append(total)
+    return solved
+
+
+def sweep(matrices, step, carry):
+    start = pl.multiple_of(step * 8, 8)
+    halves = [halved for _, _, halved in matrices]
+    panels = [ref[m, pl.ds(start, 8), :] for ref, m, _ in matrices]
+    solved = pivot_panels(panels, halves, step)
+    for (ref, m, halved), panel, fresh in zip(matrices, panels, solved):
+        height = ref.shape[1]
+        lane = iota((8, 128), 1)
+        done = (lane & 63 if halved else lane) < step * 8
+        update = outer(jnp.where(done, -panel, panel), fresh)
+        lane = iota((height, 128), 1)
+        if halved:
+            update = jnp.where(lane < 64, update[:height], update[height:])
+        offset = lane - first_lane(halved, lane, step)
+        rest = jnp.where((offset >= 0) & (offset < 8), 0.0, ref[m])
+        ref[m] = rest - update
+        ref[m, pl.ds(start, 8), :] = fresh
+    return carry
+
+
+def filter_kernel(
+    plan, order_ref, noise_ref, counts_ref, zeros_ref, recv_ref,
+    back_ref, shrink_ref, wide_ref, full_ref, pair_ref, pick_ref, held_ref,
+):
+    radial, quota, pairs, narrow = plan.radial, plan.quota, plan.pairs, plan.narrow
+    low_rows = plan.low_rows
+    rows = plan.devices * plan.vecs
+    base = lax.axis_index("freq") * plan.owned + lax.axis_index("batch") * quota
+    low_part = recv_ref[:, :low_rows, :].astype(jnp.float32)
+    wide_ref[...] = low_part.reshape(plan.devices * low_rows, radial)
+    square = (radial, radial)
+    strip = (narrow, radial)
+    eye = (iota(square, 0) == iota(square, 1)).astype(jnp.float32)
+    twins = (iota(strip, 0) == (iota(strip, 1) & (narrow - 1))).astype(jnp.float32)
+    first = iota(strip, 1) < narrow
+    noises = []
+    for s in range(quota):
+        k = order_ref[base + s]
+        noises.append(noise_ref[k])
+        zero = zeros_ref[pl.ds(k, 1), :]
+        zero = jnp.where(iota((1, radial), 1) < counts_ref[k], zero, 0)
+        pick = low_bits(iota(square, 0) + 1 == zero)
+        pick_ref[s] = pick
+        vectors = wide_ref[pl.ds(s, rows, stride=quota), :].astype(jnp.bfloat16)
+        coef = nn(vectors, pick).astype(jnp.bfloat16)
+        full_ref[s] = tn(coef, coef) / float(rows) + noises[s] * eye
+    high_part = recv_ref[:, low_rows:, :].astype(jnp.float32)
+    for i in range(pairs):
+        coef = high_part[:, i * plan.vecs : (i + 1) * plan.vecs, :].reshape(rows, radial)
+        coef = coef.astype(jnp.bfloat16)
+        held_ref[i] = coef
+        gram = tn(coef, coef)
+        gram = jnp.where(first, gram[:narrow], gram[narrow:])
+        at = base + plan.half + 2 * i
+        noise = jnp.where(first, noise_ref[order_ref[at]], noise_ref[order_ref[at + 1]])
+        noises.append(noise)
+        pair_ref[i] = gram / float(rows) + noise * twins
+    lower = [(full_ref, m, False) for m in range(quota)]
+    upper = [(pair_ref, m, True) for m in range(pairs)]
+    lax.fori_loop(0, narrow // 8, functools.partial(sweep, lower + upper), 0)
+    lax.fori_loop(narrow // 8, radial // 8, functools.partial(sweep, lower), 0)
+    for s in range(quota):
+        shrink = eye - noises[s] * full_ref[s]
+        shrink_ref[s * radial : (s + 1) * radial, :] = shrink
+        pick = pick_ref[s]
+        moved = lax.dot_general(
+            shrink.astype(jnp.bfloat16),
+            pick,
+            (((0,), (1,)), ((), ())),
+            preferred_element_type=jnp.float32,
+        ).astype(jnp.bfloat16)
+        spread = nn(pick, moved).astype(jnp.bfloat16)
+        vectors = wide_ref[pl.ds(s, rows, stride=quota), :].astype(jnp.bfloat16)
+        wide_ref[pl.ds(s, rows, stride=quota), :] = nn(vectors, spread)
+    shape = (plan.devices, low_rows, radial)
+    back_ref[:, :low_rows, :] = wide_ref[...].reshape(shape).astype(jnp.bfloat16)
+    tiles = []
+    for i in range(pairs):
+        shrink = twins - noises[quota + i] * pair_ref[i]
+        start = quota * radial + i * narrow
+        shrink_ref[start : start + narrow, :] = shrink
+        blocks = jnp.concatenate(
+            [jnp.where(first, shrink, 0.0), jnp.where(first, 0.0, shrink)], axis=0
+        )
+        filtered = nt(held_ref[i], blocks.astype(jnp.bfloat16))
+        tiles.append(filtered.reshape(plan.devices, plan.vecs, radial))
+    back_ref[:, low_rows:, :] = jnp.concatenate(tiles, axis=1).astype(jnp.bfloat16)
+
+
+def synthesis_kernel(plan, table_ref, cb_ref, sb_ref, wave_ref, zero_ref, recv_ref, out_ref, wide_ref):
+    radial, total, quota, pairs = plan.radial, plan.total, plan.quota, plan.pairs
+    lane = iota((plan.vecs, radial), 1)
+    zero_here = iota((radial, radial), 0) + 1
+    for device in range(plan.devices):
+        tile = recv_ref[device, plan.low_rows : plan.rows, :].astype(jnp.float32)
+        for i in range(pairs):
+            at = device * pairs + i
+            packed = tile[i * plan.vecs : (i + 1) * plan.vecs]
+            both = jnp.concatenate(
+                [jnp.where(lane < plan.narrow, packed, 0.0), jnp.where(lane < plan.narrow, 0.0, packed)],
+                axis=0,
+            )
+            chosen = low_bits(zero_here == zero_ref[at : at + 1, :])
+            spread = nt(both.astype(jnp.bfloat16), chosen)
+            wide_ref[pl.ds(at, 2 * plan.vecs, stride=plan.all_pairs), :] = spread
+    span = 2 * plan.all_pairs
+    for i in range(plan.count_img):
+        low = recv_ref[:, 2 * quota * i : 2 * quota * (i + 1), :].astype(jnp.float32)
+        at = [(e * plan.count_img + i) * span for e in range(2)]
+        filtered = jnp.concatenate(
+            [low.reshape(total, radial)] + [wide_ref[a : a + span, :] for a in at], axis=0
+        )
+        turned = nt(filtered.astype(jnp.bfloat16), wave_ref[...])
+        spectrum = turned[:, :radial] * cb_ref[...] + turned[:, radial:] * sb_ref[...]
+        out_ref[i] = tn(spectrum.astype(jnp.bfloat16), table_ref[...]).astype(jnp.bfloat16)
+
+
+def wiener_kernel(plan, own_ref, other_ref, out_ref):
+    radial, quota, narrow = plan.radial, plan.quota, plan.narrow
+    batch_at = lax.axis_index("batch")
+    lane = iota((narrow, radial), 1)
+    for batch, ref in ((batch_at, own_ref), (1 - batch_at, other_ref)):
+        for s in range(quota):
+            out_ref[batch * quota + s] = ref[s * radial : (s + 1) * radial, :]
+            at = plan.half + batch * quota + s
+            start = quota * radial + (s // 2) * narrow
+            pair = ref[start : start + narrow, :]
+            if s % 2:
+                pair = pltpu.roll(pair, narrow, axis=1)
+            out_ref[at, 0:narrow, :] = jnp.where(lane < narrow, pair, 0.0)
+            out_ref[at, narrow:radial, :] = jnp.zeros((radial - narrow, radial), jnp.float32)
+
+
+VMEM = pl.BlockSpec(memory_space=pltpu.VMEM)
+SMEM = pl.BlockSpec(memory_space=pltpu.SMEM)
+
+
+def call(kernel, outs, ins, scratch=()):
+    return pl.pallas_call(
+        kernel,
+        out_shape=outs,
+        in_specs=ins,
+        out_specs=jax.tree.map(lambda _: VMEM, outs),
+        scratch_shapes=scratch,
+    )
+
+
+def fast_device(plan, images, radial_counts, order, zeros_table, noise_var):
+    both = ("batch", "freq")
+    radial, total, quota, pairs = plan.radial, plan.total, plan.quota, plan.pairs
+    shape = jax.ShapeDtypeStruct
+    block = shape((plan.devices, plan.rows, radial), jnp.bfloat16)
+    coef, table, cb, sb, wave, zero = call(
+        functools.partial(analysis_kernel, plan),
+        (
+            block,
+            shape((2 * total, plan.angles), jnp.bfloat16),
+            shape((2 * total, radial), jnp.float32),
+            shape((2 * total, radial), jnp.float32),
+            shape((2 * radial, radial), jnp.bfloat16),
+            shape((plan.all_pairs, radial), jnp.int32),
+        ),
+        [VMEM] * 4,
+        [pltpu.VMEM((2 * plan.vecs * plan.all_pairs, radial), jnp.float32)],
+    )(order.reshape(1, total), radial_counts.reshape(1, total), zeros_table, images)
+    recv = lax.all_to_all(coef, both, split_axis=0, concat_axis=0, tiled=True)
+    back, shrink = call(
+        functools.partial(filter_kernel, plan),
+        (block, shape((quota * radial + pairs * plan.narrow, radial), jnp.float32)),
+        [SMEM, SMEM, SMEM, VMEM, VMEM],
+        [
+            pltpu.VMEM((plan.devices * plan.low_rows, radial), jnp.float32),
+            pltpu.VMEM((quota, radial, radial), jnp.float32),
+            pltpu.VMEM((pairs, plan.narrow, radial), jnp.float32),
+            pltpu.VMEM((quota, radial, radial), jnp.bfloat16),
+            pltpu.VMEM((pairs, plan.devices * plan.vecs, radial), jnp.bfloat16),
+        ],
+    )(order, noise_var, radial_counts, zeros_table, recv)
+    returned = lax.all_to_all(back, both, split_axis=0, concat_axis=0, tiled=True)
+    other = lax.ppermute(shrink, "batch", [(0, 1), (1, 0)])
+    wiener_blocks = call(
+        functools.partial(wiener_kernel, plan),
+        shape((plan.owned, radial, radial), jnp.float32),
+        [VMEM] * 2,
+    )(shrink, other)
+    denoised = call(
+        functools.partial(synthesis_kernel, plan),
+        shape((plan.count_img, radial, plan.angles), jnp.bfloat16),
+        [VMEM] * 6,
+        [pltpu.VMEM((2 * plan.vecs * plan.all_pairs, radial), jnp.float32)],
+    )(table, cb, sb, wave, zero, returned)
+    return denoised, wiener_blocks
+
+
 def solution(mesh):
+    owners, batches = mesh.shape["freq"], mesh.shape["batch"]
+
+    def body(images, radial_counts, order, zeros_table, noise_var):
+        plan = Plan(images.shape, order.shape[0], owners, batches)
+        device = functools.partial(fast_device, plan) if plan.fits else per_device
+        return device(images, radial_counts, order, zeros_table, noise_var)
+
     return jax.shard_map(
-        per_device,
+        body,
         mesh=mesh,
         in_specs=(P(("batch", "freq"), None, None), P(), P(), P(), P()),
         out_specs=(P(("batch", "freq"), None, None), P("freq", None, None)),

time: 536 us -> 62.1 us (0.12)
  other arithmetic: 270 us -> 0 us
  matrix products: 153 us -> 0 us
  waiting for transfers between devices: 62.5 us -> 12.2 us
  Pallas kernels: 0 us -> 22.4 us
  blocking collectives: 0 us -> 20.5 us
  starting transfers between devices: 20.1 us -> 4.45 us
  between operations: 14.4 us -> 0.65 us
  local copies, waits for them, and re-layouts: 13.4 us -> 1.49 us
    another operation x20 -> x0, other arithmetic: 264 us -> none  [the longest x6 141 us: shrink_from(): lower = jnp.linalg.cholesky(covariance)]
    dot_general x22 -> x0, matrix products: 151 us -> none  [the longest x4 72.2 us: analyse(): jnp.einsum('ircj,jqr->jciq', spectrum, basis, preferred_element_type=jnp....]
    psum x1 -> x0, waiting for transfers between devices: 32.6 us -> none  [per_device(): lax.psum((gram_of(low_recv), gram_of(high_recv)), 'batch')]
    all_to_all x4 -> x1, waiting for transfers between devices: 29.9 us -> 0.01 us  [fast_device(): lax.all_to_all(back, both, split_axis=0, concat_axis=0, tiled=True)]
    pallas_call x0 -> x4, Pallas kernels: none -> 22.4 us  [the longest x1 11.3 us: fast_device(): call(functools.partial(filter_kernel, plan), (block, shape((quota * radia...]
    all_to_all x0 -> x1, blocking collectives: none -> 20.5 us  [fast_device(): recv = lax.all_to_all(coef, both, split_axis=0, concat_axis=0, tiled=True)]
    all_to_all x4 -> x1, starting transfers between devices: 20.1 us -> 2.73 us  [fast_device(): lax.all_to_all(back, both, split_axis=0, concat_axis=0, tiled=True)]
    ppermute x0 -> x1, waiting for transfers between devices: none -> 12.2 us  [fast_device(): other = lax.ppermute(shrink, 'batch', [(0, 1), (1, 0)])]
  transfers between devices with their start and end apart: 5 -> 2, of which waited for: 5 -> 1; matrix products, arithmetic and copies ran while one was open for 1% -> 0% of each run, Pallas kernels for 0% -> 3%
where the time goes in v3:
time: 62.1 us; the launch traced here: 61.7 us
  Pallas kernels  22.4 us (36%)
  blocking collectives  20.5 us (33%)
  waiting for transfers between devices  12.2 us (20%)
  starting transfers between devices  4.45 us (7%)
  local copies, waits for them, and re-layouts  1.49 us (2%)
  between operations  0.65 us (1%)
    all_to_all x1, blocking collectives, fast_device(): recv = lax.all_to_all(coef, both, split_axis=0, concat_axis=0, tiled=True)  20.5 us
    ppermute x1, waiting for transfers between devices, fast_device(): other = lax.ppermute(shrink, 'batch', [(0, 1), (1, 0)])  12.2 us
    pallas_call x1, Pallas kernels, fast_device(): call(functools.partial(filter_kernel, plan), (block, shape((quota * radia...  11.3 us
    pallas_call x1, Pallas kernels, fast_device(): call(functools.partial(analysis_kernel, plan), (block, shape((2 * total,...  4.65 us
    pallas_call x1, Pallas kernels, fast_device(): call(functools.partial(synthesis_kernel, plan), shape((plan.count_img, ra...  4.24 us
    all_to_all x1, starting transfers between devices, fast_device(): lax.all_to_all(back, both, split_axis=0, concat_axis=0, tiled=True)  2.73 us
    pallas_call x1, Pallas kernels, fast_device(): call(functools.partial(wiener_kernel, plan), shape((plan.owned, radial, r...  2.14 us
    ppermute x1, starting transfers between devices, fast_device(): other = lax.ppermute(shrink, 'batch', [(0, 1), (1, 0)])  1.72 us
  transfers between devices with their start and end apart: 2, of which 1 were waited for; matrix products, arithmetic and copies ran while one was open for 0% of the time, Pallas kernels for 3%

profile of v3, /device:TPU:0, one launch (start us, length us, event | category | flops | bytes accessed | tf_op | source)
XLA Modules:
  0.0 61.7 jit_solution(1412037363280548149)
XLA Ops:
  0.6 4.7 %shard_map.68 = (bf16[32,48,128]{2,1,0:T(8,128)(2,1)}, bf16[512,512]{1,0:T(8,128)(2,1)}, f32[512,128]{1,0:T(8,128)}, f32[512,128]{1,0:T(8,128)}, bf16[256,128]{1,0:T(8,128)(2,1)}, /*index=5*/s32[64,128]{1,0:T(8,128)}) custom-call(s32[1,256]{1,0:T(1,128)} %bitcast.2, s32[1,256]{1,0:T(1,128)} %bitcast.3, s32[256,128]{1,0:T(8,128)} %zeros_ref.3, ...), custom_call_target="tpu_custom_call" | custom-call | tf_op jit(solution)/shard_map/pallas_call | solution.py:509
  5.3 20.5 %all_to_all.10.recv_ref = bf16[32,48,128]{2,1,0:T(8,128)(2,1)} all-to-all(bf16[32,48,128]{2,1,0:T(8,128)(2,1)} %get-tuple-element.15), channel_id=1, replica_groups=mesh['batch'=2,'freq'=16] {'batch','freq'}, dimensions={0} | all-to-all | bytes 786432 | tf_op jit(solution)/shard_map/all_to_all | solution.py:522
  25.8 11.3 %shard_map.69 = (bf16[32,48,128]{2,1,0:T(8,128)(2,1)}, f32[640,128]{1,0:T(8,128)}) custom-call(s32[256]{0:T(256)} %order_ref.1, f32[256]{0:T(256)} %noise_ref.1, s32[256]{0:T(256)} %counts_ref.1, s32[256,128]{1,0:T(8,128)} %zeros_ref.3, bf16[32,48,128]{2,1,0:T(8,128)(2,1)} %all_to_all.10.recv_ref), custom_call_target="tpu_custom_call" | custom-call | tf_op jit(solution)/shard_map/pallas_call | solution.py:523
  37.1 0.0 copy-start.1
  37.2 2.7 %all-to-all-start.1 = ((bf16[32,48,128]{2,1,0:T(8,128)(2,1)}), bf16[32,48,128]{2,1,0:T(8,128)(2,1)S(1)}, u32[]{:S(2)}, u32[]{:S(2)}) async-start(bf16[32,48,128]{2,1,0:T(8,128)(2,1)} %get-tuple-element.16), calls=%async_computation.1 | async-start | bytes 786432 | tf_op jit(solution)/shard_map/all_to_all | solution.py:535
  39.9 0.0 copy-done.1
  39.9 1.7 %collective-permute-start = (f32[640,128]{1,0:T(8,128)S(1)}, f32[640,128]{1,0:T(8,128)S(1)}, u32[]{:S(2)}, u32[]{:S(2)}) collective-permute-start(f32[640,128]{1,0:T(8,128)S(1)} %copy-done.1), channel_id=1, source_target_pairs={{0,16},{16,0},{1,17},{17,1},{2,18},{18,2},{3,19},{19,3},{4,20},{20... | collective-permute-start | bytes 983048 | tf_op jit(solution)/shard_map/ppermute | solution.py:536
  41.6 12.2 %collective-permute-done.other_ref = f32[640,128]{1,0:T(8,128)S(1)} collective-permute-done((f32[640,128]{1,0:T(8,128)S(1)}, f32[640,128]{1,0:T(8,128)S(1)}, u32[]{:S(2)}, u32[]{:S(2)}) %collective-permute-start) | collective-permute-done | bytes 327712 | tf_op jit(solution)/shard_map/ppermute | solution.py:536
  53.9 0.0 copy-start.2
  53.9 0.7 %copy-done.2 = f32[640,128]{1,0:T(8,128)} copy-done((f32[640,128]{1,0:T(8,128)}, f32[640,128]{1,0:T(8,128)S(1)}, u32[]{:S(2)}) %copy-start.2) | copy-done | bytes 327704
  54.6 2.1 %shard_map.71 = f32[16,128,128]{2,1,0:T(8,128)} custom-call(f32[640,128]{1,0:T(8,128)} %get-tuple-element.17.own_ref, f32[640,128]{1,0:T(8,128)} %copy-done.2), custom_call_target="tpu_custom_call" | custom-call | tf_op jit(solution)/shard_map/pallas_call | solution.py:537
  56.7 0.0 all-to-all-done.1.recv_ref
  56.7 0.0 copy-start
  56.7 0.8 %copy-done = bf16[32,48,128]{2,1,0:T(8,128)(2,1)} copy-done((bf16[32,48,128]{2,1,0:T(8,128)(2,1)}, bf16[32,48,128]{2,1,0:T(8,128)(2,1)S(1)}, u32[]{:S(2)}) %copy-start) | copy-done | bytes 393240
  57.5 4.2 %shard_map.70 = bf16[4,128,512]{2,1,0:T(8,128)(2,1)} custom-call(bf16[512,512]{1,0:T(8,128)(2,1)} %get-tuple-element.10.table_ref, f32[512,128]{1,0:T(8,128)} %get-tuple-element.11.cb_ref, f32[512,128]{1,0:T(8,128)} %get-tuple-element.12.sb_ref, bf16[256,128]{1,0:T(8,128)(2,1)} %get-tuple-element.13.wave_ref, s32[64,128]{1,0:T(8,128)} %get-tuple-element.14.zero_ref, ...), custom_call_target="tpu_custom_call" | custom-call | tf_op jit(solution)/shard_map/pallas_call | solution.py:542
Async XLA Ops:
  37.1 2.7 %copy-start.1 = (f32[640,128]{1,0:T(8,128)S(1)}, f32[640,128]{1,0:T(8,128)}, u32[]{:S(2)}) copy-start(f32[640,128]{1,0:T(8,128)} %get-tuple-element.17.own_ref) | copy-start | bytes 983044
  37.2 19.6 %all-to-all-start.1 = ((bf16[32,48,128]{2,1,0:T(8,128)(2,1)}), bf16[32,48,128]{2,1,0:T(8,128)(2,1)S(1)}, u32[]{:S(2)}, u32[]{:S(2)}) async-start(bf16[32,48,128]{2,1,0:T(8,128)(2,1)} %get-tuple-element.16), calls=%async_computation.1 | async-start | bytes 786432 | tf_op jit(solution)/shard_map/all_to_all | solution.py:535
  39.9 14.0 %collective-permute-start = (f32[640,128]{1,0:T(8,128)S(1)}, f32[640,128]{1,0:T(8,128)S(1)}, u32[]{:S(2)}, u32[]{:S(2)}) collective-permute-start(f32[640,128]{1,0:T(8,128)S(1)} %copy-done.1), channel_id=1, source_target_pairs={{0,16},{16,0},{1,17},{17,1},{2,18},{18,2},{3,19},{19,3},{4,20},{20... | collective-permute-start | bytes 983048 | tf_op jit(solution)/shard_map/ppermute | solution.py:536
  53.9 0.7 %copy-start.2 = (f32[640,128]{1,0:T(8,128)}, f32[640,128]{1,0:T(8,128)S(1)}, u32[]{:S(2)}) copy-start(f32[640,128]{1,0:T(8,128)S(1)} %collective-permute-done.other_ref) | copy-start | bytes 983044
  56.7 0.8 %copy-start = (bf16[32,48,128]{2,1,0:T(8,128)(2,1)}, bf16[32,48,128]{2,1,0:T(8,128)(2,1)S(1)}, u32[]{:S(2)}) copy-start(bf16[32,48,128]{2,1,0:T(8,128)(2,1)S(1)} %all-to-all-done.1.recv_ref) | copy-start | bytes 1179652

commit v4 on v3

--- a/solution.py
+++ b/solution.py
@@ -417,7 +417,7 @@
     lax.fori_loop(narrow // 8, radial // 8, functools.partial(sweep, lower), 0)
     for s in range(quota):
         shrink = eye - noises[s] * full_ref[s]
-        shrink_ref[s * radial : (s + 1) * radial, :] = shrink
+        shrink_ref[s * radial : (s + 1) * radial, :] = shrink.astype(jnp.bfloat16)
         pick = pick_ref[s]
         moved = lax.dot_general(
             shrink.astype(jnp.bfloat16),
@@ -434,7 +434,7 @@
     for i in range(pairs):
         shrink = twins - noises[quota + i] * pair_ref[i]
         start = quota * radial + i * narrow
-        shrink_ref[start : start + narrow, :] = shrink
+        shrink_ref[start : start + narrow, :] = shrink.astype(jnp.bfloat16)
         blocks = jnp.concatenate(
             [jnp.where(first, shrink, 0.0), jnp.where(first, 0.0, shrink)], axis=0
         )
@@ -477,10 +477,10 @@
     lane = iota((narrow, radial), 1)
     for batch, ref in ((batch_at, own_ref), (1 - batch_at, other_ref)):
         for s in range(quota):
-            out_ref[batch * quota + s] = ref[s * radial : (s + 1) * radial, :]
+            out_ref[batch * quota + s] = ref[s * radial : (s + 1) * radial, :].astype(jnp.float32)
             at = plan.half + batch * quota + s
             start = quota * radial + (s // 2) * narrow
-            pair = ref[start : start + narrow, :]
+            pair = ref[start : start + narrow, :].astype(jnp.float32)
             if s % 2:
                 pair = pltpu.roll(pair, narrow, axis=1)
             out_ref[at, 0:narrow, :] = jnp.where(lane < narrow, pair, 0.0)
@@ -498,6 +498,7 @@
         in_specs=ins,
         out_specs=jax.tree.map(lambda _: VMEM, outs),
         scratch_shapes=scratch,
+        compiler_params=pltpu.CompilerParams(vmem_limit_bytes=16 << 20),
     )
 
 
@@ -522,7 +523,7 @@
     recv = lax.all_to_all(coef, both, split_axis=0, concat_axis=0, tiled=True)
     back, shrink = call(
         functools.partial(filter_kernel, plan),
-        (block, shape((quota * radial + pairs * plan.narrow, radial), jnp.float32)),
+        (block, shape((quota * radial + pairs * plan.narrow, radial), jnp.bfloat16)),
         [SMEM, SMEM, SMEM, VMEM, VMEM],
         [
             pltpu.VMEM((plan.devices * plan.low_rows, radial), jnp.float32),

time: 62.1 us -> 56 us (0.902)
  Pallas kernels: 22.4 us -> 17.5 us
  waiting for transfers between devices: 12.2 us -> 10.3 us
  local copies, waits for them, and re-layouts: 1.49 us -> 2.63 us
    ppermute x1, waiting for transfers between devices: 12.2 us -> 7.55 us  [fast_device(): other = lax.ppermute(shrink, 'batch', [(0, 1), (1, 0)])]
    all_to_all x1, waiting for transfers between devices: 0.01 us -> 2.77 us  [fast_device(): lax.all_to_all(back, both, split_axis=0, concat_axis=0, tiled=True)]
    pallas_call x1, Pallas kernels: 4.65 us -> 2.74 us  [fast_device(): call(functools.partial(analysis_kernel, plan), (block, shape((2 * total,...]
    pallas_call x1, Pallas kernels: 4.24 us -> 2.88 us  [fast_device(): call(functools.partial(synthesis_kernel, plan), shape((plan.count_img, ra...]
    unnamed x6 -> x10, local copies, waits for them, and re-layouts: 1.49 us -> 2.63 us
    pallas_call x1, Pallas kernels: 2.14 us -> 1.06 us  [fast_device(): call(functools.partial(wiener_kernel, plan), shape((plan.owned, radial, r...]
  transfers between devices with their start and end apart: 2 -> 2, of which waited for: 1 -> 2; matrix products, arithmetic and copies ran while one was open for 0% -> 0% of each run, Pallas kernels for 3% -> 2%
where the time goes in v4:
time: 56 us; the launch traced here: 55.7 us
  blocking collectives  20.2 us (36%)
  Pallas kernels  17.5 us (31%)
  waiting for transfers between devices  10.3 us (18%)
  starting transfers between devices  4.31 us (8%)
  local copies, waits for them, and re-layouts  2.63 us (5%)
  between operations  0.67 us (1%)
    all_to_all x1, blocking collectives, fast_device(): recv = lax.all_to_all(coef, both, split_axis=0, concat_axis=0, tiled=True)  20.2 us
    pallas_call x1, Pallas kernels, fast_device(): call(functools.partial(filter_kernel, plan), (block, shape((quota * radia...  10.8 us
    ppermute x1, waiting for transfers between devices, fast_device(): other = lax.ppermute(shrink, 'batch', [(0, 1), (1, 0)])  7.55 us
    pallas_call x1, Pallas kernels, fast_device(): call(functools.partial(synthesis_kernel, plan), shape((plan.count_img, ra...  2.88 us
    all_to_all x1, waiting for transfers between devices, fast_device(): lax.all_to_all(back, both, split_axis=0, concat_axis=0, tiled=True)  2.77 us
    pallas_call x1, Pallas kernels, fast_device(): call(functools.partial(analysis_kernel, plan), (block, shape((2 * total,...  2.74 us
    unnamed x10, local copies, waits for them, and re-layouts  2.63 us
    all_to_all x1, starting transfers between devices, fast_device(): lax.all_to_all(back, both, split_axis=0, concat_axis=0, tiled=True)  2.6 us
  transfers between devices with their start and end apart: 2, of which 2 were waited for; matrix products, arithmetic and copies ran while one was open for 0% of the time, Pallas kernels for 2%

profile of v4, /device:TPU:0, one launch (start us, length us, event | category | flops | bytes accessed | tf_op | source)
XLA Modules:
  0.0 55.7 jit_solution(8860449640852873654)
XLA Ops:
  0.6 0.0 copy-start.3
  0.6 0.0 copy-start.2
  0.7 0.7 %copy-done.3 = s32[256]{0:T(256)S(1)} copy-done((s32[256]{0:T(256)S(1)}, s32[256]{0:T(256)}, u32[]{:S(2)}) %copy-start.3) | copy-done | bytes 1048
  1.3 0.0 copy-done.2
  1.3 0.0 copy-start
  1.3 1.0 %copy-done = bf16[4,128,512]{2,1,0:T(8,128)(2,1)S(1)} copy-done((bf16[4,128,512]{2,1,0:T(8,128)(2,1)S(1)}, bf16[4,128,512]{2,1,0:T(8,128)(2,1)}, u32[]{:S(2)}) %copy-start) | copy-done | bytes 524312
  2.4 0.0 copy-start.1
  2.4 0.9 %copy-done.1 = s32[256,128]{1,0:T(8,128)S(1)} copy-done((s32[256,128]{1,0:T(8,128)S(1)}, s32[256,128]{1,0:T(8,128)}, u32[]{:S(2)}) %copy-start.1) | copy-done | bytes 131096
  3.3 2.7 %shard_map.68 = (bf16[32,48,128]{2,1,0:T(8,128)(2,1)S(1)}, bf16[512,512]{1,0:T(8,128)(2,1)S(1)}, f32[512,128]{1,0:T(8,128)S(1)}, f32[512,128]{1,0:T(8,128)S(1)},...) custom-call(s32[1,256]{1,0:T(1,128)S(1)} %bitcast.2, s32[1,256]{1,0:T(1,128)S(1)} %bitcast.3, ...), custom_call_target="tpu_custom_call" | custom-call | tf_op jit(solution)/shard_map/pallas_call | solution.py:510
  6.0 0.0 copy-start.4
  6.0 20.2 %all_to_all.10.recv_ref = bf16[32,48,128]{2,1,0:T(8,128)(2,1)S(1)} all-to-all(bf16[32,48,128]{2,1,0:T(8,128)(2,1)S(1)} %get-tuple-element.15), channel_id=1, replica_groups=mesh['batch'=2,'freq'=16] {'batch','freq'}, dimensions={0} | all-to-all | bytes 786432 | tf_op jit(solution)/shard_map/all_to_all | solution.py:523
  26.2 0.0 copy-done.4
  26.3 10.8 %shard_map.69 = (bf16[32,48,128]{2,1,0:T(8,128)(2,1)}, bf16[640,128]{1,0:T(8,128)(2,1)S(1)}) custom-call(s32[256]{0:T(256)S(1)} %copy-done.2, f32[256]{0:T(256)S(1)} %copy-done.4, s32[256]{0:T(256)S(1)} %copy-done.3, s32[256,128]{1,0:T(8,128)S(1)} %copy-done.1, bf16[32,48,128]{2,1,0:T(8,128)(2,1)S(1)} %all_to_all.10.recv_ref), custom_call_target="tpu_custom_call" | custom-call | tf_op jit(solution)/shard_map/pallas_call | solution.py:524
  37.1 2.6 %all-to-all-start.1 = ((bf16[32,48,128]{2,1,0:T(8,128)(2,1)}), bf16[32,48,128]{2,1,0:T(8,128)(2,1)S(1)}, u32[]{:S(2)}, u32[]{:S(2)}) async-start(bf16[32,48,128]{2,1,0:T(8,128)(2,1)} %get-tuple-element.16), calls=%async_computation.1 | async-start | bytes 786432 | tf_op jit(solution)/shard_map/all_to_all | solution.py:536
  39.7 1.7 %collective-permute-start = (bf16[640,128]{1,0:T(8,128)(2,1)S(1)}, bf16[640,128]{1,0:T(8,128)(2,1)S(1)}, u32[]{:S(2)}, u32[]{:S(2)}) collective-permute-start(bf16[640,128]{1,0:T(8,128)(2,1)S(1)} %get-tuple-element.17.own_ref), channel_id=1, source_target_pairs={{0,16},{16,0},{1,17},{17,1},{2,18},{18,2},{3,19},{19,3},{4,20},{20... | collective-permute-start | bytes 491528 | tf_op jit(solution)/shard_map/ppermute | solution.py:537
  41.4 7.6 %collective-permute-done.other_ref = bf16[640,128]{1,0:T(8,128)(2,1)S(1)} collective-permute-done((bf16[640,128]{1,0:T(8,128)(2,1)S(1)}, bf16[640,128]{1,0:T(8,128)(2,1)S(1)}, u32[]{:S(2)}, u32[]{:S(2)}) %collective-permute-start) | collective-permute-done | bytes 163872 | tf_op jit(solution)/shard_map/ppermute | solution.py:537
  49.0 1.1 %shard_map.71 = f32[16,128,128]{2,1,0:T(8,128)} custom-call(bf16[640,128]{1,0:T(8,128)(2,1)S(1)} %get-tuple-element.17.own_ref, bf16[640,128]{1,0:T(8,128)(2,1)S(1)} %collective-permute-done.other_ref), custom_call_target="tpu_custom_call" | custom-call | tf_op jit(solution)/shard_map/pallas_call | solution.py:538
  50.0 2.8 %all-to-all-done.1.recv_ref = bf16[32,48,128]{2,1,0:T(8,128)(2,1)S(1)} async-done(((bf16[32,48,128]{2,1,0:T(8,128)(2,1)}), bf16[32,48,128]{2,1,0:T(8,128)(2,1)S(1)}, u32[]{:S(2)}, u32[]{:S(2)}) %all-to-all-start.1) | async-done | bytes 393248 | tf_op jit(solution)/shard_map/all_to_all | solution.py:536
  52.8 2.9 %shard_map.70 = bf16[4,128,512]{2,1,0:T(8,128)(2,1)} custom-call(bf16[512,512]{1,0:T(8,128)(2,1)S(1)} %get-tuple-element.10.table_ref, f32[512,128]{1,0:T(8,128)S(1)} %get-tuple-element.11.cb_ref, f32[512,128]{1,0:T(8,128)S(1)} %get-tuple-element.12.sb_ref, bf16[256,128]{1,0:T(8,128)(2,1)S(1)} %get-tuple-element.13.wave_ref, ...), custom_call_target="tpu_custom_call" | custom-call | tf_op jit(solution)/shard_map/pallas_call | solution.py:543
Async XLA Ops:
  0.6 0.7 %copy-start.3 = (s32[256]{0:T(256)S(1)}, s32[256]{0:T(256)}, u32[]{:S(2)}) copy-start(s32[256]{0:T(256)} %counts_ref.1) | copy-start | bytes 3076
  0.6 0.7 %copy-start.2 = (s32[256]{0:T(256)S(1)}, s32[256]{0:T(256)}, u32[]{:S(2)}) copy-start(s32[256]{0:T(256)} %order_ref.1) | copy-start | bytes 3076
  1.3 1.0 %copy-start = (bf16[4,128,512]{2,1,0:T(8,128)(2,1)S(1)}, bf16[4,128,512]{2,1,0:T(8,128)(2,1)}, u32[]{:S(2)}) copy-start(bf16[4,128,512]{2,1,0:T(8,128)(2,1)} %images_ref.1) | copy-start | bytes 1572868
  2.4 0.9 %copy-start.1 = (s32[256,128]{1,0:T(8,128)S(1)}, s32[256,128]{1,0:T(8,128)}, u32[]{:S(2)}) copy-start(s32[256,128]{1,0:T(8,128)} %zeros_ref.3) | copy-start | bytes 393220
  6.0 20.2 %copy-start.4 = (f32[256]{0:T(256)S(1)}, f32[256]{0:T(256)}, u32[]{:S(2)}) copy-start(f32[256]{0:T(256)} %noise_ref.1) | copy-start | bytes 3076
  37.1 15.7 %all-to-all-start.1 = ((bf16[32,48,128]{2,1,0:T(8,128)(2,1)}), bf16[32,48,128]{2,1,0:T(8,128)(2,1)S(1)}, u32[]{:S(2)}, u32[]{:S(2)}) async-start(bf16[32,48,128]{2,1,0:T(8,128)(2,1)} %get-tuple-element.16), calls=%async_computation.1 | async-start | bytes 786432 | tf_op jit(solution)/shard_map/all_to_all | solution.py:536
  39.7 9.3 %collective-permute-start = (bf16[640,128]{1,0:T(8,128)(2,1)S(1)}, bf16[640,128]{1,0:T(8,128)(2,1)S(1)}, u32[]{:S(2)}, u32[]{:S(2)}) collective-permute-start(bf16[640,128]{1,0:T(8,128)(2,1)S(1)} %get-tuple-element.17.own_ref), channel_id=1, source_target_pairs={{0,16},{16,0},{1,17},{17,1},{2,18},{18,2},{3,19},{19,3},{4,20},{20... | collective-permute-start | bytes 491528 | tf_op jit(solution)/shard_map/ppermute | solution.py:537

commit v5 on v4

--- a/solution.py
+++ b/solution.py
@@ -209,11 +209,32 @@
 
 
 def analysis_kernel(
-    plan, order_ref, counts_ref, zeros_ref, images_ref,
-    coef_ref, table_ref, cb_ref, sb_ref, wave_ref, zero_ref, wide_ref,
+    plan, order_hbm, counts_hbm, noise_hbm, zeros_hbm, images_hbm,
+    coef_ref, table_ref, cb_ref, sb_ref, wave_ref, zero_ref, info_ref,
+    wide_ref, order_ref, counts_ref, noise_ref, zeros_ref, images_ref, sems,
 ):
     radial, angles, total = plan.radial, plan.angles, plan.total
     quota, pairs, narrow = plan.quota, plan.pairs, plan.narrow
+    copies = [
+        pltpu.make_async_copy(source, target, sems.at[at])
+        for at, (source, target) in enumerate(
+            (
+                (order_hbm, order_ref),
+                (counts_hbm, counts_ref),
+                (noise_hbm, noise_ref),
+                (zeros_hbm, zeros_ref),
+                (images_hbm, images_ref),
+            )
+        )
+    ]
+    for copy in copies:
+        copy.start()
+    turns = (iota((radial, radial), 1) + 1) * (2 * iota((radial, radial), 0) + 1)
+    factor = math.sqrt(2.0 / radial)
+    wave_ref[0:radial, :] = (factor * cosine_of(turns, 4 * radial)).astype(jnp.bfloat16)
+    wave_ref[radial : 2 * radial, :] = (-factor * cosine_of(turns - radial, 4 * radial)).astype(
+        jnp.bfloat16
+    )
     row = iota((2 * total, total), 0)
     high = row - total
     low_slot = plan.slot_of(row // (2 * quota), row & (quota - 1))
@@ -224,6 +245,7 @@
     slot = jnp.where(row < total, low_slot, high_slot)
     pick = low_bits(slot == iota((2 * total, total), 1))
     spread = lambda ref: jnp.broadcast_to(ref[...].astype(jnp.float32), (128, total)).astype(jnp.bfloat16)
+    copies[0].wait()
     held = spread(order_ref)
     freq = nt(pick, held).astype(jnp.int32)
     row = iota((2 * total, 128), 0)
@@ -241,12 +263,8 @@
     turns = (2 * freq - 1) * (2 * lane + 1) - 4 * radial * freq - 2 * radial
     cb_ref[...] = cosine_of(turns, steps)
     sb_ref[...] = cosine_of(turns - steps // 4, steps)
-    turns = (iota((radial, radial), 1) + 1) * (2 * iota((radial, radial), 0) + 1)
-    factor = math.sqrt(2.0 / radial)
-    wave_ref[0:radial, :] = (factor * cosine_of(turns, 4 * radial)).astype(jnp.bfloat16)
-    wave_ref[radial : 2 * radial, :] = (-factor * cosine_of(turns - radial, 4 * radial)).astype(
-        jnp.bfloat16
-    )
+    for copy in copies[1:4]:
+        copy.wait()
     by_freq = low_bits(iota((total, total), 0) == iota((total, total), 1))
     counts = nt(by_freq, spread(counts_ref)).astype(jnp.int32)
     zeros = jnp.where(iota((total, radial), 1) < counts, zeros_ref[...], 0)
@@ -262,6 +280,15 @@
     zero_ref[...] = jnp.where(lane < narrow, sides[0], pltpu.roll(sides[1], narrow, axis=1)).astype(
         jnp.int32
     )
+    place = iota((8, total), 0)
+    device = lax.axis_index("batch") * plan.owners + lax.axis_index("freq")
+    slot = plan.slot_of(device, (place // quota) * plan.half + (place & (quota - 1)))
+    mine = nt(low_bits(slot == iota((8, total), 1)), held).astype(jnp.int32)
+    mine = jnp.concatenate([mine] * (total // 128), axis=1) == iota((8, total), 1)
+    info_ref[0:8, :] = nn(low_bits(mine), zeros)
+    noise = jnp.sum(jnp.where(mine, noise_ref[...], 0.0), axis=1, keepdims=True)
+    info_ref[8:16, :] = jnp.broadcast_to(noise, (8, 128))
+    copies[4].wait()
     images = images_ref[...].reshape(plan.count_img * radial, angles)
     for two in range(plan.count_img // 2):
         spectrum = nt(table_ref[...], images[2 * two * radial : 2 * (two + 1) * radial])
@@ -331,27 +358,37 @@
         for panel, halved in zip(panels, halves)
     ]
     for i in range(8):
+        unit = (sub == i).astype(jnp.float32)
         for at, cols in enumerate(blocks):
             inverse = 1.0 / jnp.broadcast_to(cols[i][i : i + 1], shape)
-            fresh = []
-            for j in range(8):
-                if j == i:
-                    fresh.append(jnp.where(sub == i, inverse, -cols[i] * inverse))
-                else:
-                    line = jnp.broadcast_to(cols[j][i : i + 1], shape) * inverse
-                    fresh.append(jnp.where(sub == i, line, cols[j] - cols[i] * line))
-            blocks[at] = fresh
+            weight = (cols[i] - unit) * inverse
+            blocks[at] = [
+                unit - weight
+                if j == i
+                else cols[j] - weight * jnp.broadcast_to(cols[j][i : i + 1], shape)
+                for j in range(8)
+            ]
     solved = []
     for panel, halved, cols in zip(panels, halves, blocks):
         offset = lane - first_lane(halved, lane, step)
-        outside = (offset < 0) | (offset >= 8)
-        total = jnp.zeros(shape, jnp.float32)
-        for j in range(8):
-            line = jnp.broadcast_to(panel[j : j + 1], shape)
-            line = jnp.where(outside, line, jnp.where(offset == j, 1.0, 0.0))
-            total = total + cols[j] * line
+        unit = (sub == offset).astype(jnp.float32)
+        lines = jnp.where((offset < 0) | (offset >= 8), panel, unit)
+        total = cols[0] * jnp.broadcast_to(lines[0:1], shape)
+        for j in range(1, 8):
+            total = total + cols[j] * jnp.broadcast_to(lines[j : j + 1], shape)
         solved.append(total)
     return solved
+
+
+def scales_of(matrix, halved):
+    row, lane = iota(matrix.shape, 0), iota(matrix.shape, 1)
+    diagonal = jnp.where(row == (lane & 63 if halved else lane), matrix, 0.0)
+    across = lax.rsqrt(jnp.sum(diagonal, axis=0, keepdims=True))
+    if not halved:
+        return across * lax.rsqrt(jnp.sum(diagonal, axis=1, keepdims=True))
+    left = lax.rsqrt(jnp.sum(jnp.where(lane < 64, diagonal, 0.0), axis=1, keepdims=True))
+    right = lax.rsqrt(jnp.sum(jnp.where(lane < 64, 0.0, diagonal), axis=1, keepdims=True))
+    return across * jnp.where(lane < 64, left, right)
 
 
 def sweep(matrices, step, carry):
@@ -359,29 +396,26 @@
     halves = [halved for _, _, halved in matrices]
     panels = [ref[m, pl.ds(start, 8), :] for ref, m, _ in matrices]
     solved = pivot_panels(panels, halves, step)
+    sub, lane = iota((8, 128), 0), iota((8, 128), 1)
     for (ref, m, halved), panel, fresh in zip(matrices, panels, solved):
         height = ref.shape[1]
-        lane = iota((8, 128), 1)
         done = (lane & 63 if halved else lane) < step * 8
-        update = outer(jnp.where(done, -panel, panel), fresh)
-        lane = iota((height, 128), 1)
+        unit = (sub == lane - first_lane(halved, lane, step)).astype(jnp.float32)
+        update = outer(jnp.where(done, -panel, panel), fresh + unit)
         if halved:
-            update = jnp.where(lane < 64, update[:height], update[height:])
-        offset = lane - first_lane(halved, lane, step)
-        rest = jnp.where((offset >= 0) & (offset < 8), 0.0, ref[m])
-        ref[m] = rest - update
+            update = jnp.where(iota((height, 128), 1) < 64, update[:height], update[height:])
+        ref[m] = ref[m] - update
         ref[m, pl.ds(start, 8), :] = fresh
     return carry
 
 
 def filter_kernel(
-    plan, order_ref, noise_ref, counts_ref, zeros_ref, recv_ref,
-    back_ref, shrink_ref, wide_ref, full_ref, pair_ref, pick_ref, held_ref,
+    plan, info_ref, recv_ref,
+    back_ref, shrink_ref, wide_ref, full_ref, pair_ref, pick_ref, held_ref, full_scale_ref, pair_scale_ref,
 ):
     radial, quota, pairs, narrow = plan.radial, plan.quota, plan.pairs, plan.narrow
     low_rows = plan.low_rows
     rows = plan.devices * plan.vecs
-    base = lax.axis_index("freq") * plan.owned + lax.axis_index("batch") * quota
     low_part = recv_ref[:, :low_rows, :].astype(jnp.float32)
     wide_ref[...] = low_part.reshape(plan.devices * low_rows, radial)
     square = (radial, radial)
@@ -391,15 +425,16 @@
     first = iota(strip, 1) < narrow
     noises = []
     for s in range(quota):
-        k = order_ref[base + s]
-        noises.append(noise_ref[k])
-        zero = zeros_ref[pl.ds(k, 1), :]
-        zero = jnp.where(iota((1, radial), 1) < counts_ref[k], zero, 0)
+        noises.append(info_ref[8 + s : 9 + s, :])
+        zero = info_ref[s : s + 1, :].astype(jnp.int32)
         pick = low_bits(iota(square, 0) + 1 == zero)
         pick_ref[s] = pick
         vectors = wide_ref[pl.ds(s, rows, stride=quota), :].astype(jnp.bfloat16)
         coef = nn(vectors, pick).astype(jnp.bfloat16)
-        full_ref[s] = tn(coef, coef) / float(rows) + noises[s] * eye
+        covariance = tn(coef, coef) / float(rows) + noises[s] * eye
+        scale = scales_of(covariance, False)
+        full_scale_ref[s] = scale
+        full_ref[s] = covariance * scale
     high_part = recv_ref[:, low_rows:, :].astype(jnp.float32)
     for i in range(pairs):
         coef = high_part[:, i * plan.vecs : (i + 1) * plan.vecs, :].reshape(rows, radial)
@@ -407,16 +442,19 @@
         held_ref[i] = coef
         gram = tn(coef, coef)
         gram = jnp.where(first, gram[:narrow], gram[narrow:])
-        at = base + plan.half + 2 * i
-        noise = jnp.where(first, noise_ref[order_ref[at]], noise_ref[order_ref[at + 1]])
+        at = 8 + quota + 2 * i
+        noise = jnp.where(first, info_ref[at : at + 1, :], info_ref[at + 1 : at + 2, :])
         noises.append(noise)
-        pair_ref[i] = gram / float(rows) + noise * twins
+        covariance = gram / float(rows) + noise * twins
+        scale = scales_of(covariance, True)
+        pair_scale_ref[i] = scale
+        pair_ref[i] = covariance * scale
     lower = [(full_ref, m, False) for m in range(quota)]
     upper = [(pair_ref, m, True) for m in range(pairs)]
     lax.fori_loop(0, narrow // 8, functools.partial(sweep, lower + upper), 0)
     lax.fori_loop(narrow // 8, radial // 8, functools.partial(sweep, lower), 0)
     for s in range(quota):
-        shrink = eye - noises[s] * full_ref[s]
+        shrink = eye - noises[s] * (full_ref[s] * full_scale_ref[s])
         shrink_ref[s * radial : (s + 1) * radial, :] = shrink.astype(jnp.bfloat16)
         pick = pick_ref[s]
         moved = lax.dot_general(
@@ -432,7 +470,7 @@
     back_ref[:, :low_rows, :] = wide_ref[...].reshape(shape).astype(jnp.bfloat16)
     tiles = []
     for i in range(pairs):
-        shrink = twins - noises[quota + i] * pair_ref[i]
+        shrink = twins - noises[quota + i] * (pair_ref[i] * pair_scale_ref[i])
         start = quota * radial + i * narrow
         shrink_ref[start : start + narrow, :] = shrink.astype(jnp.bfloat16)
         blocks = jnp.concatenate(
@@ -443,7 +481,7 @@
     back_ref[:, low_rows:, :] = jnp.concatenate(tiles, axis=1).astype(jnp.bfloat16)
 
 
-def synthesis_kernel(plan, table_ref, cb_ref, sb_ref, wave_ref, zero_ref, recv_ref, out_ref, wide_ref):
+def synthesis_kernel(plan, table_ref, cb_ref, sb_ref, wave_ref, zero_ref, recv_ref, out_ref, wide_ref, held_ref):
     radial, total, quota, pairs = plan.radial, plan.total, plan.quota, plan.pairs
     lane = iota((plan.vecs, radial), 1)
     zero_here = iota((radial, radial), 0) + 1
@@ -468,7 +506,9 @@
         )
         turned = nt(filtered.astype(jnp.bfloat16), wave_ref[...])
         spectrum = turned[:, :radial] * cb_ref[...] + turned[:, radial:] * sb_ref[...]
-        out_ref[i] = tn(spectrum.astype(jnp.bfloat16), table_ref[...]).astype(jnp.bfloat16)
+        held_ref[:, i * radial : (i + 1) * radial] = spectrum.astype(jnp.bfloat16)
+    image = tn(held_ref[...], table_ref[...]).astype(jnp.bfloat16)
+    out_ref[...] = image.reshape(out_ref.shape)
 
 
 def wiener_kernel(plan, own_ref, other_ref, out_ref):
@@ -488,7 +528,7 @@
 
 
 VMEM = pl.BlockSpec(memory_space=pltpu.VMEM)
-SMEM = pl.BlockSpec(memory_space=pltpu.SMEM)
+HBM = pl.BlockSpec(memory_space=pltpu.HBM)
 
 
 def call(kernel, outs, ins, scratch=()):
@@ -507,7 +547,7 @@
     radial, total, quota, pairs = plan.radial, plan.total, plan.quota, plan.pairs
     shape = jax.ShapeDtypeStruct
     block = shape((plan.devices, plan.rows, radial), jnp.bfloat16)
-    coef, table, cb, sb, wave, zero = call(
+    coef, table, cb, sb, wave, zero, info = call(
         functools.partial(analysis_kernel, plan),
         (
             block,
@@ -516,23 +556,45 @@
             shape((2 * total, radial), jnp.float32),
             shape((2 * radial, radial), jnp.bfloat16),
             shape((plan.all_pairs, radial), jnp.int32),
+            shape((16, radial), jnp.float32),
         ),
-        [VMEM] * 4,
-        [pltpu.VMEM((2 * plan.vecs * plan.all_pairs, radial), jnp.float32)],
-    )(order.reshape(1, total), radial_counts.reshape(1, total), zeros_table, images)
+        [HBM] * 5,
+        [
+            pltpu.VMEM((2 * plan.vecs * plan.all_pairs, radial), jnp.float32),
+            pltpu.VMEM((1, total), jnp.int32),
+            pltpu.VMEM((1, total), jnp.int32),
+            pltpu.VMEM((1, total), jnp.float32),
+            pltpu.VMEM(zeros_table.shape, jnp.int32),
+            pltpu.VMEM(images.shape, jnp.bfloat16),
+            pltpu.SemaphoreType.DMA((5,)),
+        ],
+    )(
+        *(
+            pltpu.with_memory_space_constraint(array, pltpu.HBM)
+            for array in (
+                order.reshape(1, total),
+                radial_counts.reshape(1, total),
+                noise_var.reshape(1, total),
+                zeros_table,
+                images,
+            )
+        )
+    )
     recv = lax.all_to_all(coef, both, split_axis=0, concat_axis=0, tiled=True)
     back, shrink = call(
         functools.partial(filter_kernel, plan),
         (block, shape((quota * radial + pairs * plan.narrow, radial), jnp.bfloat16)),
-        [SMEM, SMEM, SMEM, VMEM, VMEM],
+        [VMEM, VMEM],
         [
             pltpu.VMEM((plan.devices * plan.low_rows, radial), jnp.float32),
             pltpu.VMEM((quota, radial, radial), jnp.float32),
             pltpu.VMEM((pairs, plan.narrow, radial), jnp.float32),
             pltpu.VMEM((quota, radial, radial), jnp.bfloat16),
             pltpu.VMEM((pairs, plan.devices * plan.vecs, radial), jnp.bfloat16),
+            pltpu.VMEM((quota, radial, radial), jnp.float32),
+            pltpu.VMEM((pairs, plan.narrow, radial), jnp.float32),
         ],
-    )(order, noise_var, radial_counts, zeros_table, recv)
+    )(info, recv)
     returned = lax.all_to_all(back, both, split_axis=0, concat_axis=0, tiled=True)
     other = lax.ppermute(shrink, "batch", [(0, 1), (1, 0)])
     wiener_blocks = call(
@@ -544,7 +606,10 @@
         functools.partial(synthesis_kernel, plan),
         shape((plan.count_img, radial, plan.angles), jnp.bfloat16),
         [VMEM] * 6,
-        [pltpu.VMEM((2 * plan.vecs * plan.all_pairs, radial), jnp.float32)],
+        [
+            pltpu.VMEM((2 * plan.vecs * plan.all_pairs, radial), jnp.float32),
+            pltpu.VMEM((2 * total, plan.count_img * radial), jnp.bfloat16),
+        ],
     )(table, cb, sb, wave, zero, returned)
     return denoised, wiener_blocks
 

time: 56 us -> 52.8 us (0.943)
  local copies, waits for them, and re-layouts: 2.63 us -> 0 us
    unnamed x10 -> x0, local copies, waits for them, and re-layouts: 2.63 us -> none
    pallas_call x1, Pallas kernels: 10.8 us -> 9.1 us  [fast_device(): call(functools.partial(filter_kernel, plan), (block, shape((quota * radia...]
    pallas_call x1, Pallas kernels: 2.74 us -> 4.12 us  [fast_device(): call(functools.partial(analysis_kernel, plan), (block, shape((2 * total,...]
where the time goes in v5:
time: 52.8 us; the launch traced here: 52.5 us
  blocking collectives  20.2 us (38%)
  Pallas kernels  17 us (32%)
  waiting for transfers between devices  10.3 us (20%)
  starting transfers between devices  4.31 us (8%)
  between operations  0.65 us (1%)
    all_to_all x1, blocking collectives, fast_device(): recv = lax.all_to_all(coef, both, split_axis=0, concat_axis=0, tiled=True)  20.2 us
    pallas_call x1, Pallas kernels, fast_device(): call(functools.partial(filter_kernel, plan), (block, shape((quota * radia...  9.1 us
    ppermute x1, waiting for transfers between devices, fast_device(): other = lax.ppermute(shrink, 'batch', [(0, 1), (1, 0)])  7.55 us
    pallas_call x1, Pallas kernels, fast_device(): call(functools.partial(analysis_kernel, plan), (block, shape((2 * total,...  4.12 us
    all_to_all x1, waiting for transfers between devices, fast_device(): lax.all_to_all(back, both, split_axis=0, concat_axis=0, tiled=True)  2.77 us
    pallas_call x1, Pallas kernels, fast_device(): call(functools.partial(synthesis_kernel, plan), shape((plan.count_img, ra...  2.72 us
    all_to_all x1, starting transfers between devices, fast_device(): lax.all_to_all(back, both, split_axis=0, concat_axis=0, tiled=True)  2.6 us
    ppermute x1, starting transfers between devices, fast_device(): other = lax.ppermute(shrink, 'batch', [(0, 1), (1, 0)])  1.72 us
  transfers between devices with their start and end apart: 2, of which 2 were waited for; matrix products, arithmetic and copies ran while one was open for 0% of the time, Pallas kernels for 2%

profile of v5, /device:TPU:0, one launch (start us, length us, event | category | flops | bytes accessed | tf_op | source)
XLA Modules:
  0.0 52.5 jit_solution(4027190430449047291)
XLA Ops:
  0.6 4.1 %shard_map.68 = (bf16[32,48,128]{2,1,0:T(8,128)(2,1)S(1)}, bf16[512,512]{1,0:T(8,128)(2,1)S(1)}, f32[512,128]{1,0:T(8,128)S(1)}, f32[512,128]{1,0:T(8,128)S(1)},...) custom-call(s32[1,256]{1,0:T(1,128)} %bitcast.3, s32[1,256]{1,0:T(1,128)} %bitcast.4, ...), custom_call_target="tpu_custom_call" | custom-call | tf_op jit(solution)/shard_map/pallas_call | solution.py:550
  4.8 20.2 %all_to_all.10.recv_ref = bf16[32,48,128]{2,1,0:T(8,128)(2,1)S(1)} all-to-all(bf16[32,48,128]{2,1,0:T(8,128)(2,1)S(1)} %get-tuple-element.17), channel_id=1, replica_groups=mesh['batch'=2,'freq'=16] {'batch','freq'}, dimensions={0} | all-to-all | bytes 786432 | tf_op jit(solution)/shard_map/all_to_all | solution.py:583
  25.0 9.1 %shard_map.69 = (bf16[32,48,128]{2,1,0:T(8,128)(2,1)}, bf16[640,128]{1,0:T(8,128)(2,1)S(1)}) custom-call(f32[16,128]{1,0:T(8,128)S(1)} %get-tuple-element.16.info_ref, bf16[32,48,128]{2,1,0:T(8,128)(2,1)S(1)} %all_to_all.10.recv_ref), custom_call_target="tpu_custom_call" | custom-call | tf_op jit(solution)/shard_map/pallas_call | solution.py:584
  34.1 2.6 %all-to-all-start.1 = ((bf16[32,48,128]{2,1,0:T(8,128)(2,1)}), bf16[32,48,128]{2,1,0:T(8,128)(2,1)S(1)}, u32[]{:S(2)}, u32[]{:S(2)}) async-start(bf16[32,48,128]{2,1,0:T(8,128)(2,1)} %get-tuple-element.18), calls=%async_computation.1 | async-start | bytes 786432 | tf_op jit(solution)/shard_map/all_to_all | solution.py:598
  36.7 1.7 %collective-permute-start = (bf16[640,128]{1,0:T(8,128)(2,1)S(1)}, bf16[640,128]{1,0:T(8,128)(2,1)S(1)}, u32[]{:S(2)}, u32[]{:S(2)}) collective-permute-start(bf16[640,128]{1,0:T(8,128)(2,1)S(1)} %get-tuple-element.19.own_ref), channel_id=1, source_target_pairs={{0,16},{16,0},{1,17},{17,1},{2,18},{18,2},{3,19},{19,3},{4,20},{20... | collective-permute-start | bytes 491528 | tf_op jit(solution)/shard_map/ppermute | solution.py:599
  38.4 7.6 %collective-permute-done.other_ref = bf16[640,128]{1,0:T(8,128)(2,1)S(1)} collective-permute-done((bf16[640,128]{1,0:T(8,128)(2,1)S(1)}, bf16[640,128]{1,0:T(8,128)(2,1)S(1)}, u32[]{:S(2)}, u32[]{:S(2)}) %collective-permute-start) | collective-permute-done | bytes 163872 | tf_op jit(solution)/shard_map/ppermute | solution.py:599
  46.0 1.1 %shard_map.71 = f32[16,128,128]{2,1,0:T(8,128)} custom-call(bf16[640,128]{1,0:T(8,128)(2,1)S(1)} %get-tuple-element.19.own_ref, bf16[640,128]{1,0:T(8,128)(2,1)S(1)} %collective-permute-done.other_ref), custom_call_target="tpu_custom_call" | custom-call | tf_op jit(solution)/shard_map/pallas_call | solution.py:600
  47.0 2.8 %all-to-all-done.1.recv_ref = bf16[32,48,128]{2,1,0:T(8,128)(2,1)S(1)} async-done(((bf16[32,48,128]{2,1,0:T(8,128)(2,1)}), bf16[32,48,128]{2,1,0:T(8,128)(2,1)S(1)}, u32[]{:S(2)}, u32[]{:S(2)}) %all-to-all-start.1) | async-done | bytes 393248 | tf_op jit(solution)/shard_map/all_to_all | solution.py:598
  49.8 2.7 %shard_map.70 = bf16[4,128,512]{2,1,0:T(8,128)(2,1)} custom-call(bf16[512,512]{1,0:T(8,128)(2,1)S(1)} %get-tuple-element.11.table_ref, f32[512,128]{1,0:T(8,128)S(1)} %get-tuple-element.12.cb_ref, f32[512,128]{1,0:T(8,128)S(1)} %get-tuple-element.13.sb_ref, bf16[256,128]{1,0:T(8,128)(2,1)S(1)} %get-tuple-element.14.wave_ref, ...), custom_call_target="tpu_custom_call" | custom-call | tf_op jit(solution)/shard_map/pallas_call | solution.py:605
Async XLA Ops:
  34.1 15.7 %all-to-all-start.1 = ((bf16[32,48,128]{2,1,0:T(8,128)(2,1)}), bf16[32,48,128]{2,1,0:T(8,128)(2,1)S(1)}, u32[]{:S(2)}, u32[]{:S(2)}) async-start(bf16[32,48,128]{2,1,0:T(8,128)(2,1)} %get-tuple-element.18), calls=%async_computation.1 | async-start | bytes 786432 | tf_op jit(solution)/shard_map/all_to_all | solution.py:598
  36.7 9.3 %collective-permute-start = (bf16[640,128]{1,0:T(8,128)(2,1)S(1)}, bf16[640,128]{1,0:T(8,128)(2,1)S(1)}, u32[]{:S(2)}, u32[]{:S(2)}) collective-permute-start(bf16[640,128]{1,0:T(8,128)(2,1)S(1)} %get-tuple-element.19.own_ref), channel_id=1, source_target_pairs={{0,16},{16,0},{1,17},{17,1},{2,18},{18,2},{3,19},{19,3},{4,20},{20... | collective-permute-start | bytes 491528 | tf_op jit(solution)/shard_map/ppermute | solution.py:599

commit v6 on v5

--- a/solution.py
+++ b/solution.py
@@ -235,22 +235,32 @@
     wave_ref[radial : 2 * radial, :] = (-factor * cosine_of(turns - radial, 4 * radial)).astype(
         jnp.bfloat16
     )
-    row = iota((2 * total, total), 0)
-    high = row - total
-    low_slot = plan.slot_of(row // (2 * quota), row & (quota - 1))
-    pair = high & (plan.all_pairs - 1)
-    side = high // (2 * plan.all_pairs)
-    place = plan.half + 2 * (pair & (pairs - 1)) + side
-    high_slot = plan.slot_of(pair // pairs, place)
-    slot = jnp.where(row < total, low_slot, high_slot)
-    pick = low_bits(slot == iota((2 * total, total), 1))
+    sub, lane = iota((8, total), 0), iota((8, total), 1)
+    place = sub & (quota - 1)
+    jump = (place // pairs) * plan.owned + 2 * (place & (pairs - 1))
+    slots = [place + plan.slot_of(device, 0) for device in range(plan.devices)]
+    slots += [
+        jump + (plan.slot_of(2 * four, 0) + plan.half + e)
+        for e in range(2)
+        for four in range(plan.all_pairs // 4)
+    ]
+    jump = (sub // pairs) * plan.owned + 2 * (sub & (pairs - 1))
+    slots += [
+        jump + (plan.slot_of(4 * eight, 0) + plan.half + e)
+        for e in range(2)
+        for eight in range(plan.all_pairs // 8)
+    ]
+    device = lax.axis_index("batch") * plan.owners + lax.axis_index("freq")
+    slots.append(plan.slot_of(device, (sub // quota) * plan.half + place))
+    slots.append(slots[-1])
+    pick = jnp.concatenate([(slot == lane).astype(jnp.float32) for slot in slots], axis=0)
+    pick = pick.astype(jnp.bfloat16)
+    copies[0].wait()
     spread = lambda ref: jnp.broadcast_to(ref[...].astype(jnp.float32), (128, total)).astype(jnp.bfloat16)
-    copies[0].wait()
-    held = spread(order_ref)
-    freq = nt(pick, held).astype(jnp.int32)
-    row = iota((2 * total, 128), 0)
+    every_freq = nt(pick, spread(order_ref)).astype(jnp.int32)
+    freq = every_freq[: 2 * total]
     lane = iota((2 * total, 128), 1)
-    sine_row = jnp.where(row < total, row // quota, row // plan.all_pairs) & 1
+    sine_row = (iota((2 * total, 128), 0) // quota) & 1
     lag = sine_row * (angles // 4)
     flip = (1 - 2 * (freq & 1)).astype(jnp.float32)
     factor = math.sqrt(2.0 / angles)
@@ -265,27 +275,19 @@
     sb_ref[...] = cosine_of(turns - steps // 4, steps)
     for copy in copies[1:4]:
         copy.wait()
-    by_freq = low_bits(iota((total, total), 0) == iota((total, total), 1))
-    counts = nt(by_freq, spread(counts_ref)).astype(jnp.int32)
-    zeros = jnp.where(iota((total, radial), 1) < counts, zeros_ref[...], 0)
-    zeros = zeros.astype(jnp.float32).astype(jnp.bfloat16)
-    freq_lane = iota((plan.all_pairs, total), 1)
-    sides = []
-    for e in range(2):
-        start = total + e * 2 * plan.all_pairs
-        named = freq[start : start + plan.all_pairs]
-        named = jnp.concatenate([named] * (total // 128), axis=1)
-        sides.append(nn(low_bits(named == freq_lane), zeros))
+    named = every_freq[2 * total :]
+    named = jnp.concatenate([named] * (total // 128), axis=1) == iota((named.shape[0], total), 1)
+    pick = low_bits(named)
+    zeros = nn(pick, zeros_ref[...].astype(jnp.float32).astype(jnp.bfloat16))
+    counts = nt(pick, spread(counts_ref)).astype(jnp.int32)
+    zeros = jnp.where(iota(zeros.shape, 1) < counts, zeros, 0.0)
+    first, second = zeros[: plan.all_pairs], zeros[plan.all_pairs : 2 * plan.all_pairs]
     lane = iota((plan.all_pairs, radial), 1)
-    zero_ref[...] = jnp.where(lane < narrow, sides[0], pltpu.roll(sides[1], narrow, axis=1)).astype(
+    zero_ref[...] = jnp.where(lane < narrow, first, pltpu.roll(second, narrow, axis=1)).astype(
         jnp.int32
     )
-    place = iota((8, total), 0)
-    device = lax.axis_index("batch") * plan.owners + lax.axis_index("freq")
-    slot = plan.slot_of(device, (place // quota) * plan.half + (place & (quota - 1)))
-    mine = nt(low_bits(slot == iota((8, total), 1)), held).astype(jnp.int32)
-    mine = jnp.concatenate([mine] * (total // 128), axis=1) == iota((8, total), 1)
-    info_ref[0:8, :] = nn(low_bits(mine), zeros)
+    info_ref[0:8, :] = zeros[2 * plan.all_pairs : 2 * plan.all_pairs + 8]
+    mine = named[2 * plan.all_pairs : 2 * plan.all_pairs + 8]
     noise = jnp.sum(jnp.where(mine, noise_ref[...], 0.0), axis=1, keepdims=True)
     info_ref[8:16, :] = jnp.broadcast_to(noise, (8, 128))
     copies[4].wait()
@@ -303,8 +305,9 @@
             lows.append(coef[:total].reshape(plan.devices, 2 * quota, radial))
             span = 2 * plan.all_pairs
             for e in range(2):
-                at = (e * plan.count_img + 2 * two + i) * span
-                wide_ref[at : at + span, :] = coef[total + e * span : total + (e + 1) * span]
+                at = 8 * (e * plan.count_img + 2 * two + i)
+                part = coef[total + e * span : total + (e + 1) * span]
+                wide_ref[:, at : at + 8, :] = part.reshape(span // 8, 8, radial)
         size = 4 * quota
         coef_ref[:, size * two : size * (two + 1), :] = jnp.concatenate(lows, axis=1).astype(
             jnp.bfloat16
@@ -312,12 +315,17 @@
     lane = iota((plan.vecs, radial), 1)
     zero_here = iota((radial, radial), 0) + 1
     for device in range(plan.devices):
+        rows, chosen = [], []
+        for i in range(pairs):
+            at = device * pairs + i
+            rows.append(wide_ref[at // 4, pl.ds(at % 4, 2 * plan.vecs, stride=4), :])
+            chosen.append(low_bits(zero_here == zero_ref[at : at + 1, :]))
+        rows = jnp.concatenate(rows, axis=0).astype(jnp.bfloat16)
+        packed = nn(rows, jnp.concatenate(chosen, axis=1))
         tiles = []
         for i in range(pairs):
-            at = device * pairs + i
-            vectors = wide_ref[pl.ds(at, 2 * plan.vecs, stride=plan.all_pairs), :]
-            chosen = low_bits(zero_here == zero_ref[at : at + 1, :])
-            both = nn(vectors.astype(jnp.bfloat16), chosen)
+            start = 2 * i * plan.vecs
+            both = packed[start : start + 2 * plan.vecs, i * radial : (i + 1) * radial]
             tiles.append(jnp.where(lane < narrow, both[: plan.vecs], both[plan.vecs :]))
         coef_ref[device, plan.low_rows : plan.rows, :] = jnp.concatenate(tiles, axis=0).astype(
             jnp.bfloat16
@@ -487,23 +495,26 @@
     zero_here = iota((radial, radial), 0) + 1
     for device in range(plan.devices):
         tile = recv_ref[device, plan.low_rows : plan.rows, :].astype(jnp.float32)
+        rows, chosen = [], []
         for i in range(pairs):
             at = device * pairs + i
             packed = tile[i * plan.vecs : (i + 1) * plan.vecs]
-            both = jnp.concatenate(
-                [jnp.where(lane < plan.narrow, packed, 0.0), jnp.where(lane < plan.narrow, 0.0, packed)],
-                axis=0,
-            )
-            chosen = low_bits(zero_here == zero_ref[at : at + 1, :])
-            spread = nt(both.astype(jnp.bfloat16), chosen)
-            wide_ref[pl.ds(at, 2 * plan.vecs, stride=plan.all_pairs), :] = spread
+            rows += [jnp.where(lane < plan.narrow, packed, 0.0), jnp.where(lane < plan.narrow, 0.0, packed)]
+            chosen.append(low_bits(zero_here == zero_ref[at : at + 1, :]))
+        rows = jnp.concatenate(rows, axis=0).astype(jnp.bfloat16)
+        spread = nt(rows, jnp.concatenate(chosen, axis=0))
+        for i in range(pairs):
+            at = device * pairs + i
+            start = 2 * i * plan.vecs
+            wide_ref[at // 4, pl.ds(at % 4, 2 * plan.vecs, stride=4), :] = spread[
+                start : start + 2 * plan.vecs, i * radial : (i + 1) * radial
+            ]
     span = 2 * plan.all_pairs
     for i in range(plan.count_img):
         low = recv_ref[:, 2 * quota * i : 2 * quota * (i + 1), :].astype(jnp.float32)
-        at = [(e * plan.count_img + i) * span for e in range(2)]
-        filtered = jnp.concatenate(
-            [low.reshape(total, radial)] + [wide_ref[a : a + span, :] for a in at], axis=0
-        )
+        at = [8 * (e * plan.count_img + i) for e in range(2)]
+        high = [wide_ref[:, a : a + 8, :].reshape(span, radial) for a in at]
+        filtered = jnp.concatenate([low.reshape(total, radial)] + high, axis=0)
         turned = nt(filtered.astype(jnp.bfloat16), wave_ref[...])
         spectrum = turned[:, :radial] * cb_ref[...] + turned[:, radial:] * sb_ref[...]
         held_ref[:, i * radial : (i + 1) * radial] = spectrum.astype(jnp.bfloat16)
@@ -560,7 +571,7 @@
         ),
         [HBM] * 5,
         [
-            pltpu.VMEM((2 * plan.vecs * plan.all_pairs, radial), jnp.float32),
+            pltpu.VMEM((plan.all_pairs // 4, 8 * plan.vecs, radial), jnp.float32),
             pltpu.VMEM((1, total), jnp.int32),
             pltpu.VMEM((1, total), jnp.int32),
             pltpu.VMEM((1, total), jnp.float32),
@@ -607,7 +618,7 @@
         shape((plan.count_img, radial, plan.angles), jnp.bfloat16),
         [VMEM] * 6,
         [
-            pltpu.VMEM((2 * plan.vecs * plan.all_pairs, radial), jnp.float32),
+            pltpu.VMEM((plan.all_pairs // 4, 8 * plan.vecs, radial), jnp.float32),
             pltpu.VMEM((2 * total, plan.count_img * radial), jnp.bfloat16),
         ],
     )(table, cb, sb, wave, zero, returned)

time: 52.8 us -> 51.7 us (0.979)
  Pallas kernels: 17 us -> 15.9 us
    pallas_call x1, Pallas kernels: 4.12 us -> 3.39 us  [fast_device(): call(functools.partial(analysis_kernel, plan), (block, shape((2 * total,...]
where the time goes in v6:
time: 51.7 us; the launch traced here: 51.4 us
  blocking collectives  20.2 us (39%)
  Pallas kernels  15.9 us (31%)
  waiting for transfers between devices  10.3 us (20%)
  starting transfers between devices  4.31 us (8%)
  between operations  0.65 us (1%)
    all_to_all x1, blocking collectives, fast_device(): recv = lax.all_to_all(coef, both, split_axis=0, concat_axis=0, tiled=True)  20.2 us
    pallas_call x1, Pallas kernels, fast_device(): call(functools.partial(filter_kernel, plan), (block, shape((quota * radia...  9.1 us
    ppermute x1, waiting for transfers between devices, fast_device(): other = lax.ppermute(shrink, 'batch', [(0, 1), (1, 0)])  7.55 us
    pallas_call x1, Pallas kernels, fast_device(): call(functools.partial(analysis_kernel, plan), (block, shape((2 * total,...  3.39 us
    all_to_all x1, waiting for transfers between devices, fast_device(): lax.all_to_all(back, both, split_axis=0, concat_axis=0, tiled=True)  2.77 us
    all_to_all x1, starting transfers between devices, fast_device(): lax.all_to_all(back, both, split_axis=0, concat_axis=0, tiled=True)  2.6 us
    pallas_call x1, Pallas kernels, fast_device(): call(functools.partial(synthesis_kernel, plan), shape((plan.count_img, ra...  2.33 us
    ppermute x1, starting transfers between devices, fast_device(): other = lax.ppermute(shrink, 'batch', [(0, 1), (1, 0)])  1.72 us
  transfers between devices with their start and end apart: 2, of which 2 were waited for; matrix products, arithmetic and copies ran while one was open for 0% of the time, Pallas kernels for 2%

profile of v6, /device:TPU:0, one launch (start us, length us, event | category | flops | bytes accessed | tf_op | source)
XLA Modules:
  0.0 51.4 jit_solution(11693590266285635894)
XLA Ops:
  0.6 3.4 %shard_map.68 = (bf16[32,48,128]{2,1,0:T(8,128)(2,1)S(1)}, bf16[512,512]{1,0:T(8,128)(2,1)S(1)}, f32[512,128]{1,0:T(8,128)S(1)}, f32[512,128]{1,0:T(8,128)S(1)},...) custom-call(s32[1,256]{1,0:T(1,128)} %bitcast.3, s32[1,256]{1,0:T(1,128)} %bitcast.4, ...), custom_call_target="tpu_custom_call" | custom-call | tf_op jit(solution)/shard_map/pallas_call | solution.py:561
  4.0 20.2 %all_to_all.10.recv_ref = bf16[32,48,128]{2,1,0:T(8,128)(2,1)S(1)} all-to-all(bf16[32,48,128]{2,1,0:T(8,128)(2,1)S(1)} %get-tuple-element.17), channel_id=1, replica_groups=mesh['batch'=2,'freq'=16] {'batch','freq'}, dimensions={0} | all-to-all | bytes 786432 | tf_op jit(solution)/shard_map/all_to_all | solution.py:594
  24.3 9.1 %shard_map.69 = (bf16[32,48,128]{2,1,0:T(8,128)(2,1)}, bf16[640,128]{1,0:T(8,128)(2,1)S(1)}) custom-call(f32[16,128]{1,0:T(8,128)S(1)} %get-tuple-element.16.info_ref, bf16[32,48,128]{2,1,0:T(8,128)(2,1)S(1)} %all_to_all.10.recv_ref), custom_call_target="tpu_custom_call" | custom-call | tf_op jit(solution)/shard_map/pallas_call | solution.py:595
  33.4 2.6 %all-to-all-start.1 = ((bf16[32,48,128]{2,1,0:T(8,128)(2,1)}), bf16[32,48,128]{2,1,0:T(8,128)(2,1)S(1)}, u32[]{:S(2)}, u32[]{:S(2)}) async-start(bf16[32,48,128]{2,1,0:T(8,128)(2,1)} %get-tuple-element.18), calls=%async_computation.1 | async-start | bytes 786432 | tf_op jit(solution)/shard_map/all_to_all | solution.py:609
  36.0 1.7 %collective-permute-start = (bf16[640,128]{1,0:T(8,128)(2,1)S(1)}, bf16[640,128]{1,0:T(8,128)(2,1)S(1)}, u32[]{:S(2)}, u32[]{:S(2)}) collective-permute-start(bf16[640,128]{1,0:T(8,128)(2,1)S(1)} %get-tuple-element.19.own_ref), channel_id=1, source_target_pairs={{0,16},{16,0},{1,17},{17,1},{2,18},{18,2},{3,19},{19,3},{4,20},{20... | collective-permute-start | bytes 491528 | tf_op jit(solution)/shard_map/ppermute | solution.py:610
  37.7 7.6 %collective-permute-done.other_ref = bf16[640,128]{1,0:T(8,128)(2,1)S(1)} collective-permute-done((bf16[640,128]{1,0:T(8,128)(2,1)S(1)}, bf16[640,128]{1,0:T(8,128)(2,1)S(1)}, u32[]{:S(2)}, u32[]{:S(2)}) %collective-permute-start) | collective-permute-done | bytes 163872 | tf_op jit(solution)/shard_map/ppermute | solution.py:610
  45.2 1.1 %shard_map.71 = f32[16,128,128]{2,1,0:T(8,128)} custom-call(bf16[640,128]{1,0:T(8,128)(2,1)S(1)} %get-tuple-element.19.own_ref, bf16[640,128]{1,0:T(8,128)(2,1)S(1)} %collective-permute-done.other_ref), custom_call_target="tpu_custom_call" | custom-call | tf_op jit(solution)/shard_map/pallas_call | solution.py:611
  46.3 2.8 %all-to-all-done.1.recv_ref = bf16[32,48,128]{2,1,0:T(8,128)(2,1)S(1)} async-done(((bf16[32,48,128]{2,1,0:T(8,128)(2,1)}), bf16[32,48,128]{2,1,0:T(8,128)(2,1)S(1)}, u32[]{:S(2)}, u32[]{:S(2)}) %all-to-all-start.1) | async-done | bytes 393248 | tf_op jit(solution)/shard_map/all_to_all | solution.py:609
  49.1 2.3 %shard_map.70 = bf16[4,128,512]{2,1,0:T(8,128)(2,1)} custom-call(bf16[512,512]{1,0:T(8,128)(2,1)S(1)} %get-tuple-element.11.table_ref, f32[512,128]{1,0:T(8,128)S(1)} %get-tuple-element.12.cb_ref, f32[512,128]{1,0:T(8,128)S(1)} %get-tuple-element.13.sb_ref, bf16[256,128]{1,0:T(8,128)(2,1)S(1)} %get-tuple-element.14.wave_ref, ...), custom_call_target="tpu_custom_call" | custom-call | tf_op jit(solution)/shard_map/pallas_call | solution.py:616
Async XLA Ops:
  33.4 15.7 %all-to-all-start.1 = ((bf16[32,48,128]{2,1,0:T(8,128)(2,1)}), bf16[32,48,128]{2,1,0:T(8,128)(2,1)S(1)}, u32[]{:S(2)}, u32[]{:S(2)}) async-start(bf16[32,48,128]{2,1,0:T(8,128)(2,1)} %get-tuple-element.18), calls=%async_computation.1 | async-start | bytes 786432 | tf_op jit(solution)/shard_map/all_to_all | solution.py:609
  36.0 9.3 %collective-permute-start = (bf16[640,128]{1,0:T(8,128)(2,1)S(1)}, bf16[640,128]{1,0:T(8,128)(2,1)S(1)}, u32[]{:S(2)}, u32[]{:S(2)}) collective-permute-start(bf16[640,128]{1,0:T(8,128)(2,1)S(1)} %get-tuple-element.19.own_ref), channel_id=1, source_target_pairs={{0,16},{16,0},{1,17},{17,1},{2,18},{18,2},{3,19},{19,3},{4,20},{20... | collective-permute-start | bytes 491528 | tf_op jit(solution)/shard_map/ppermute | solution.py:610

commit v7 on v6

--- a/solution.py
+++ b/solution.py
@@ -351,41 +351,53 @@
     )
 
 
-def first_lane(halved, lane, step):
-    return (lane & 64 if halved else jnp.zeros_like(lane)) + step * 8
-
-
-def pivot_panels(panels, halves, step):
-    shape = (8, 128)
-    sub, lane = iota(shape, 0), iota(shape, 1)
-    blocks = [
-        [
-            jnp.take_along_axis(panel, first_lane(halved, lane, step) + j, axis=1)
-            for j in range(8)
-        ]
-        for panel, halved in zip(panels, halves)
-    ]
+def columns(panel, halved, first):
+    lane = iota(panel.shape, 1)
+    base = (lane & 64 if halved else jnp.zeros_like(lane)) + first
+    return [jnp.take_along_axis(panel, base + j, axis=1) for j in range(8)]
+
+
+def offset_of(shape, halved, first):
+    lane = iota(shape, 1)
+    return (lane & 63 if halved else lane) - first
+
+
+def spread_row(panel, j):
+    return jnp.broadcast_to(panel[j : j + 1], panel.shape)
+
+
+def invert_blocks(blocks):
+    sub = iota((8, 128), 0)
     for i in range(8):
         unit = (sub == i).astype(jnp.float32)
         for at, cols in enumerate(blocks):
-            inverse = 1.0 / jnp.broadcast_to(cols[i][i : i + 1], shape)
-            weight = (cols[i] - unit) * inverse
+            weight = (cols[i] - unit) * (1.0 / spread_row(cols[i], i))
             blocks[at] = [
-                unit - weight
-                if j == i
-                else cols[j] - weight * jnp.broadcast_to(cols[j][i : i + 1], shape)
+                unit - weight if j == i else cols[j] - weight * spread_row(cols[j], i)
                 for j in range(8)
             ]
-    solved = []
-    for panel, halved, cols in zip(panels, halves, blocks):
-        offset = lane - first_lane(halved, lane, step)
-        unit = (sub == offset).astype(jnp.float32)
-        lines = jnp.where((offset < 0) | (offset >= 8), panel, unit)
-        total = cols[0] * jnp.broadcast_to(lines[0:1], shape)
-        for j in range(1, 8):
-            total = total + cols[j] * jnp.broadcast_to(lines[j : j + 1], shape)
-        solved.append(total)
-    return solved
+    return blocks
+
+
+def solve_panel(panel, cols, halved, first):
+    offset = offset_of(panel.shape, halved, first)
+    unit = (iota(panel.shape, 0) == offset).astype(jnp.float32)
+    lines = jnp.where((offset < 0) | (offset >= 8), panel, unit)
+    total = cols[0] * spread_row(lines, 0)
+    for j in range(1, 8):
+        total = total + cols[j] * spread_row(lines, j)
+    return total
+
+
+def take_away(panel, factors, solved, halved, first):
+    offset = offset_of(panel.shape, halved, first)
+    total = jnp.where((offset >= 0) & (offset < 8), 0.0, panel)
+    other = factors[1] * spread_row(solved, 1)
+    for j in range(0, 8, 2):
+        total = total - factors[j] * spread_row(solved, j)
+        if j:
+            other = other + factors[j + 1] * spread_row(solved, j + 1)
+    return total - other
 
 
 def scales_of(matrix, halved):
@@ -399,22 +411,34 @@
     return across * jnp.where(lane < 64, left, right)
 
 
-def sweep(matrices, step, carry):
-    start = pl.multiple_of(step * 8, 8)
-    halves = [halved for _, _, halved in matrices]
-    panels = [ref[m, pl.ds(start, 8), :] for ref, m, _ in matrices]
-    solved = pivot_panels(panels, halves, step)
-    sub, lane = iota((8, 128), 0), iota((8, 128), 1)
-    for (ref, m, halved), panel, fresh in zip(matrices, panels, solved):
+def sweep(matrices):
+    upper, lower, starts = [], [], []
+    for ref, m, _, first in matrices:
+        start = pl.multiple_of(first, 16)
+        starts.append(start)
+        upper.append(ref[m, pl.ds(start, 8), :])
+        lower.append(ref[m, pl.ds(start + 8, 8), :])
+    kinds = [(halved, first) for _, _, halved, first in matrices]
+    blocks = invert_blocks([columns(p, h, f) for p, (h, f) in zip(upper, kinds)])
+    factors = [columns(p, h, f) for p, (h, f) in zip(lower, kinds)]
+    tops = [solve_panel(p, c, h, f) for p, c, (h, f) in zip(upper, blocks, kinds)]
+    rests = [take_away(p, c, t, h, f) for p, c, t, (h, f) in zip(lower, factors, tops, kinds)]
+    factors = [columns(t, h, f + 8) for t, (h, f) in zip(tops, kinds)]
+    blocks = invert_blocks([columns(r, h, f + 8) for r, (h, f) in zip(rests, kinds)])
+    bottoms = [solve_panel(r, c, h, f + 8) for r, c, (h, f) in zip(rests, blocks, kinds)]
+    tops = [take_away(t, c, b, h, f + 8) for t, c, b, (h, f) in zip(tops, factors, bottoms, kinds)]
+    shape = (16, 128)
+    for at, (ref, m, halved, first) in enumerate(matrices):
         height = ref.shape[1]
-        done = (lane & 63 if halved else lane) < step * 8
-        unit = (sub == lane - first_lane(halved, lane, step)).astype(jnp.float32)
-        update = outer(jnp.where(done, -panel, panel), fresh + unit)
+        panel = jnp.concatenate([upper[at], lower[at]], axis=0)
+        fresh = jnp.concatenate([tops[at], bottoms[at]], axis=0)
+        offset = offset_of(shape, halved, first)
+        unit = (iota(shape, 0) == offset).astype(jnp.float32)
+        update = outer(jnp.where(offset < 0, -panel, panel), fresh + unit)
         if halved:
             update = jnp.where(iota((height, 128), 1) < 64, update[:height], update[height:])
         ref[m] = ref[m] - update
-        ref[m, pl.ds(start, 8), :] = fresh
-    return carry
+        ref[m, pl.ds(starts[at], 16), :] = fresh
 
 
 def filter_kernel(
@@ -457,10 +481,15 @@
         scale = scales_of(covariance, True)
         pair_scale_ref[i] = scale
         pair_ref[i] = covariance * scale
-    lower = [(full_ref, m, False) for m in range(quota)]
-    upper = [(pair_ref, m, True) for m in range(pairs)]
-    lax.fori_loop(0, narrow // 8, functools.partial(sweep, lower + upper), 0)
-    lax.fori_loop(narrow // 8, radial // 8, functools.partial(sweep, lower), 0)
+    steps, half_steps = radial // 16, narrow // 16
+
+    def body(step, carry):
+        matrices = [(full_ref, m, False, 16 * step) for m in range(quota)]
+        part = 16 * (step % half_steps)
+        sweep(matrices + [(pair_ref, step // half_steps, True, part)])
+        return carry
+
+    lax.fori_loop(0, steps, body, 0)
     for s in range(quota):
         shrink = eye - noises[s] * (full_ref[s] * full_scale_ref[s])
         shrink_ref[s * radial : (s + 1) * radial, :] = shrink.astype(jnp.bfloat16)

time: 51.7 us -> 50.8 us (0.983)
  Pallas kernels: 15.9 us -> 15 us
    pallas_call x1, Pallas kernels: 9.1 us -> 8.2 us  [fast_device(): call(functools.partial(filter_kernel, plan), (block, shape((quota * radia...]
where the time goes in v7:
time: 50.8 us; the launch traced here: 50.5 us
  blocking collectives  20.2 us (40%)
  Pallas kernels  15 us (30%)
  waiting for transfers between devices  10.3 us (20%)
  starting transfers between devices  4.31 us (8%)
  between operations  0.65 us (1%)
    all_to_all x1, blocking collectives, fast_device(): recv = lax.all_to_all(coef, both, split_axis=0, concat_axis=0, tiled=True)  20.2 us
    pallas_call x1, Pallas kernels, fast_device(): call(functools.partial(filter_kernel, plan), (block, shape((quota * radia...  8.2 us
    ppermute x1, waiting for transfers between devices, fast_device(): other = lax.ppermute(shrink, 'batch', [(0, 1), (1, 0)])  7.55 us
    pallas_call x1, Pallas kernels, fast_device(): call(functools.partial(analysis_kernel, plan), (block, shape((2 * total,...  3.39 us
    all_to_all x1, waiting for transfers between devices, fast_device(): lax.all_to_all(back, both, split_axis=0, concat_axis=0, tiled=True)  2.77 us
    all_to_all x1, starting transfers between devices, fast_device(): lax.all_to_all(back, both, split_axis=0, concat_axis=0, tiled=True)  2.6 us
    pallas_call x1, Pallas kernels, fast_device(): call(functools.partial(synthesis_kernel, plan), shape((plan.count_img, ra...  2.33 us
    ppermute x1, starting transfers between devices, fast_device(): other = lax.ppermute(shrink, 'batch', [(0, 1), (1, 0)])  1.72 us
  transfers between devices with their start and end apart: 2, of which 2 were waited for; matrix products, arithmetic and copies ran while one was open for 0% of the time, Pallas kernels for 2%

profile of v7, /device:TPU:0, one launch (start us, length us, event | category | flops | bytes accessed | tf_op | source)
XLA Modules:
  0.0 50.5 jit_solution(15007628692055704718)
XLA Ops:
  0.6 3.4 %shard_map.68 = (bf16[32,48,128]{2,1,0:T(8,128)(2,1)S(1)}, bf16[512,512]{1,0:T(8,128)(2,1)S(1)}, f32[512,128]{1,0:T(8,128)S(1)}, f32[512,128]{1,0:T(8,128)S(1)},...) custom-call(s32[1,256]{1,0:T(1,128)} %bitcast.3, s32[1,256]{1,0:T(1,128)} %bitcast.4, ...), custom_call_target="tpu_custom_call" | custom-call | tf_op jit(solution)/shard_map/pallas_call | solution.py:590
  4.0 20.2 %all_to_all.10.recv_ref = bf16[32,48,128]{2,1,0:T(8,128)(2,1)S(1)} all-to-all(bf16[32,48,128]{2,1,0:T(8,128)(2,1)S(1)} %get-tuple-element.17), channel_id=1, replica_groups=mesh['batch'=2,'freq'=16] {'batch','freq'}, dimensions={0} | all-to-all | bytes 786432 | tf_op jit(solution)/shard_map/all_to_all | solution.py:623
  24.3 8.2 %shard_map.69 = (bf16[32,48,128]{2,1,0:T(8,128)(2,1)}, bf16[640,128]{1,0:T(8,128)(2,1)S(1)}) custom-call(f32[16,128]{1,0:T(8,128)S(1)} %get-tuple-element.16.info_ref, bf16[32,48,128]{2,1,0:T(8,128)(2,1)S(1)} %all_to_all.10.recv_ref), custom_call_target="tpu_custom_call" | custom-call | tf_op jit(solution)/shard_map/pallas_call | solution.py:624
  32.5 2.6 %all-to-all-start.1 = ((bf16[32,48,128]{2,1,0:T(8,128)(2,1)}), bf16[32,48,128]{2,1,0:T(8,128)(2,1)S(1)}, u32[]{:S(2)}, u32[]{:S(2)}) async-start(bf16[32,48,128]{2,1,0:T(8,128)(2,1)} %get-tuple-element.18), calls=%async_computation.1 | async-start | bytes 786432 | tf_op jit(solution)/shard_map/all_to_all | solution.py:638
  35.1 1.7 %collective-permute-start = (bf16[640,128]{1,0:T(8,128)(2,1)S(1)}, bf16[640,128]{1,0:T(8,128)(2,1)S(1)}, u32[]{:S(2)}, u32[]{:S(2)}) collective-permute-start(bf16[640,128]{1,0:T(8,128)(2,1)S(1)} %get-tuple-element.19.own_ref), channel_id=1, source_target_pairs={{0,16},{16,0},{1,17},{17,1},{2,18},{18,2},{3,19},{19,3},{4,20},{20... | collective-permute-start | bytes 491528 | tf_op jit(solution)/shard_map/ppermute | solution.py:639
  36.8 7.6 %collective-permute-done.other_ref = bf16[640,128]{1,0:T(8,128)(2,1)S(1)} collective-permute-done((bf16[640,128]{1,0:T(8,128)(2,1)S(1)}, bf16[640,128]{1,0:T(8,128)(2,1)S(1)}, u32[]{:S(2)}, u32[]{:S(2)}) %collective-permute-start) | collective-permute-done | bytes 163872 | tf_op jit(solution)/shard_map/ppermute | solution.py:639
  44.3 1.1 %shard_map.71 = f32[16,128,128]{2,1,0:T(8,128)} custom-call(bf16[640,128]{1,0:T(8,128)(2,1)S(1)} %get-tuple-element.19.own_ref, bf16[640,128]{1,0:T(8,128)(2,1)S(1)} %collective-permute-done.other_ref), custom_call_target="tpu_custom_call" | custom-call | tf_op jit(solution)/shard_map/pallas_call | solution.py:640
  45.4 2.8 %all-to-all-done.1.recv_ref = bf16[32,48,128]{2,1,0:T(8,128)(2,1)S(1)} async-done(((bf16[32,48,128]{2,1,0:T(8,128)(2,1)}), bf16[32,48,128]{2,1,0:T(8,128)(2,1)S(1)}, u32[]{:S(2)}, u32[]{:S(2)}) %all-to-all-start.1) | async-done | bytes 393248 | tf_op jit(solution)/shard_map/all_to_all | solution.py:638
  48.2 2.3 %shard_map.70 = bf16[4,128,512]{2,1,0:T(8,128)(2,1)} custom-call(bf16[512,512]{1,0:T(8,128)(2,1)S(1)} %get-tuple-element.11.table_ref, f32[512,128]{1,0:T(8,128)S(1)} %get-tuple-element.12.cb_ref, f32[512,128]{1,0:T(8,128)S(1)} %get-tuple-element.13.sb_ref, bf16[256,128]{1,0:T(8,128)(2,1)S(1)} %get-tuple-element.14.wave_ref, ...), custom_call_target="tpu_custom_call" | custom-call | tf_op jit(solution)/shard_map/pallas_call | solution.py:645
Async XLA Ops:
  32.5 15.7 %all-to-all-start.1 = ((bf16[32,48,128]{2,1,0:T(8,128)(2,1)}), bf16[32,48,128]{2,1,0:T(8,128)(2,1)S(1)}, u32[]{:S(2)}, u32[]{:S(2)}) async-start(bf16[32,48,128]{2,1,0:T(8,128)(2,1)} %get-tuple-element.18), calls=%async_computation.1 | async-start | bytes 786432 | tf_op jit(solution)/shard_map/all_to_all | solution.py:638
  35.1 9.3 %collective-permute-start = (bf16[640,128]{1,0:T(8,128)(2,1)S(1)}, bf16[640,128]{1,0:T(8,128)(2,1)S(1)}, u32[]{:S(2)}, u32[]{:S(2)}) collective-permute-start(bf16[640,128]{1,0:T(8,128)(2,1)S(1)} %get-tuple-element.19.own_ref), channel_id=1, source_target_pairs={{0,16},{16,0},{1,17},{17,1},{2,18},{18,2},{3,19},{19,3},{4,20},{20... | collective-permute-start | bytes 491528 | tf_op jit(solution)/shard_map/ppermute | solution.py:639

commit v8 on v7

--- a/solution.py
+++ b/solution.py
@@ -200,12 +200,21 @@
             and self.radial == 128
             and self.count_img == 4
             and all(power(n) for n in (self.angles, self.total, owners))
-            and self.angles == 2 * self.total
+            and self.angles == 2 * self.total == 4 * self.radial
         )
 
     def slot_of(self, device, place):
         batch, owner = device // self.owners, device & (self.owners - 1)
         return owner * self.owned + batch * self.quota + place
+
+
+def row_pairs(x, y):
+    blocks, width = x.shape[0] // 8, x.shape[1]
+    x, y = x.reshape(blocks, 8, width), y.reshape(blocks, 8, width)
+    front = iota(x.shape, 1) < 4
+    first = jnp.where(front, x, pltpu.roll(y, 4, axis=1))
+    second = jnp.where(front, pltpu.roll(x, 4, axis=1), y)
+    return jnp.concatenate([first, second], axis=1).reshape(16 * blocks, width)
 
 
 def analysis_kernel(
@@ -237,13 +246,8 @@
     )
     sub, lane = iota((8, total), 0), iota((8, total), 1)
     place = sub & (quota - 1)
-    jump = (place // pairs) * plan.owned + 2 * (place & (pairs - 1))
-    slots = [place + plan.slot_of(device, 0) for device in range(plan.devices)]
-    slots += [
-        jump + (plan.slot_of(2 * four, 0) + plan.half + e)
-        for e in range(2)
-        for four in range(plan.all_pairs // 4)
-    ]
+    jump = (sub // quota) * plan.owned + place
+    slots = [jump + plan.slot_of(2 * two, 0) for two in range(plan.devices // 2)]
     jump = (sub // pairs) * plan.owned + 2 * (sub & (pairs - 1))
     slots += [
         jump + (plan.slot_of(4 * eight, 0) + plan.half + e)
@@ -251,31 +255,40 @@
         for eight in range(plan.all_pairs // 8)
     ]
     device = lax.axis_index("batch") * plan.owners + lax.axis_index("freq")
-    slots.append(plan.slot_of(device, (sub // quota) * plan.half + place))
-    slots.append(slots[-1])
+    partner = (1 - lax.axis_index("batch")) * plan.owners + lax.axis_index("freq")
+    slots += [plan.slot_of(d, (sub // quota) * plan.half + place) for d in (device, partner)]
     pick = jnp.concatenate([(slot == lane).astype(jnp.float32) for slot in slots], axis=0)
     pick = pick.astype(jnp.bfloat16)
     copies[0].wait()
     spread = lambda ref: jnp.broadcast_to(ref[...].astype(jnp.float32), (128, total)).astype(jnp.bfloat16)
     every_freq = nt(pick, spread(order_ref)).astype(jnp.int32)
-    freq = every_freq[: 2 * total]
-    lane = iota((2 * total, 128), 1)
-    sine_row = (iota((2 * total, 128), 0) // quota) & 1
-    lag = sine_row * (angles // 4)
-    flip = (1 - 2 * (freq & 1)).astype(jnp.float32)
+    freq = every_freq[:total]
+    lane = iota((total, 128), 1)
     factor = math.sqrt(2.0 / angles)
-    for part in range(angles // 256):
-        cosine = cosine_of((lane + part * 128) * freq - lag, angles) * factor
-        table_ref[:, part * 128 : part * 128 + 128] = cosine.astype(jnp.bfloat16)
-        start = angles // 2 + part * 128
-        table_ref[:, start : start + 128] = (cosine * flip).astype(jnp.bfloat16)
+    turns = lane * freq
+    cosine = cosine_of(turns, angles) * factor
+    sine = cosine_of(turns - angles // 4, angles) * factor
+    odd, flip = freq & 1, (1 - (freq & 2)).astype(jnp.float32)
+    even_part, odd_part = (1 - odd).astype(jnp.float32) * flip, odd.astype(jnp.float32) * flip
+    mirror = (1 - 2 * odd).astype(jnp.float32)
+    turned_cosine = even_part * cosine - odd_part * sine
+    turned_sine = even_part * sine + odd_part * cosine
+    parts = [
+        (cosine, sine),
+        (turned_cosine, turned_sine),
+        (mirror * cosine, mirror * sine),
+        (mirror * turned_cosine, mirror * turned_sine),
+    ]
+    for part, (x, y) in enumerate(parts):
+        table_ref[:, part * 128 : part * 128 + 128] = row_pairs(x, y).astype(jnp.bfloat16)
     steps = 16 * radial
     turns = (2 * freq - 1) * (2 * lane + 1) - 4 * radial * freq - 2 * radial
-    cb_ref[...] = cosine_of(turns, steps)
-    sb_ref[...] = cosine_of(turns - steps // 4, steps)
+    cosine, sine = cosine_of(turns, steps), cosine_of(turns - steps // 4, steps)
+    cb_ref[...] = row_pairs(cosine, cosine)
+    sb_ref[...] = row_pairs(sine, sine)
     for copy in copies[1:4]:
         copy.wait()
-    named = every_freq[2 * total :]
+    named = every_freq[total - 2 * plan.all_pairs :]
     named = jnp.concatenate([named] * (total // 128), axis=1) == iota((named.shape[0], total), 1)
     pick = low_bits(named)
     zeros = nn(pick, zeros_ref[...].astype(jnp.float32).astype(jnp.bfloat16))
@@ -286,10 +299,16 @@
     zero_ref[...] = jnp.where(lane < narrow, first, pltpu.roll(second, narrow, axis=1)).astype(
         jnp.int32
     )
-    info_ref[0:8, :] = zeros[2 * plan.all_pairs : 2 * plan.all_pairs + 8]
+    square = (radial, radial)
+    ones = jnp.ones((8, radial), jnp.bfloat16)
+    for s in range(quota):
+        at = 2 * plan.all_pairs + s
+        chosen = low_bits(iota(square, 0) + 1 == zeros[at : at + 1].astype(jnp.int32))
+        info_ref[s : s + 1, :] = nt(ones, chosen)[0:1]
     mine = named[2 * plan.all_pairs : 2 * plan.all_pairs + 8]
     noise = jnp.sum(jnp.where(mine, noise_ref[...], 0.0), axis=1, keepdims=True)
     info_ref[8:16, :] = jnp.broadcast_to(noise, (8, 128))
+    info_ref[16:32, :] = zeros[2 * plan.all_pairs :]
     copies[4].wait()
     images = images_ref[...].reshape(plan.count_img * radial, angles)
     for two in range(plan.count_img // 2):
@@ -443,7 +462,7 @@
 
 def filter_kernel(
     plan, info_ref, recv_ref,
-    back_ref, shrink_ref, wide_ref, full_ref, pair_ref, pick_ref, held_ref, full_scale_ref, pair_scale_ref,
+    back_ref, shrink_ref, wide_ref, full_ref, pair_ref, kept_ref, held_ref, full_scale_ref, pair_scale_ref,
 ):
     radial, quota, pairs, narrow = plan.radial, plan.quota, plan.pairs, plan.narrow
     low_rows = plan.low_rows
@@ -458,11 +477,9 @@
     noises = []
     for s in range(quota):
         noises.append(info_ref[8 + s : 9 + s, :])
-        zero = info_ref[s : s + 1, :].astype(jnp.int32)
-        pick = low_bits(iota(square, 0) + 1 == zero)
-        pick_ref[s] = pick
-        vectors = wide_ref[pl.ds(s, rows, stride=quota), :].astype(jnp.bfloat16)
-        coef = nn(vectors, pick).astype(jnp.bfloat16)
+        coef = wide_ref[pl.ds(s, rows, stride=quota), :] * info_ref[s : s + 1, :]
+        coef = coef.astype(jnp.bfloat16)
+        kept_ref[s] = coef
         covariance = tn(coef, coef) / float(rows) + noises[s] * eye
         scale = scales_of(covariance, False)
         full_scale_ref[s] = scale
@@ -493,16 +510,7 @@
     for s in range(quota):
         shrink = eye - noises[s] * (full_ref[s] * full_scale_ref[s])
         shrink_ref[s * radial : (s + 1) * radial, :] = shrink.astype(jnp.bfloat16)
-        pick = pick_ref[s]
-        moved = lax.dot_general(
-            shrink.astype(jnp.bfloat16),
-            pick,
-            (((0,), (1,)), ((), ())),
-            preferred_element_type=jnp.float32,
-        ).astype(jnp.bfloat16)
-        spread = nn(pick, moved).astype(jnp.bfloat16)
-        vectors = wide_ref[pl.ds(s, rows, stride=quota), :].astype(jnp.bfloat16)
-        wide_ref[pl.ds(s, rows, stride=quota), :] = nn(vectors, spread)
+        wide_ref[pl.ds(s, rows, stride=quota), :] = nt(kept_ref[s], shrink.astype(jnp.bfloat16))
     shape = (plan.devices, low_rows, radial)
     back_ref[:, :low_rows, :] = wide_ref[...].reshape(shape).astype(jnp.bfloat16)
     tiles = []
@@ -551,16 +559,20 @@
     out_ref[...] = image.reshape(out_ref.shape)
 
 
-def wiener_kernel(plan, own_ref, other_ref, out_ref):
+def wiener_kernel(plan, own_ref, other_ref, info_ref, out_ref):
     radial, quota, narrow = plan.radial, plan.quota, plan.narrow
     batch_at = lax.axis_index("batch")
     lane = iota((narrow, radial), 1)
-    for batch, ref in ((batch_at, own_ref), (1 - batch_at, other_ref)):
+    zero_here = iota((radial, radial), 0) + 1
+    for batch, ref, start in ((batch_at, own_ref, 16), (1 - batch_at, other_ref, 24)):
         for s in range(quota):
-            out_ref[batch * quota + s] = ref[s * radial : (s + 1) * radial, :].astype(jnp.float32)
+            zero = info_ref[start + s : start + s + 1, :].astype(jnp.int32)
+            chosen = low_bits(zero_here == zero)
+            half_way = nn(ref[s * radial : (s + 1) * radial, :], chosen).astype(jnp.bfloat16)
+            out_ref[batch * quota + s] = tn(chosen, half_way)
             at = plan.half + batch * quota + s
-            start = quota * radial + (s // 2) * narrow
-            pair = ref[start : start + narrow, :].astype(jnp.float32)
+            first = quota * radial + (s // 2) * narrow
+            pair = ref[first : first + narrow, :].astype(jnp.float32)
             if s % 2:
                 pair = pltpu.roll(pair, narrow, axis=1)
             out_ref[at, 0:narrow, :] = jnp.where(lane < narrow, pair, 0.0)
@@ -596,7 +608,7 @@
             shape((2 * total, radial), jnp.float32),
             shape((2 * radial, radial), jnp.bfloat16),
             shape((plan.all_pairs, radial), jnp.int32),
-            shape((16, radial), jnp.float32),
+            shape((32, radial), jnp.float32),
         ),
         [HBM] * 5,
         [
@@ -629,7 +641,7 @@
             pltpu.VMEM((plan.devices * plan.low_rows, radial), jnp.float32),
             pltpu.VMEM((quota, radial, radial), jnp.float32),
             pltpu.VMEM((pairs, plan.narrow, radial), jnp.float32),
-            pltpu.VMEM((quota, radial, radial), jnp.bfloat16),
+            pltpu.VMEM((quota, plan.devices * plan.vecs, radial), jnp.bfloat16),
             pltpu.VMEM((pairs, plan.devices * plan.vecs, radial), jnp.bfloat16),
             pltpu.VMEM((quota, radial, radial), jnp.float32),
             pltpu.VMEM((pairs, plan.narrow, radial), jnp.float32),
@@ -640,8 +652,8 @@
     wiener_blocks = call(
         functools.partial(wiener_kernel, plan),
         shape((plan.owned, radial, radial), jnp.float32),
-        [VMEM] * 2,
-    )(shrink, other)
+        [VMEM] * 3,
+    )(shrink, other, info)
     denoised = call(
         functools.partial(synthesis_kernel, plan),
         shape((plan.count_img, radial, plan.angles), jnp.bfloat16),

time: 50.8 us -> 49.9 us (0.982)
  Pallas kernels: 15 us -> 14.4 us
    pallas_call x1, Pallas kernels: 8.2 us -> 7.23 us  [fast_device(): call(functools.partial(filter_kernel, plan), (block, shape((quota * radia...]
  transfers between devices with their start and end apart: 2 -> 2, of which waited for: 2 -> 2; matrix products, arithmetic and copies ran while one was open for 0% -> 0% of each run, Pallas kernels for 2% -> 3%
where the time goes in v8:
time: 49.9 us; the launch traced here: 49.6 us
  blocking collectives  20.2 us (40%)
  Pallas kernels  14.4 us (29%)
  waiting for transfers between devices  10 us (20%)
  starting transfers between devices  4.31 us (9%)
  between operations  0.65 us (1%)
    all_to_all x1, blocking collectives, fast_device(): recv = lax.all_to_all(coef, both, split_axis=0, concat_axis=0, tiled=True)  20.2 us
    ppermute x1, waiting for transfers between devices, fast_device(): other = lax.ppermute(shrink, 'batch', [(0, 1), (1, 0)])  7.55 us
    pallas_call x1, Pallas kernels, fast_device(): call(functools.partial(filter_kernel, plan), (block, shape((quota * radia...  7.23 us
    pallas_call x1, Pallas kernels, fast_device(): call(functools.partial(analysis_kernel, plan), (block, shape((2 * total,...  3.49 us
    all_to_all x1, starting transfers between devices, fast_device(): lax.all_to_all(back, both, split_axis=0, concat_axis=0, tiled=True)  2.6 us
    all_to_all x1, waiting for transfers between devices, fast_device(): lax.all_to_all(back, both, split_axis=0, concat_axis=0, tiled=True)  2.45 us
    pallas_call x1, Pallas kernels, fast_device(): call(functools.partial(synthesis_kernel, plan), shape((plan.count_img, ra...  2.33 us
    ppermute x1, starting transfers between devices, fast_device(): other = lax.ppermute(shrink, 'batch', [(0, 1), (1, 0)])  1.72 us
  transfers between devices with their start and end apart: 2, of which 2 were waited for; matrix products, arithmetic and copies ran while one was open for 0% of the time, Pallas kernels for 3%

profile of v8, /device:TPU:0, one launch (start us, length us, event | category | flops | bytes accessed | tf_op | source)
XLA Modules:
  0.0 49.6 jit_solution(2627733242567182526)
XLA Ops:
  0.6 3.5 %shard_map.68 = (bf16[32,48,128]{2,1,0:T(8,128)(2,1)S(1)}, bf16[512,512]{1,0:T(8,128)(2,1)S(1)}, f32[512,128]{1,0:T(8,128)S(1)}, f32[512,128]{1,0:T(8,128)S(1)},...) custom-call(s32[1,256]{1,0:T(1,128)} %bitcast.3, s32[1,256]{1,0:T(1,128)} %bitcast.4, ...), custom_call_target="tpu_custom_call" | custom-call | tf_op jit(solution)/shard_map/pallas_call | solution.py:602
  4.1 20.2 %all_to_all.10.recv_ref = bf16[32,48,128]{2,1,0:T(8,128)(2,1)S(1)} all-to-all(bf16[32,48,128]{2,1,0:T(8,128)(2,1)S(1)} %get-tuple-element.17), channel_id=1, replica_groups=mesh['batch'=2,'freq'=16] {'batch','freq'}, dimensions={0} | all-to-all | bytes 786432 | tf_op jit(solution)/shard_map/all_to_all | solution.py:635
  24.4 7.2 %shard_map.69 = (bf16[32,48,128]{2,1,0:T(8,128)(2,1)}, bf16[640,128]{1,0:T(8,128)(2,1)S(1)}) custom-call(f32[32,128]{1,0:T(8,128)S(1)} %get-tuple-element.16.info_ref, bf16[32,48,128]{2,1,0:T(8,128)(2,1)S(1)} %all_to_all.10.recv_ref), custom_call_target="tpu_custom_call" | custom-call | tf_op jit(solution)/shard_map/pallas_call | solution.py:636
  31.6 2.6 %all-to-all-start.1 = ((bf16[32,48,128]{2,1,0:T(8,128)(2,1)}), bf16[32,48,128]{2,1,0:T(8,128)(2,1)S(1)}, u32[]{:S(2)}, u32[]{:S(2)}) async-start(bf16[32,48,128]{2,1,0:T(8,128)(2,1)} %get-tuple-element.18), calls=%async_computation.1 | async-start | bytes 786432 | tf_op jit(solution)/shard_map/all_to_all | solution.py:650
  34.2 1.7 %collective-permute-start = (bf16[640,128]{1,0:T(8,128)(2,1)S(1)}, bf16[640,128]{1,0:T(8,128)(2,1)S(1)}, u32[]{:S(2)}, u32[]{:S(2)}) collective-permute-start(bf16[640,128]{1,0:T(8,128)(2,1)S(1)} %get-tuple-element.19.own_ref), channel_id=1, source_target_pairs={{0,16},{16,0},{1,17},{17,1},{2,18},{18,2},{3,19},{19,3},{4,20},{20... | collective-permute-start | bytes 491528 | tf_op jit(solution)/shard_map/ppermute | solution.py:651
  35.9 7.6 %collective-permute-done.other_ref = bf16[640,128]{1,0:T(8,128)(2,1)S(1)} collective-permute-done((bf16[640,128]{1,0:T(8,128)(2,1)S(1)}, bf16[640,128]{1,0:T(8,128)(2,1)S(1)}, u32[]{:S(2)}, u32[]{:S(2)}) %collective-permute-start) | collective-permute-done | bytes 163872 | tf_op jit(solution)/shard_map/ppermute | solution.py:651
  43.5 1.4 %shard_map.71 = f32[16,128,128]{2,1,0:T(8,128)} custom-call(bf16[640,128]{1,0:T(8,128)(2,1)S(1)} %get-tuple-element.19.own_ref, bf16[640,128]{1,0:T(8,128)(2,1)S(1)} %collective-permute-done.other_ref, f32[32,128]{1,0:T(8,128)S(1)} %get-tuple-element.16.info_ref), custom_call_target="tpu_custom_call" | custom-call | tf_op jit(solution)/shard_map/pallas_call | solution.py:652
  44.8 2.4 %all-to-all-done.1.recv_ref = bf16[32,48,128]{2,1,0:T(8,128)(2,1)S(1)} async-done(((bf16[32,48,128]{2,1,0:T(8,128)(2,1)}), bf16[32,48,128]{2,1,0:T(8,128)(2,1)S(1)}, u32[]{:S(2)}, u32[]{:S(2)}) %all-to-all-start.1) | async-done | bytes 393248 | tf_op jit(solution)/shard_map/all_to_all | solution.py:650
  47.3 2.3 %shard_map.70 = bf16[4,128,512]{2,1,0:T(8,128)(2,1)} custom-call(bf16[512,512]{1,0:T(8,128)(2,1)S(1)} %get-tuple-element.11.table_ref, f32[512,128]{1,0:T(8,128)S(1)} %get-tuple-element.12.cb_ref, f32[512,128]{1,0:T(8,128)S(1)} %get-tuple-element.13.sb_ref, bf16[256,128]{1,0:T(8,128)(2,1)S(1)} %get-tuple-element.14.wave_ref, ...), custom_call_target="tpu_custom_call" | custom-call | tf_op jit(solution)/shard_map/pallas_call | solution.py:657
Async XLA Ops:
  31.6 15.7 %all-to-all-start.1 = ((bf16[32,48,128]{2,1,0:T(8,128)(2,1)}), bf16[32,48,128]{2,1,0:T(8,128)(2,1)S(1)}, u32[]{:S(2)}, u32[]{:S(2)}) async-start(bf16[32,48,128]{2,1,0:T(8,128)(2,1)} %get-tuple-element.18), calls=%async_computation.1 | async-start | bytes 786432 | tf_op jit(solution)/shard_map/all_to_all | solution.py:650
  34.2 9.3 %collective-permute-start = (bf16[640,128]{1,0:T(8,128)(2,1)S(1)}, bf16[640,128]{1,0:T(8,128)(2,1)S(1)}, u32[]{:S(2)}, u32[]{:S(2)}) collective-permute-start(bf16[640,128]{1,0:T(8,128)(2,1)S(1)} %get-tuple-element.19.own_ref), channel_id=1, source_target_pairs={{0,16},{16,0},{1,17},{17,1},{2,18},{18,2},{3,19},{19,3},{4,20},{20... | collective-permute-start | bytes 491528 | tf_op jit(solution)/shard_map/ppermute | solution.py:651

commit v9 on v8

--- a/solution.py
+++ b/solution.py
@@ -385,27 +385,22 @@
     return jnp.broadcast_to(panel[j : j + 1], panel.shape)
 
 
-def invert_blocks(blocks):
+def eliminate(panels, kinds):
     sub = iota((8, 128), 0)
+    blocks, lines = [], []
+    for panel, (halved, first) in zip(panels, kinds):
+        offset = offset_of(panel.shape, halved, first)
+        unit = (sub == offset).astype(jnp.float32)
+        blocks.append(columns(panel, halved, first))
+        lines.append(jnp.where((offset < 0) | (offset >= 8), panel, unit))
     for i in range(8):
         unit = (sub == i).astype(jnp.float32)
         for at, cols in enumerate(blocks):
             weight = (cols[i] - unit) * (1.0 / spread_row(cols[i], i))
-            blocks[at] = [
-                unit - weight if j == i else cols[j] - weight * spread_row(cols[j], i)
-                for j in range(8)
-            ]
-    return blocks
-
-
-def solve_panel(panel, cols, halved, first):
-    offset = offset_of(panel.shape, halved, first)
-    unit = (iota(panel.shape, 0) == offset).astype(jnp.float32)
-    lines = jnp.where((offset < 0) | (offset >= 8), panel, unit)
-    total = cols[0] * spread_row(lines, 0)
-    for j in range(1, 8):
-        total = total + cols[j] * spread_row(lines, j)
-    return total
+            for j in range(i + 1, 8):
+                cols[j] = cols[j] - weight * spread_row(cols[j], i)
+            lines[at] = lines[at] - weight * spread_row(lines[at], i)
+    return lines
 
 
 def take_away(panel, factors, solved, halved, first):
@@ -438,13 +433,11 @@
         upper.append(ref[m, pl.ds(start, 8), :])
         lower.append(ref[m, pl.ds(start + 8, 8), :])
     kinds = [(halved, first) for _, _, halved, first in matrices]
-    blocks = invert_blocks([columns(p, h, f) for p, (h, f) in zip(upper, kinds)])
     factors = [columns(p, h, f) for p, (h, f) in zip(lower, kinds)]
-    tops = [solve_panel(p, c, h, f) for p, c, (h, f) in zip(upper, blocks, kinds)]
+    tops = eliminate(upper, kinds)
     rests = [take_away(p, c, t, h, f) for p, c, t, (h, f) in zip(lower, factors, tops, kinds)]
     factors = [columns(t, h, f + 8) for t, (h, f) in zip(tops, kinds)]
-    blocks = invert_blocks([columns(r, h, f + 8) for r, (h, f) in zip(rests, kinds)])
-    bottoms = [solve_panel(r, c, h, f + 8) for r, c, (h, f) in zip(rests, blocks, kinds)]
+    bottoms = eliminate(rests, [(h, f + 8) for h, f in kinds])
     tops = [take_away(t, c, b, h, f + 8) for t, c, b, (h, f) in zip(tops, factors, bottoms, kinds)]
     shape = (16, 128)
     for at, (ref, m, halved, first) in enumerate(matrices):

time: 49.9 us -> 49.6 us (level)
  no operation moved by 1% of the time
where the time goes in v9:
time: 49.6 us; the launch traced here: 49.4 us
  blocking collectives  20.2 us (41%)
  Pallas kernels  14.2 us (29%)
  waiting for transfers between devices  10 us (20%)
  starting transfers between devices  4.31 us (9%)
  between operations  0.65 us (1%)
    all_to_all x1, blocking collectives, fast_device(): recv = lax.all_to_all(coef, both, split_axis=0, concat_axis=0, tiled=True)  20.2 us
    ppermute x1, waiting for transfers between devices, fast_device(): other = lax.ppermute(shrink, 'batch', [(0, 1), (1, 0)])  7.55 us
    pallas_call x1, Pallas kernels, fast_device(): call(functools.partial(filter_kernel, plan), (block, shape((quota * radia...  6.97 us
    pallas_call x1, Pallas kernels, fast_device(): call(functools.partial(analysis_kernel, plan), (block, shape((2 * total,...  3.49 us
    all_to_all x1, starting transfers between devices, fast_device(): lax.all_to_all(back, both, split_axis=0, concat_axis=0, tiled=True)  2.6 us
    all_to_all x1, waiting for transfers between devices, fast_device(): lax.all_to_all(back, both, split_axis=0, concat_axis=0, tiled=True)  2.45 us
    pallas_call x1, Pallas kernels, fast_device(): call(functools.partial(synthesis_kernel, plan), shape((plan.count_img, ra...  2.33 us
    ppermute x1, starting transfers between devices, fast_device(): other = lax.ppermute(shrink, 'batch', [(0, 1), (1, 0)])  1.72 us
  transfers between devices with their start and end apart: 2, of which 2 were waited for; matrix products, arithmetic and copies ran while one was open for 0% of the time, Pallas kernels for 3%

profile of v9, /device:TPU:0, one launch (start us, length us, event | category | flops | bytes accessed | tf_op | source)
XLA Modules:
  0.0 49.4 jit_solution(5719478537372279732)
XLA Ops:
  0.6 3.5 %shard_map.68 = (bf16[32,48,128]{2,1,0:T(8,128)(2,1)S(1)}, bf16[512,512]{1,0:T(8,128)(2,1)S(1)}, f32[512,128]{1,0:T(8,128)S(1)}, f32[512,128]{1,0:T(8,128)S(1)},...) custom-call(s32[1,256]{1,0:T(1,128)} %bitcast.3, s32[1,256]{1,0:T(1,128)} %bitcast.4, ...), custom_call_target="tpu_custom_call" | custom-call | tf_op jit(solution)/shard_map/pallas_call | solution.py:595
  4.1 20.2 %all_to_all.10.recv_ref = bf16[32,48,128]{2,1,0:T(8,128)(2,1)S(1)} all-to-all(bf16[32,48,128]{2,1,0:T(8,128)(2,1)S(1)} %get-tuple-element.17), channel_id=1, replica_groups=mesh['batch'=2,'freq'=16] {'batch','freq'}, dimensions={0} | all-to-all | bytes 786432 | tf_op jit(solution)/shard_map/all_to_all | solution.py:628
  24.4 7.0 %shard_map.69 = (bf16[32,48,128]{2,1,0:T(8,128)(2,1)}, bf16[640,128]{1,0:T(8,128)(2,1)S(1)}) custom-call(f32[32,128]{1,0:T(8,128)S(1)} %get-tuple-element.16.info_ref, bf16[32,48,128]{2,1,0:T(8,128)(2,1)S(1)} %all_to_all.10.recv_ref), custom_call_target="tpu_custom_call" | custom-call | tf_op jit(solution)/shard_map/pallas_call | solution.py:629
  31.3 2.6 %all-to-all-start.1 = ((bf16[32,48,128]{2,1,0:T(8,128)(2,1)}), bf16[32,48,128]{2,1,0:T(8,128)(2,1)S(1)}, u32[]{:S(2)}, u32[]{:S(2)}) async-start(bf16[32,48,128]{2,1,0:T(8,128)(2,1)} %get-tuple-element.18), calls=%async_computation.1 | async-start | bytes 786432 | tf_op jit(solution)/shard_map/all_to_all | solution.py:643
  33.9 1.7 %collective-permute-start = (bf16[640,128]{1,0:T(8,128)(2,1)S(1)}, bf16[640,128]{1,0:T(8,128)(2,1)S(1)}, u32[]{:S(2)}, u32[]{:S(2)}) collective-permute-start(bf16[640,128]{1,0:T(8,128)(2,1)S(1)} %get-tuple-element.19.own_ref), channel_id=1, source_target_pairs={{0,16},{16,0},{1,17},{17,1},{2,18},{18,2},{3,19},{19,3},{4,20},{20... | collective-permute-start | bytes 491528 | tf_op jit(solution)/shard_map/ppermute | solution.py:644
  35.6 7.6 %collective-permute-done.other_ref = bf16[640,128]{1,0:T(8,128)(2,1)S(1)} collective-permute-done((bf16[640,128]{1,0:T(8,128)(2,1)S(1)}, bf16[640,128]{1,0:T(8,128)(2,1)S(1)}, u32[]{:S(2)}, u32[]{:S(2)}) %collective-permute-start) | collective-permute-done | bytes 163872 | tf_op jit(solution)/shard_map/ppermute | solution.py:644
  43.2 1.4 %shard_map.71 = f32[16,128,128]{2,1,0:T(8,128)} custom-call(bf16[640,128]{1,0:T(8,128)(2,1)S(1)} %get-tuple-element.19.own_ref, bf16[640,128]{1,0:T(8,128)(2,1)S(1)} %collective-permute-done.other_ref, f32[32,128]{1,0:T(8,128)S(1)} %get-tuple-element.16.info_ref), custom_call_target="tpu_custom_call" | custom-call | tf_op jit(solution)/shard_map/pallas_call | solution.py:645
  44.6 2.4 %all-to-all-done.1.recv_ref = bf16[32,48,128]{2,1,0:T(8,128)(2,1)S(1)} async-done(((bf16[32,48,128]{2,1,0:T(8,128)(2,1)}), bf16[32,48,128]{2,1,0:T(8,128)(2,1)S(1)}, u32[]{:S(2)}, u32[]{:S(2)}) %all-to-all-start.1) | async-done | bytes 393248 | tf_op jit(solution)/shard_map/all_to_all | solution.py:643
  47.0 2.3 %shard_map.70 = bf16[4,128,512]{2,1,0:T(8,128)(2,1)} custom-call(bf16[512,512]{1,0:T(8,128)(2,1)S(1)} %get-tuple-element.11.table_ref, f32[512,128]{1,0:T(8,128)S(1)} %get-tuple-element.12.cb_ref, f32[512,128]{1,0:T(8,128)S(1)} %get-tuple-element.13.sb_ref, bf16[256,128]{1,0:T(8,128)(2,1)S(1)} %get-tuple-element.14.wave_ref, ...), custom_call_target="tpu_custom_call" | custom-call | tf_op jit(solution)/shard_map/pallas_call | solution.py:650
Async XLA Ops:
  31.3 15.7 %all-to-all-start.1 = ((bf16[32,48,128]{2,1,0:T(8,128)(2,1)}), bf16[32,48,128]{2,1,0:T(8,128)(2,1)S(1)}, u32[]{:S(2)}, u32[]{:S(2)}) async-start(bf16[32,48,128]{2,1,0:T(8,128)(2,1)} %get-tuple-element.18), calls=%async_computation.1 | async-start | bytes 786432 | tf_op jit(solution)/shard_map/all_to_all | solution.py:643
  33.9 9.3 %collective-permute-start = (bf16[640,128]{1,0:T(8,128)(2,1)S(1)}, bf16[640,128]{1,0:T(8,128)(2,1)S(1)}, u32[]{:S(2)}, u32[]{:S(2)}) collective-permute-start(bf16[640,128]{1,0:T(8,128)(2,1)S(1)} %get-tuple-element.19.own_ref), channel_id=1, source_target_pairs={{0,16},{16,0},{1,17},{17,1},{2,18},{18,2},{3,19},{19,3},{4,20},{20... | collective-permute-start | bytes 491528 | tf_op jit(solution)/shard_map/ppermute | solution.py:644

commit v10 on v9

--- a/solution.py
+++ b/solution.py
@@ -286,7 +286,7 @@
     cosine, sine = cosine_of(turns, steps), cosine_of(turns - steps // 4, steps)
     cb_ref[...] = row_pairs(cosine, cosine)
     sb_ref[...] = row_pairs(sine, sine)
-    for copy in copies[1:4]:
+    for copy in copies[1:]:
         copy.wait()
     named = every_freq[total - 2 * plan.all_pairs :]
     named = jnp.concatenate([named] * (total // 128), axis=1) == iota((named.shape[0], total), 1)
@@ -309,7 +309,6 @@
     noise = jnp.sum(jnp.where(mine, noise_ref[...], 0.0), axis=1, keepdims=True)
     info_ref[8:16, :] = jnp.broadcast_to(noise, (8, 128))
     info_ref[16:32, :] = zeros[2 * plan.all_pairs :]
-    copies[4].wait()
     images = images_ref[...].reshape(plan.count_img * radial, angles)
     for two in range(plan.count_img // 2):
         spectrum = nt(table_ref[...], images[2 * two * radial : 2 * (two + 1) * radial])

time: 49.6 us -> 49.5 us (level)
  no operation moved by 1% of the time
where the time goes in v10:
time: 49.5 us; the launch traced here: 49.2 us
  blocking collectives  20.2 us (41%)
  Pallas kernels  14 us (28%)
  waiting for transfers between devices  10 us (20%)
  starting transfers between devices  4.31 us (9%)
  between operations  0.65 us (1%)
    all_to_all x1, blocking collectives, fast_device(): recv = lax.all_to_all(coef, both, split_axis=0, concat_axis=0, tiled=True)  20.2 us
    ppermute x1, waiting for transfers between devices, fast_device(): other = lax.ppermute(shrink, 'batch', [(0, 1), (1, 0)])  7.55 us
    pallas_call x1, Pallas kernels, fast_device(): call(functools.partial(filter_kernel, plan), (block, shape((quota * radia...  6.97 us
    pallas_call x1, Pallas kernels, fast_device(): call(functools.partial(analysis_kernel, plan), (block, shape((2 * total,...  3.37 us
    all_to_all x1, starting transfers between devices, fast_device(): lax.all_to_all(back, both, split_axis=0, concat_axis=0, tiled=True)  2.6 us
    all_to_all x1, waiting for transfers between devices, fast_device(): lax.all_to_all(back, both, split_axis=0, concat_axis=0, tiled=True)  2.45 us
    pallas_call x1, Pallas kernels, fast_device(): call(functools.partial(synthesis_kernel, plan), shape((plan.count_img, ra...  2.33 us
    ppermute x1, starting transfers between devices, fast_device(): other = lax.ppermute(shrink, 'batch', [(0, 1), (1, 0)])  1.72 us
  transfers between devices with their start and end apart: 2, of which 2 were waited for; matrix products, arithmetic and copies ran while one was open for 0% of the time, Pallas kernels for 3%

profile of v10, /device:TPU:0, one launch (start us, length us, event | category | flops | bytes accessed | tf_op | source)
XLA Modules:
  0.0 49.2 jit_solution(6415314342690274171)
XLA Ops:
  0.6 3.4 %shard_map.68 = (bf16[32,48,128]{2,1,0:T(8,128)(2,1)S(1)}, bf16[512,512]{1,0:T(8,128)(2,1)S(1)}, f32[512,128]{1,0:T(8,128)S(1)}, f32[512,128]{1,0:T(8,128)S(1)},...) custom-call(s32[1,256]{1,0:T(1,128)} %bitcast.3, s32[1,256]{1,0:T(1,128)} %bitcast.4, ...), custom_call_target="tpu_custom_call" | custom-call | tf_op jit(solution)/shard_map/pallas_call | solution.py:594
  4.0 20.2 %all_to_all.10.recv_ref = bf16[32,48,128]{2,1,0:T(8,128)(2,1)S(1)} all-to-all(bf16[32,48,128]{2,1,0:T(8,128)(2,1)S(1)} %get-tuple-element.17), channel_id=1, replica_groups=mesh['batch'=2,'freq'=16] {'batch','freq'}, dimensions={0} | all-to-all | bytes 786432 | tf_op jit(solution)/shard_map/all_to_all | solution.py:627
  24.2 7.0 %shard_map.69 = (bf16[32,48,128]{2,1,0:T(8,128)(2,1)}, bf16[640,128]{1,0:T(8,128)(2,1)S(1)}) custom-call(f32[32,128]{1,0:T(8,128)S(1)} %get-tuple-element.16.info_ref, bf16[32,48,128]{2,1,0:T(8,128)(2,1)S(1)} %all_to_all.10.recv_ref), custom_call_target="tpu_custom_call" | custom-call | tf_op jit(solution)/shard_map/pallas_call | solution.py:628
  31.2 2.6 %all-to-all-start.1 = ((bf16[32,48,128]{2,1,0:T(8,128)(2,1)}), bf16[32,48,128]{2,1,0:T(8,128)(2,1)S(1)}, u32[]{:S(2)}, u32[]{:S(2)}) async-start(bf16[32,48,128]{2,1,0:T(8,128)(2,1)} %get-tuple-element.18), calls=%async_computation.1 | async-start | bytes 786432 | tf_op jit(solution)/shard_map/all_to_all | solution.py:642
  33.8 1.7 %collective-permute-start = (bf16[640,128]{1,0:T(8,128)(2,1)S(1)}, bf16[640,128]{1,0:T(8,128)(2,1)S(1)}, u32[]{:S(2)}, u32[]{:S(2)}) collective-permute-start(bf16[640,128]{1,0:T(8,128)(2,1)S(1)} %get-tuple-element.19.own_ref), channel_id=1, source_target_pairs={{0,16},{16,0},{1,17},{17,1},{2,18},{18,2},{3,19},{19,3},{4,20},{20... | collective-permute-start | bytes 491528 | tf_op jit(solution)/shard_map/ppermute | solution.py:643
  35.5 7.6 %collective-permute-done.other_ref = bf16[640,128]{1,0:T(8,128)(2,1)S(1)} collective-permute-done((bf16[640,128]{1,0:T(8,128)(2,1)S(1)}, bf16[640,128]{1,0:T(8,128)(2,1)S(1)}, u32[]{:S(2)}, u32[]{:S(2)}) %collective-permute-start) | collective-permute-done | bytes 163872 | tf_op jit(solution)/shard_map/ppermute | solution.py:643
  43.1 1.4 %shard_map.71 = f32[16,128,128]{2,1,0:T(8,128)} custom-call(bf16[640,128]{1,0:T(8,128)(2,1)S(1)} %get-tuple-element.19.own_ref, bf16[640,128]{1,0:T(8,128)(2,1)S(1)} %collective-permute-done.other_ref, f32[32,128]{1,0:T(8,128)S(1)} %get-tuple-element.16.info_ref), custom_call_target="tpu_custom_call" | custom-call | tf_op jit(solution)/shard_map/pallas_call | solution.py:644
  44.5 2.4 %all-to-all-done.1.recv_ref = bf16[32,48,128]{2,1,0:T(8,128)(2,1)S(1)} async-done(((bf16[32,48,128]{2,1,0:T(8,128)(2,1)}), bf16[32,48,128]{2,1,0:T(8,128)(2,1)S(1)}, u32[]{:S(2)}, u32[]{:S(2)}) %all-to-all-start.1) | async-done | bytes 393248 | tf_op jit(solution)/shard_map/all_to_all | solution.py:642
  46.9 2.3 %shard_map.70 = bf16[4,128,512]{2,1,0:T(8,128)(2,1)} custom-call(bf16[512,512]{1,0:T(8,128)(2,1)S(1)} %get-tuple-element.11.table_ref, f32[512,128]{1,0:T(8,128)S(1)} %get-tuple-element.12.cb_ref, f32[512,128]{1,0:T(8,128)S(1)} %get-tuple-element.13.sb_ref, bf16[256,128]{1,0:T(8,128)(2,1)S(1)} %get-tuple-element.14.wave_ref, ...), custom_call_target="tpu_custom_call" | custom-call | tf_op jit(solution)/shard_map/pallas_call | solution.py:649
Async XLA Ops:
  31.2 15.7 %all-to-all-start.1 = ((bf16[32,48,128]{2,1,0:T(8,128)(2,1)}), bf16[32,48,128]{2,1,0:T(8,128)(2,1)S(1)}, u32[]{:S(2)}, u32[]{:S(2)}) async-start(bf16[32,48,128]{2,1,0:T(8,128)(2,1)} %get-tuple-element.18), calls=%async_computation.1 | async-start | bytes 786432 | tf_op jit(solution)/shard_map/all_to_all | solution.py:642
  33.8 9.3 %collective-permute-start = (bf16[640,128]{1,0:T(8,128)(2,1)S(1)}, bf16[640,128]{1,0:T(8,128)(2,1)S(1)}, u32[]{:S(2)}, u32[]{:S(2)}) collective-permute-start(bf16[640,128]{1,0:T(8,128)(2,1)S(1)} %get-tuple-element.19.own_ref), channel_id=1, source_target_pairs={{0,16},{16,0},{1,17},{17,1},{2,18},{18,2},{3,19},{19,3},{4,20},{20... | collective-permute-start | bytes 491528 | tf_op jit(solution)/shard_map/ppermute | solution.py:643

commit v11 on v10

--- a/solution.py
+++ b/solution.py
@@ -427,7 +427,7 @@
 def sweep(matrices):
     upper, lower, starts = [], [], []
     for ref, m, _, first in matrices:
-        start = pl.multiple_of(first, 16)
+        start = first
         starts.append(start)
         upper.append(ref[m, pl.ds(start, 8), :])
         lower.append(ref[m, pl.ds(start + 8, 8), :])
@@ -492,13 +492,10 @@
         pair_ref[i] = covariance * scale
     steps, half_steps = radial // 16, narrow // 16
 
-    def body(step, carry):
+    for step in range(steps):
         matrices = [(full_ref, m, False, 16 * step) for m in range(quota)]
         part = 16 * (step % half_steps)
         sweep(matrices + [(pair_ref, step // half_steps, True, part)])
-        return carry
-
-    lax.fori_loop(0, steps, body, 0)
     for s in range(quota):
         shrink = eye - noises[s] * (full_ref[s] * full_scale_ref[s])
         shrink_ref[s * radial : (s + 1) * radial, :] = shrink.astype(jnp.bfloat16)

time: 49.5 us -> 49.2 us (level)
  no operation moved by 1% of the time
where the time goes in v11:
time: 49.2 us; the launch traced here: 48.9 us
  blocking collectives  20.2 us (41%)
  Pallas kernels  13.7 us (28%)
  waiting for transfers between devices  10 us (20%)
  starting transfers between devices  4.31 us (9%)
  between operations  0.65 us (1%)
    all_to_all x1, blocking collectives, fast_device(): recv = lax.all_to_all(coef, both, split_axis=0, concat_axis=0, tiled=True)  20.2 us
    ppermute x1, waiting for transfers between devices, fast_device(): other = lax.ppermute(shrink, 'batch', [(0, 1), (1, 0)])  7.55 us
    pallas_call x1, Pallas kernels, fast_device(): call(functools.partial(filter_kernel, plan), (block, shape((quota * radia...  6.62 us
    pallas_call x1, Pallas kernels, fast_device(): call(functools.partial(analysis_kernel, plan), (block, shape((2 * total,...  3.37 us
    all_to_all x1, starting transfers between devices, fast_device(): lax.all_to_all(back, both, split_axis=0, concat_axis=0, tiled=True)  2.6 us
    all_to_all x1, waiting for transfers between devices, fast_device(): lax.all_to_all(back, both, split_axis=0, concat_axis=0, tiled=True)  2.45 us
    pallas_call x1, Pallas kernels, fast_device(): call(functools.partial(synthesis_kernel, plan), shape((plan.count_img, ra...  2.33 us
    ppermute x1, starting transfers between devices, fast_device(): other = lax.ppermute(shrink, 'batch', [(0, 1), (1, 0)])  1.72 us
  transfers between devices with their start and end apart: 2, of which 2 were waited for; matrix products, arithmetic and copies ran while one was open for 0% of the time, Pallas kernels for 3%

profile of v11, /device:TPU:0, one launch (start us, length us, event | category | flops | bytes accessed | tf_op | source)
XLA Modules:
  0.0 48.9 jit_solution(14069829818845308685)
XLA Ops:
  0.6 3.4 %shard_map.68 = (bf16[32,48,128]{2,1,0:T(8,128)(2,1)S(1)}, bf16[512,512]{1,0:T(8,128)(2,1)S(1)}, f32[512,128]{1,0:T(8,128)S(1)}, f32[512,128]{1,0:T(8,128)S(1)},...) custom-call(s32[1,256]{1,0:T(1,128)} %bitcast.3, s32[1,256]{1,0:T(1,128)} %bitcast.4, ...), custom_call_target="tpu_custom_call" | custom-call | tf_op jit(solution)/shard_map/pallas_call | solution.py:591
  4.0 20.2 %all_to_all.10.recv_ref = bf16[32,48,128]{2,1,0:T(8,128)(2,1)S(1)} all-to-all(bf16[32,48,128]{2,1,0:T(8,128)(2,1)S(1)} %get-tuple-element.17), channel_id=1, replica_groups=mesh['batch'=2,'freq'=16] {'batch','freq'}, dimensions={0} | all-to-all | bytes 786432 | tf_op jit(solution)/shard_map/all_to_all | solution.py:624
  24.2 6.6 %shard_map.69 = (bf16[32,48,128]{2,1,0:T(8,128)(2,1)}, bf16[640,128]{1,0:T(8,128)(2,1)S(1)}) custom-call(f32[32,128]{1,0:T(8,128)S(1)} %get-tuple-element.16.info_ref, bf16[32,48,128]{2,1,0:T(8,128)(2,1)S(1)} %all_to_all.10.recv_ref), custom_call_target="tpu_custom_call" | custom-call | tf_op jit(solution)/shard_map/pallas_call | solution.py:625
  30.9 2.6 %all-to-all-start.1 = ((bf16[32,48,128]{2,1,0:T(8,128)(2,1)}), bf16[32,48,128]{2,1,0:T(8,128)(2,1)S(1)}, u32[]{:S(2)}, u32[]{:S(2)}) async-start(bf16[32,48,128]{2,1,0:T(8,128)(2,1)} %get-tuple-element.18), calls=%async_computation.1 | async-start | bytes 786432 | tf_op jit(solution)/shard_map/all_to_all | solution.py:639
  33.5 1.7 %collective-permute-start = (bf16[640,128]{1,0:T(8,128)(2,1)S(1)}, bf16[640,128]{1,0:T(8,128)(2,1)S(1)}, u32[]{:S(2)}, u32[]{:S(2)}) collective-permute-start(bf16[640,128]{1,0:T(8,128)(2,1)S(1)} %get-tuple-element.19.own_ref), channel_id=1, source_target_pairs={{0,16},{16,0},{1,17},{17,1},{2,18},{18,2},{3,19},{19,3},{4,20},{20... | collective-permute-start | bytes 491528 | tf_op jit(solution)/shard_map/ppermute | solution.py:640
  35.2 7.6 %collective-permute-done.other_ref = bf16[640,128]{1,0:T(8,128)(2,1)S(1)} collective-permute-done((bf16[640,128]{1,0:T(8,128)(2,1)S(1)}, bf16[640,128]{1,0:T(8,128)(2,1)S(1)}, u32[]{:S(2)}, u32[]{:S(2)}) %collective-permute-start) | collective-permute-done | bytes 163872 | tf_op jit(solution)/shard_map/ppermute | solution.py:640
  42.7 1.4 %shard_map.71 = f32[16,128,128]{2,1,0:T(8,128)} custom-call(bf16[640,128]{1,0:T(8,128)(2,1)S(1)} %get-tuple-element.19.own_ref, bf16[640,128]{1,0:T(8,128)(2,1)S(1)} %collective-permute-done.other_ref, f32[32,128]{1,0:T(8,128)S(1)} %get-tuple-element.16.info_ref), custom_call_target="tpu_custom_call" | custom-call | tf_op jit(solution)/shard_map/pallas_call | solution.py:641
  44.1 2.4 %all-to-all-done.1.recv_ref = bf16[32,48,128]{2,1,0:T(8,128)(2,1)S(1)} async-done(((bf16[32,48,128]{2,1,0:T(8,128)(2,1)}), bf16[32,48,128]{2,1,0:T(8,128)(2,1)S(1)}, u32[]{:S(2)}, u32[]{:S(2)}) %all-to-all-start.1) | async-done | bytes 393248 | tf_op jit(solution)/shard_map/all_to_all | solution.py:639
  46.6 2.3 %shard_map.70 = bf16[4,128,512]{2,1,0:T(8,128)(2,1)} custom-call(bf16[512,512]{1,0:T(8,128)(2,1)S(1)} %get-tuple-element.11.table_ref, f32[512,128]{1,0:T(8,128)S(1)} %get-tuple-element.12.cb_ref, f32[512,128]{1,0:T(8,128)S(1)} %get-tuple-element.13.sb_ref, bf16[256,128]{1,0:T(8,128)(2,1)S(1)} %get-tuple-element.14.wave_ref, ...), custom_call_target="tpu_custom_call" | custom-call | tf_op jit(solution)/shard_map/pallas_call | solution.py:646
Async XLA Ops:
  30.9 15.7 %all-to-all-start.1 = ((bf16[32,48,128]{2,1,0:T(8,128)(2,1)}), bf16[32,48,128]{2,1,0:T(8,128)(2,1)S(1)}, u32[]{:S(2)}, u32[]{:S(2)}) async-start(bf16[32,48,128]{2,1,0:T(8,128)(2,1)} %get-tuple-element.18), calls=%async_computation.1 | async-start | bytes 786432 | tf_op jit(solution)/shard_map/all_to_all | solution.py:639
  33.5 9.3 %collective-permute-start = (bf16[640,128]{1,0:T(8,128)(2,1)S(1)}, bf16[640,128]{1,0:T(8,128)(2,1)S(1)}, u32[]{:S(2)}, u32[]{:S(2)}) collective-permute-start(bf16[640,128]{1,0:T(8,128)(2,1)S(1)} %get-tuple-element.19.own_ref), channel_id=1, source_target_pairs={{0,16},{16,0},{1,17},{17,1},{2,18},{18,2},{3,19},{19,3},{4,20},{20... | collective-permute-start | bytes 491528 | tf_op jit(solution)/shard_map/ppermute | solution.py:640
